TPU v7x, 32 devices: a whole 2x2x4 slice. The times are simulated.
32 devices in a mesh: grp: 4 (over y, core), col: 8 (over z, x).
Axes of the slice: x: 2, y: 2, z: 4, core: 2. Of those that a mesh axis runs over, the one named last changes fastest.
Arguments:
- descriptors: float32 [4096, 2000], P(('grp', 'col')), may hold values from 0 to 1
Outputs:
- kernel: float32 [4096, 4, 1024], P('grp', None, 'col')
All inputs are finite; a program needn't handle non-finite values.
Results may differ from a plain program's by a relative error of at most 0.00056.
Values may be sent and summed in bfloat16 or wider, within the bound.
No kernel may reach another device: no remote copies, remote signals or barrier semaphores. Data moves between devices by JAX's collectives and lax.ppermute only.
A program may use at most 128 MiB of HBM per device.

v0:
```python
import jax
import jax.numpy as jnp
from jax import lax
from jax.sharding import PartitionSpec as P


def fourth(left, right):
    intersection = lax.dot_general(
        left, right, (((1,), (1,)), ((), ())), preferred_element_type=jnp.float32
    )
    second = intersection * intersection
    return second * second


def shards(descriptors):
    ngroups = lax.axis_size("grp")
    ncolumns = lax.axis_size("col")
    block = descriptors.shape[0]
    squares = jnp.sum(descriptors * descriptors, axis=1, keepdims=True)
    unit = (descriptors * lax.rsqrt(squares + 1e-06)).astype(jnp.bfloat16)
    columns = lax.all_gather(unit, "grp", axis=0, tiled=True)
    tile = fourth(lax.all_gather(unit, "col", axis=0, tiled=True), columns)
    return tile.reshape(ncolumns * block, ngroups, block)


def solution(mesh):
    in_specs = (P(("grp", "col"), None),)
    out_specs = P("grp", None, "col")
    return jax.shard_map(shards, mesh=mesh, in_specs=in_specs, out_specs=out_specs, check_vma=False)
```

profile of v0, /device:TPU:0, one launch (start us, length us, event | category | flops | bytes accessed | tf_op | source)
XLA Modules:
  0.0 125.0 jit_solution(44521792384588481)
XLA Ops:
  6.5 0.0 all-gather.5.cloned.1.call-start
  6.5 1.5 %multiply_reduce_fusion = f32[128]{0:T(128)S(1)} fusion(f32[128,2000]{0,1:T(8,128)} %param.1), kind=kLoop, calls=%fused_computation.2 | loop fusion | flops 511872 | bytes 1024512 | tf_op jit(solution)/shard_map/reduce_sum | solution.py:19
  8.0 2.1 %multiply_convert_fusion = bf16[128,2000]{0,1:T(8,128)(2,1)} fusion(f32[128,2000]{0,1:T(8,128)} %param.1, f32[128]{0:T(128)S(1)} %add_rsqrt_fusion), kind=kLoop, calls=%fused_computation.1 | loop fusion | flops 512000 | bytes 1536512 | tf_op jit(solution)/shard_map/convert_element_type | solution.py:20
  10.1 0.0 all-gather.5.cloned.1.call-update
  10.1 0.0 all-gather.3.cloned.1.call-start
  10.2 0.7 all-gather.3.cloned.1.call-update
  10.9 24.7 %all-gather.5.cloned.1.call-done = bf16[512,2000]{0,1:T(8,128)(2,1)} async-done(((bf16[128,2000]{0,1:T(8,128)(2,1)}), bf16[512,2000]{0,1:T(8,128)(2,1)}) %all-gather.5.cloned.1.call-update) | async-done | bytes 2048016 | tf_op jit(solution)/shard_map/all_gather | solution.py:21
  35.5 75.6 %all-gather.3.cloned.1.call-done = bf16[1024,2000]{0,1:T(8,128)(2,1)} async-done(((bf16[128,2000]{0,1:T(8,128)(2,1)}), bf16[1024,2000]{0,1:T(8,128)(2,1)}) %all-gather.3.cloned.1.call-update) | async-done | bytes 4096016 | tf_op jit(solution)/shard_map/all_gather | solution.py:22
  111.1 5.2 %multiply_multiply_fusion = f32[1024,512]{0,1:T(8,128)S(1)} fusion(bf16[1024,2000]{0,1:T(8,128)(2,1)} %all-gather.3.cloned.1.call-done, bf16[512,2000]{0,1:T(8,128)(2,1)} %all-gather.5.cloned.1.call-done), kind=kOutput, calls=%fused_computation | convolution fusion | flops 2098200576 | bytes 8241152 | tf_op jit(solution)/shard_map/dot_general | solution.py:8
  116.3 1.8 %copy.2 = f32[1024,4,128]{2,1,0:T(4,128)} copy(f32[1024,4,128]{0,2,1:T(8,128)S(1)} %bitcast.3) | data formatting | bytes 4194304 | tf_op jit(solution)/shard_map/reshape | solution.py:23
  (1 shorter events, 0.0 us)
Async XLA Ops:
  6.5 29.0 %all-gather.5.cloned.1.call-start = ((), (), s32[]{:S(2)}) async-start(), calls=%async_computation.1 | async-start | bytes 2560000 | tf_op jit(solution)/shard_map/all_gather | solution.py:21
  10.1 101.0 %all-gather.3.cloned.1.call-start = ((), (), s32[]{:S(2)}) async-start(), calls=%async_computation | async-start | bytes 4608000 | tf_op jit(solution)/shard_map/all_gather | solution.py:22
Sparse Core Ops, SparseCore 0:
  10.2 25.2 all-gather.4
  37.6 73.5 all-gather.2
where the time goes:
time: 125 us
  waiting for transfers between devices  101 us (81%)
  between operations  13.4 us (11%)
  matrix products  5.18 us (4%)
  other arithmetic  3.56 us (3%)
  local copies, waits for them, and re-layouts  1.81 us (1%)
    all_gather x1, waiting for transfers between devices, shards(): tile = fourth(lax.all_gather(unit, 'col', axis=0, tiled=True), columns)  75.6 us
    all_gather x1, waiting for transfers between devices, shards(): columns = lax.all_gather(unit, 'grp', axis=0, tiled=True)  24.7 us
    dot_general x1, matrix products, fourth(): lax.dot_general(left, right, (((1,), (1,)), ((), ())), preferred_element_...  5.18 us
  transfers between devices with their start and end apart: 2, of which 2 were waited for; matrix products, arithmetic and copies ran while one was open for 0% of the time, Pallas kernels for 0%

commit v1 on v0

v1 whole, which is shorter than its diff:
```python
import functools

import jax
import jax.numpy as jnp
from jax import lax
from jax.experimental import pallas as pl
from jax.experimental.pallas import tpu as pltpu
from jax.sharding import PartitionSpec as P


AXES = ("grp", "col")
LINE = 4
SCALE = 32768.0


HBM = pl.BlockSpec(memory_space=pl.ANY)
VMEM = pl.BlockSpec(memory_space=pltpu.VMEM)
SMEM = pl.BlockSpec(memory_space=pltpu.SMEM)


def unit_kernel(cut, data, first, second):
    squares = jnp.sum(data[...] * data[...], axis=0, keepdims=True)
    scale = lax.rsqrt(squares + 1e-06)
    first[...] = (data[:cut] * scale).astype(jnp.bfloat16)
    second[...] = (data[cut:] * scale).astype(jnp.bfloat16)


def normalize(data, cut):
    features, block = data.shape
    return pl.pallas_call(
        functools.partial(unit_kernel, cut),
        out_shape=[
            jax.ShapeDtypeStruct((cut, block), jnp.bfloat16),
            jax.ShapeDtypeStruct((features - cut, block), jnp.bfloat16),
        ],
        in_specs=[VMEM],
        out_specs=[VMEM, VMEM],
        cost_estimate=pl.CostEstimate(flops=0, bytes_accessed=6 * data.size, transcendentals=0),
        name="normalize",
    )(data)


def product_kernel(nparts, nblocks, cut, placed, *refs):
    slots, parts, refs = refs[0], refs[1 : 1 + 2 * nparts], refs[1 + 2 * nparts :]
    blocks, refs = refs[: 2 * nblocks], refs[2 * nblocks :]
    out, cols, rows, tile, sem_cols, sem_rows, sem_out = refs[-7:]
    size = rows.shape[2]

    def load(i, h, ref, dst, sem):
        span = pl.ds(0, cut) if h == 0 else pl.ds(cut, rows.shape[1] - cut)
        return pltpu.make_async_copy(ref, dst(span), sem.at[i, h])

    def column(i, h):
        at = pl.multiple_of(slots[i] * size, size)
        dst = lambda span: cols.at[span, pl.ds(at, size)]
        return load(i, h, parts[2 * i + h], dst, sem_cols)

    def row(i, h):
        return load(i, h, blocks[2 * i + h], lambda span: rows.at[i, span], sem_rows)

    def store(i):
        at = slots[nparts + i] if placed else i
        return pltpu.make_async_copy(tile.at[i], out.at[at], sem_out.at[i])

    for i in range(nparts):
        for h in (0, 1):
            column(i, h).start()
    for i in range(nblocks):
        for h in (0, 1):
            row(i, h).start()
    for i in range(nparts):
        for h in (0, 1):
            column(i, h).wait()
    for i in range(nblocks):
        for h in (0, 1):
            row(i, h).wait()
        value = lax.dot_general(
            rows[i], cols[...], (((0,), (0,)), ((), ())), preferred_element_type=jnp.float32
        )
        value = value * value
        value = value * value
        if placed:
            for a in range(nparts):
                tile[i, :, a, :] = value[:, a * size : (a + 1) * size]
        else:
            tile[i] = value * SCALE
        store(i).start()
    for i in range(nblocks):
        store(i).wait()


def products(blocks, parts, slots, out=None, shape=None):
    nparts, nblocks = len(parts), len(blocks)
    cut, size = blocks[0][0].shape
    features = cut + blocks[0][1].shape[0]
    placed = shape is not None
    operands = [slots] + [h for part in parts for h in part] + [h for b in blocks for h in b]
    alias = {}
    if out is not None:
        alias = {len(operands): 0}
        operands.append(out)
    panel = (size, nparts, size) if placed else (size, nparts * size)
    return pl.pallas_call(
        functools.partial(product_kernel, nparts, nblocks, cut, placed),
        out_shape=jax.ShapeDtypeStruct(shape if placed else (nblocks,) + panel, jnp.float32),
        in_specs=[SMEM] + [HBM] * (len(operands) - 1),
        out_specs=HBM,
        input_output_aliases=alias,
        scratch_shapes=[
            pltpu.VMEM((features, nparts * size), jnp.bfloat16),
            pltpu.VMEM((nblocks, features, size), jnp.bfloat16),
            pltpu.VMEM((nblocks,) + panel, jnp.float32),
            pltpu.SemaphoreType.DMA((nparts, 2)),
            pltpu.SemaphoreType.DMA((nblocks, 2)),
            pltpu.SemaphoreType.DMA((nblocks,)),
        ],
        cost_estimate=pl.CostEstimate(
            flops=2 * nblocks * size * features * nparts * size,
            bytes_accessed=2 * (nparts + nblocks) * features * size,
            transcendentals=0,
        ),
    )(*operands)


def place_kernel(count, slots, panels, old, out, tile, sem):
    del old
    size, nparts = tile.shape[1], tile.shape[2]

    def store(i):
        return pltpu.make_async_copy(tile.at[i], out.at[slots[i]], sem.at[i])

    @pl.when(slots[count] == 0)
    def _():
        for i in range(count):
            value = panels[i]
            for a in range(nparts):
                tile[i, :, a, :] = value[:, a * size : (a + 1) * size]
            store(i).start()
        for i in range(count):
            store(i).wait()


def place(panels, slots, out):
    count, size = panels.shape[:2]
    nparts = panels.shape[2] // size
    return pl.pallas_call(
        functools.partial(place_kernel, count),
        out_shape=jax.ShapeDtypeStruct(out.shape, out.dtype),
        in_specs=[SMEM, VMEM, HBM],
        out_specs=HBM,
        input_output_aliases={2: 0},
        scratch_shapes=[
            pltpu.VMEM((count, size, nparts, size), jnp.float32),
            pltpu.SemaphoreType.DMA((count,)),
        ],
        cost_estimate=pl.CostEstimate(flops=0, bytes_accessed=8 * panels.size, transcendentals=0),
        name="place",
    )(slots, panels, out)


def shards(descriptors):
    return exchange(descriptors)


def exchange(descriptors):
    ngroups = lax.axis_size("grp")
    ncolumns = lax.axis_size("col")
    block = descriptors.shape[0]
    inner = ncolumns // LINE
    offsets = range(1, inner)
    grp = lax.axis_index("grp")
    col = lax.axis_index("col")
    z, x = col // inner, col % inner
    middle = jnp.logical_or(z == 1, z == 2)

    def mid(zz):
        return zz in (1, 2)

    def send(array, move):
        pairs = []
        for g in range(ngroups):
            for c in range(ncolumns):
                tg, tz, tx = move(g, c // inner, c % inner)
                pairs.append((g * ncolumns + c, (tg * LINE + tz) * inner + tx % inner))
        return lax.ppermute(array, AXES, pairs)

    def line_swap(g, zz, xx):
        return g, zz ^ 1, xx

    def centre_swap(k):
        if k % inner == 0:
            return lambda g, zz, xx: (g, zz ^ 3, xx) if mid(zz) else (g ^ 1, zz, xx)
        return lambda g, zz, xx: (g, zz ^ 3, xx) if mid(zz) else (g, zz, xx - k)

    def shift(k, ends):
        if ends % inner == 0:
            return lambda g, zz, xx: (g, zz, xx - k) if mid(zz) else (g ^ 1, zz, xx)
        return lambda g, zz, xx: (g, zz, xx - (k if mid(zz) else ends))

    def other(j):
        return lambda g, zz, xx: ((g - j) % ngroups, zz, xx)

    def core_swap(g, zz, xx):
        return g ^ 1, zz, xx

    data = descriptors.T
    cut = data.shape[0] // 32 * 16
    unit = normalize(data, cut)
    others = range(2, ngroups, 2)
    halves = (0, 1)
    head, pair = [None, None], [None, None]
    across = [[None, None] for _ in offsets]
    own = {0: unit}
    for j in others:
        own[j] = [None, None]
    for h in halves:
        head[h] = send(unit[h], centre_swap(1))
        pair[h] = send(unit[h], line_swap)
        for k in offsets:
            across[k - 1][h] = send(unit[h], shift(k, k + 1))
        for j in others:
            own[j][h] = send(unit[h], other(j))
    relay, head_pair, end = [None, None], [None, None], {0: pair}
    across_pair = [[None, None] for _ in range(2, inner)]
    centre_across = [[None, None] for _ in offsets]
    for j in others:
        end[j] = [None, None]
    for h in halves:
        relay[h] = send(pair[h], centre_swap(inner - 1))
        for k in offsets:
            centre_across[k - 1][h] = send(head[h], shift(k, 0))
        head_pair[h] = send(head[h], line_swap)
        for k in range(2, inner):
            across_pair[k - 2][h] = send(across[k - 2][h], line_swap)
        for j in others:
            end[j][h] = send(pair[h], other(j))

    def with_cores(parts):
        full, at = [], []
        for j in sorted(parts):
            full += [parts[j], [send(part, core_swap) for part in parts[j]]]
            at += [(grp + j) % ngroups, ((grp ^ 1) + j) % ngroups]
        return full, at

    def slot(dz, k):
        return (z ^ dz) * inner + (x + k) % inner

    def where(for_middle, for_end):
        return jnp.where(middle, slot(*for_middle), slot(*for_end))

    def table(values):
        return jnp.stack([jnp.asarray(v, jnp.int32) for v in values])

    columns, columns_at = with_cores(own)
    shape = (ncolumns, block, ngroups, block)
    early = [(unit, slot(0, 0)), (pair, slot(1, 0)), (head, where((3, 0), (0, 1)))]
    for k in offsets:
        ends = (0, k + 1) if k + 1 < inner else (3, 0)
        early.append((across[k - 1], where((0, k), ends)))
    out = products(
        [b for b, _ in early], columns, table(columns_at + [at for _, at in early]), shape=shape,
    )
    end_columns, _ = with_cores(end)
    far_across = []
    for k in offsets:
        source = head_pair if k == 1 else across_pair[k - 2]
        second = send(source[1], centre_swap(0))
        far_across.append([send(relay[0], shift(k, 0)), second])

    def back(blocks):
        panels = products(blocks, end_columns, table(columns_at))
        return send(panels.astype(jnp.float16), line_swap)

    returned = [back([relay] + centre_across), back(far_across)]
    late = [(head_pair, where((1, 1), (2, 0))), (relay, where((2, 0), (1, inner - 1)))]
    for k in range(2, inner):
        late.append((across_pair[k - 2], where((1, k), (1, k - 1))))
    late += [(b, where((3, k), (2, k))) for k, b in zip(offsets, centre_across)]
    late += [(b, where((2, k), (3, k))) for k, b in zip(offsets, far_across)]
    out = products(
        [b for b, _ in late], columns, table(columns_at + [at for _, at in late]), out=out,
        shape=shape,
    )
    panels = jnp.concatenate(returned).astype(jnp.float32) * (1.0 / SCALE)
    slots = [slot(3, 0)] + [slot(2, k) for k in offsets] + [slot(3, k) for k in offsets]
    out = place(panels, table(slots + [middle]), out)
    return out.reshape(ncolumns * block, ngroups, block)


def plain(descriptors):
    squares = jnp.sum(descriptors * descriptors, axis=1, keepdims=True)
    unit = (descriptors * lax.rsqrt(squares + 1e-06)).astype(jnp.bfloat16)
    columns = lax.all_gather(unit, "grp", axis=0, tiled=True)
    rows = lax.all_gather(unit, "col", axis=0, tiled=True)
    intersection = jnp.dot(rows, columns.T, preferred_element_type=jnp.float32)
    second = intersection * intersection
    return (second * second).reshape(rows.shape[0], -1, unit.shape[0])


def solution(mesh):
    ngroups, ncolumns = mesh.shape["grp"], mesh.shape["col"]
    fits = ncolumns % (2 * LINE) == 0 and ngroups % 2 == 0
    return jax.shard_map(
        shards if fits else plain,
        mesh=mesh,
        in_specs=(P(AXES, None),),
        out_specs=P("grp", None, "col"),
        check_vma=False,
    )
```

time: 125 us -> 75.8 us (0.61)
  waiting for transfers between devices: 101 us -> 15.4 us
  starting transfers between devices: 0.04 us -> 28 us
  Pallas kernels: 0 us -> 24.8 us
  between operations: 13.4 us -> 0.24 us
  matrix products: 5.18 us -> 0 us
    all_gather x2 -> x0, waiting for transfers between devices: 100 us -> none  [the longest x1 75.6 us: shards(): tile = fourth(lax.all_gather(unit, 'col', axis=0, tiled=True), columns)]
    ppermute x0 -> x28, starting transfers between devices: none -> 28 us  [send(): return lax.ppermute(array, AXES, pairs)]
    pallas_call x0 -> x6, Pallas kernels: none -> 24.8 us  [the longest x4 20.1 us: products(): pl.pallas_call(functools.partial(product_kernel, nparts, nblocks, cut, pl...]
    ppermute x0 -> x28, waiting for transfers between devices: none -> 15.4 us  [send(): return lax.ppermute(array, AXES, pairs)]
    dot_general x1 -> x0, matrix products: 5.18 us -> none  [fourth(): lax.dot_general(left, right, (((1,), (1,)), ((), ())), preferred_element_...]
    reshape x1 -> x0, local copies, waits for them, and re-layouts: 1.81 us -> none  [shards(): return tile.reshape(ncolumns * block, ngroups, block)]
    reduce_sum x1 -> x0, other arithmetic: 1.49 us -> none  [shards(): squares = jnp.sum(descriptors * descriptors, axis=1, keepdims=True)]
    another operation x0 -> x2, local copies, waits for them, and re-layouts: none -> 1.37 us  [table(): return jnp.stack([jnp.asarray(v, jnp.int32) for v in values])]
  transfers between devices with their start and end apart: 2 -> 28, of which waited for: 2 -> 8; matrix products, arithmetic and copies ran while one was open for 0% -> 6% of each run, Pallas kernels for 0% -> 27%
where the time goes in v1:
time: 75.8 us; the launch traced here: 75.4 us
  starting transfers between devices  28 us (37%)
  Pallas kernels  24.8 us (33%)
  waiting for transfers between devices  15.4 us (20%)
  other arithmetic  4.29 us (6%)
  local copies, waits for them, and re-layouts  2.71 us (4%)
    ppermute x28, starting transfers between devices, send(): return lax.ppermute(array, AXES, pairs)  28 us
    pallas_call x4, Pallas kernels, products(): pl.pallas_call(functools.partial(product_kernel, nparts, nblocks, cut, pl...  20.1 us
    ppermute x28, waiting for transfers between devices, send(): return lax.ppermute(array, AXES, pairs)  15.4 us
    pallas_call x1, Pallas kernels, normalize(): pl.pallas_call(functools.partial(unit_kernel, cut), out_shape=[jax.ShapeD...  2.32 us
    pallas_call x1, Pallas kernels, place(): pl.pallas_call(functools.partial(place_kernel, count), out_shape=jax.Shap...  2.31 us
    convert_element_type x2, other arithmetic, back(): return send(panels.astype(jnp.float16), line_swap)  2.05 us
  transfers between devices with their start and end apart: 28, of which 8 were waited for; matrix products, arithmetic and copies ran while one was open for 6% of the time, Pallas kernels for 27%

profile of v1, /device:TPU:0, one launch (start us, length us, event | category | flops | bytes accessed | tf_op | source)
XLA Modules:
  0.0 75.4 jit_solution(1938524577100215835)
XLA Ops:
  0.0 2.3 %normalize.1 = (bf16[992,128]{1,0:T(8,128)(2,1)}, bf16[1008,128]{1,0:T(8,128)(2,1)}) custom-call(f32[2000,128]{1,0:T(8,128)} %bitcast.18), custom_call_target="tpu_custom_call" | custom-call | bytes 1536000 | tf_op jit(solution)/shard_map/normalize/pallas_call | solution.py:30
  2.3 3.1 %collective-permute-start = (bf16[992,128]{1,0:T(8,128)(2,1)}, bf16[992,128]{1,0:T(8,128)(2,1)S(1)}, u32[]{:S(2)}, u32[]{:S(2)}) collective-permute-start(bf16[992,128]{1,0:T(8,128)(2,1)} %get-tuple-element.7.refs_1_.refs_9_), channel_id=1, source_target_pairs={{0,2},{1,3},{2,0},{3,1},{4,6},{5,7},{6,4},{7,5},{8,10},{9,11},{10,... | collective-permute-start | bytes 761864 | tf_op jit(solution)/shard_map/ppermute | solution.py:185
  5.4 1.5 %collective-permute-start.21 = (bf16[992,128]{1,0:T(8,128)(2,1)}, bf16[992,128]{1,0:T(8,128)(2,1)S(1)}, u32[]{:S(2)}, u32[]{:S(2)}) collective-permute-start(bf16[992,128]{1,0:T(8,128)(2,1)} %get-tuple-element.7.refs_1_.refs_9_), channel_id=1, source_target_pairs={{0,16},{1,17},{2,18},{3,19},{4,20},{5,21},{6,22},{7,23},{8,24},{9,... | collective-permute-start | bytes 761864 | tf_op jit(solution)/shard_map/ppermute | solution.py:185
  6.9 1.5 %collective-permute-start.10 = (bf16[992,128]{1,0:T(8,128)(2,1)}, bf16[992,128]{1,0:T(8,128)(2,1)}, u32[]{:S(2)}, u32[]{:S(2)}) collective-permute-start(bf16[992,128]{1,0:T(8,128)(2,1)} %get-tuple-element.7.refs_1_.refs_9_), channel_id=1, source_target_pairs={{0,1},{1,0},{2,4},{3,5},{4,2},{5,3},{6,7},{7,6},{8,9},{9,8},{10,12... | collective-permute-start | bytes 761864 | tf_op jit(solution)/shard_map/ppermute | solution.py:185
  8.4 0.5 collective-permute-start.26
  8.9 2.8 %collective-permute-done.refs_1_.refs_11_ = bf16[992,128]{1,0:T(8,128)(2,1)S(1)} collective-permute-done((bf16[992,128]{1,0:T(8,128)(2,1)}, bf16[992,128]{1,0:T(8,128)(2,1)S(1)}, u32[]{:S(2)}, u32[]{:S(2)}) %collective-permute-start) | collective-permute-done | bytes 253984 | tf_op jit(solution)/shard_map/ppermute | solution.py:185
  11.7 1.7 %collective-permute-start.1 = (bf16[1008,128]{1,0:T(8,128)(2,1)}, bf16[1008,128]{1,0:T(8,128)(2,1)S(1)}, u32[]{:S(2)}, u32[]{:S(2)}) collective-permute-start(bf16[1008,128]{1,0:T(8,128)(2,1)} %get-tuple-element.8.refs_2_.refs_10_), channel_id=1, source_target_pairs={{0,2},{1,3},{2,0},{3,1},{4,6},{5,7},{6,4},{7,5},{8,10},{9,11},{10,... | collective-permute-start | bytes 774152 | tf_op jit(solution)/shard_map/ppermute | solution.py:185
  13.5 0.0 collective-permute-done.21.refs_5_
  13.5 1.5 %collective-permute-start.22 = (bf16[1008,128]{1,0:T(8,128)(2,1)}, bf16[1008,128]{1,0:T(8,128)(2,1)S(1)}, u32[]{:S(2)}, u32[]{:S(2)}) collective-permute-start(bf16[1008,128]{1,0:T(8,128)(2,1)} %get-tuple-element.8.refs_2_.refs_10_), channel_id=1, source_target_pairs={{0,16},{1,17},{2,18},{3,19},{4,20},{5,21},{6,22},{7,23},{8,24},{9,... | collective-permute-start | bytes 774152 | tf_op jit(solution)/shard_map/ppermute | solution.py:185
  15.0 1.5 %collective-permute-start.12 = (bf16[1008,128]{1,0:T(8,128)(2,1)}, bf16[1008,128]{1,0:T(8,128)(2,1)S(1)}, u32[]{:S(2)}, u32[]{:S(2)}) collective-permute-start(bf16[1008,128]{1,0:T(8,128)(2,1)} %get-tuple-element.8.refs_2_.refs_10_), channel_id=1, source_target_pairs={{0,1},{1,0},{2,4},{3,5},{4,2},{5,3},{6,7},{7,6},{8,9},{9,8},{10,12... | collective-permute-start | bytes 774152 | tf_op jit(solution)/shard_map/ppermute | solution.py:185
  16.5 0.0 collective-permute-done.26.refs_15_
  16.5 0.6 collective-permute-start.8
  17.1 2.3 %collective-permute-done.1.refs_2_.refs_12_ = bf16[1008,128]{1,0:T(8,128)(2,1)S(1)} collective-permute-done((bf16[1008,128]{1,0:T(8,128)(2,1)}, bf16[1008,128]{1,0:T(8,128)(2,1)S(1)}, u32[]{:S(2)}, u32[]{:S(2)}) %collective-permute-start.1) | collective-permute-done | bytes 258080 | tf_op jit(solution)/shard_map/ppermute | solution.py:185
  19.4 0.0 collective-permute-start.11
  19.4 1.2 %collective-permute-done.22.refs_6_ = bf16[1008,128]{1,0:T(8,128)(2,1)S(1)} collective-permute-done((bf16[1008,128]{1,0:T(8,128)(2,1)}, bf16[1008,128]{1,0:T(8,128)(2,1)S(1)}, u32[]{:S(2)}, u32[]{:S(2)}) %collective-permute-start.22) | collective-permute-done | bytes 258080 | tf_op jit(solution)/shard_map/ppermute | solution.py:185
  20.6 1.5 %collective-permute-start.4 = (bf16[992,128]{1,0:T(8,128)(2,1)S(1)}, bf16[992,128]{1,0:T(8,128)(2,1)}, u32[]{:S(2)}, u32[]{:S(2)}) collective-permute-start(bf16[992,128]{1,0:T(8,128)(2,1)S(1)} %collective-permute-done.refs_1_.refs_11_), channel_id=1, source_target_pairs={{0,16},{1,17},{2,18},{3,19},{4,20},{5,21},{6,22},{7,23},{8,24},{9,... | collective-permute-start | bytes 761864 | tf_op jit(solution)/shard_map/ppermute | solution.py:185
  22.1 2.0 %collective-permute-done.12.refs_14_ = bf16[1008,128]{1,0:T(8,128)(2,1)S(1)} collective-permute-done((bf16[1008,128]{1,0:T(8,128)(2,1)}, bf16[1008,128]{1,0:T(8,128)(2,1)S(1)}, u32[]{:S(2)}, u32[]{:S(2)}) %collective-permute-start.12) | collective-permute-done | bytes 258080 | tf_op jit(solution)/shard_map/ppermute | solution.py:185
  24.1 0.0 collective-permute-start.2
  24.1 1.7 %collective-permute-start.9 = (bf16[1008,128]{1,0:T(8,128)(2,1)S(1)}, bf16[1008,128]{1,0:T(8,128)(2,1)S(1)}, u32[]{:S(2)}, u32[]{:S(2)}) collective-permute-start(bf16[1008,128]{1,0:T(8,128)(2,1)S(1)} %collective-permute-done.1.refs_2_.refs_12_), channel_id=1, source_target_pairs={{0,1},{1,0},{2,4},{3,5},{4,2},{5,3},{6,7},{7,6},{8,9},{9,8},{10,12... | collective-permute-start | bytes 774152 | tf_op jit(solution)/shard_map/ppermute | solution.py:185
  25.9 1.6 %collective-permute-done.8.refs_9_.refs_11_ = bf16[992,128]{1,0:T(8,128)(2,1)} collective-permute-done((bf16[992,128]{1,0:T(8,128)(2,1)S(1)}, bf16[992,128]{1,0:T(8,128)(2,1)}, u32[]{:S(2)}, u32[]{:S(2)}) %collective-permute-start.8) | collective-permute-done | bytes 253984 | tf_op jit(solution)/shard_map/ppermute | solution.py:185
  27.5 1.4 %collective-permute-start.16 = (bf16[1008,128]{1,0:T(8,128)(2,1)S(1)}, bf16[1008,128]{1,0:T(8,128)(2,1)}, u32[]{:S(2)}, u32[]{:S(2)}) collective-permute-start(bf16[1008,128]{1,0:T(8,128)(2,1)S(1)} %collective-permute-done.12.refs_14_), channel_id=1, source_target_pairs={{0,2},{1,3},{2,0},{3,1},{4,6},{5,7},{6,4},{7,5},{8,10},{9,11},{10,... | collective-permute-start | bytes 774152 | tf_op jit(solution)/shard_map/ppermute | solution.py:185
  28.8 0.5 collective-permute-start.5
  29.3 0.2 copy-done.14
  29.5 0.5 collective-permute-start.3
  30.1 2.8 %collective-permute-done.9.refs_10_.refs_12_ = bf16[1008,128]{1,0:T(8,128)(2,1)S(1)} collective-permute-done((bf16[1008,128]{1,0:T(8,128)(2,1)S(1)}, bf16[1008,128]{1,0:T(8,128)(2,1)S(1)}, u32[]{:S(2)}, u32[]{:S(2)}) %collective-permute-start.9) | collective-permute-done | bytes 258080 | tf_op jit(solution)/shard_map/ppermute | solution.py:185
  32.8 1.4 %collective-permute-done.16.refs_10_ = bf16[1008,128]{1,0:T(8,128)(2,1)} collective-permute-done((bf16[1008,128]{1,0:T(8,128)(2,1)S(1)}, bf16[1008,128]{1,0:T(8,128)(2,1)}, u32[]{:S(2)}, u32[]{:S(2)}) %collective-permute-start.16) | collective-permute-done | bytes 258080 | tf_op jit(solution)/shard_map/ppermute | solution.py:185
  34.2 1.3 %collective-permute-done.5.refs_6_ = bf16[1008,128]{1,0:T(8,128)(2,1)S(1)} collective-permute-done((bf16[1008,128]{1,0:T(8,128)(2,1)S(1)}, bf16[1008,128]{1,0:T(8,128)(2,1)S(1)}, u32[]{:S(2)}, u32[]{:S(2)}) %collective-permute-start.5) | collective-permute-done | bytes 258080 | tf_op jit(solution)/shard_map/ppermute | solution.py:185
  35.6 0.6 collective-permute-start.17
  36.1 0.2 collective-permute-start.27
  36.3 0.3 collective-permute-start.23
  36.6 0.4 copy-done.13
  37.0 0.3 collective-permute-start.24
  37.4 0.6 pad_add_fusion.1.refs_0_
  38.0 6.9 %collective-permute-start.25 = (bf16[992,128]{1,0:T(8,128)(2,1)}, bf16[992,128]{1,0:T(8,128)(2,1)}, u32[]{:S(2)}, u32[]{:S(2)}) collective-permute-start(bf16[992,128]{1,0:T(8,128)(2,1)} %collective-permute-done.10.refs_13_), channel_id=1, source_target_pairs={{0,2},{1,3},{2,0},{3,1},{4,6},{5,7},{6,4},{7,5},{8,10},{9,11},{10,... | collective-permute-start | bytes 761864 | tf_op jit(solution)/shard_map/ppermute | solution.py:185
  44.9 4.3 %shard_map.17 = f32[2,128,512]{2,1,0:T(8,128)} custom-call(s32[4]{0:T(128)} %pad_add_fusion.1.refs_0_, bf16[992,128]{1,0:T(8,128)(2,1)} %copy-done.1, bf16[1008,128]{1,0:T(8,128)(2,1)} %copy-done, bf16[992,128]{1,0:T(8,128)(2,1)} %collective-permute-done.2.refs_3_, bf16[1008,128]{1,0:T(8,128)(2,1)} %copy-done.3, ...), custom_call_target="tpu_custom_call" | custom-call | flops 524288000 | bytes 3072000 | tf_op jit(solution)/shard_map/pallas_call | solution.py:103
  49.3 1.1 %convert_element_type.10 = f16[2,128,512]{2,1,0:T(8,128)(2,1)S(1)} convert(f32[2,128,512]{2,1,0:T(8,128)} %shard_map.17) | non-fusion elementwise | flops 131072 | bytes 786432 | tf_op jit(solution)/shard_map/convert_element_type | solution.py:272
  50.4 0.7 collective-permute-start.14
  51.1 0.6 pad_add_fusion.slots
  51.7 0.7 stack.96.refs_0_
  52.4 0.7 stack.91.refs_0_
  53.0 3.7 %shard_map.18 = f32[1,128,512]{2,1,0:T(8,128)} custom-call(s32[4]{0:T(128)} %pad_add_fusion.1.refs_0_, bf16[992,128]{1,0:T(8,128)(2,1)} %copy-done.1, bf16[1008,128]{1,0:T(8,128)(2,1)} %copy-done, bf16[992,128]{1,0:T(8,128)(2,1)} %collective-permute-done.2.refs_3_, bf16[1008,128]{1,0:T(8,128)(2,1)} %copy-done.3, ...), custom_call_target="tpu_custom_call" | custom-call | flops 262144000 | bytes 2560000 | tf_op jit(solution)/shard_map/pallas_call | solution.py:103
  56.8 1.0 %convert_element_type.11 = f16[1,128,512]{2,1,0:T(8,128)(2,1)S(1)} convert(f32[1,128,512]{2,1,0:T(8,128)} %shard_map.18) | non-fusion elementwise | flops 65536 | bytes 393216 | tf_op jit(solution)/shard_map/convert_element_type | solution.py:272
  57.7 1.5 %collective-permute-start.18 = (f16[1,128,512]{2,1,0:T(8,128)(2,1)S(1)}, f16[1,128,512]{2,1,0:T(8,128)(2,1)S(1)}, u32[]{:S(2)}, u32[]{:S(2)}) collective-permute-start(f16[1,128,512]{2,1,0:T(8,128)(2,1)S(1)} %convert_element_type.11), channel_id=1, source_target_pairs={{0,2},{1,3},{2,0},{3,1},{4,6},{5,7},{6,4},{7,5},{8,10},{9,11},{10,... | collective-permute-start | bytes 393224 | tf_op jit(solution)/shard_map/ppermute | solution.py:185
  59.3 0.7 copy-done.7
  60.0 6.0 %shard_map.19.refs_17_ = f32[8,128,4,128]{3,2,1,0:T(4,128)} custom-call(s32[8]{0:T(128)} %stack.96.refs_0_, bf16[992,128]{1,0:T(8,128)(2,1)} %get-tuple-element.7.refs_1_.refs_9_, bf16[1008,128]{1,0:T(8,128)(2,1)} %get-tuple-element.8.refs_2_.refs_10_, bf16[992,128]{1,0:T(8,128)(2,1)} %copy-done.12, bf16[1008,128]{1,0:T(8,128)(2,1)} %copy-done.6, ...), custom_call_target="tpu_custom_call" | custom-call | flops 1048576000 | bytes 4096000 | tf_op jit(solution)/shard_map/pallas_call | solution.py:103
  66.0 6.1 %shard_map.20.old = f32[8,128,4,128]{3,2,1,0:T(4,128)} custom-call(s32[8]{0:T(128)} %stack.91.refs_0_, bf16[992,128]{1,0:T(8,128)(2,1)} %get-tuple-element.7.refs_1_.refs_9_, bf16[1008,128]{1,0:T(8,128)(2,1)} %get-tuple-element.8.refs_2_.refs_10_, bf16[992,128]{1,0:T(8,128)(2,1)} %copy-done.12, ...), custom_call_target="tpu_custom_call", output_to_operand_aliasing={{}: (17, {})} | custom-call | flops 1048576000 | bytes 4096000 | tf_op jit(solution)/shard_map/pallas_call | solution.py:103
  72.1 1.0 %convert_multiply_fusion.panels = f32[3,128,512]{2,1,0:T(8,128)} fusion(f16[1,128,512]{2,1,0:T(8,128)(2,1)S(1)} %collective-permute-done.18, f16[2,128,512]{2,1,0:T(8,128)(2,1)S(1)} %collective-permute-done.14), kind=kLoop, calls=%fused_computation | loop fusion | flops 589824 | bytes 1179648 | tf_op jit(solution)/shard_map/mul | solution.py:284
  73.1 2.3 %place.1 = f32[8,128,4,128]{3,2,1,0:T(4,128)} custom-call(s32[4]{0:T(128)} %pad_add_fusion.slots, f32[3,128,512]{2,1,0:T(8,128)} %convert_multiply_fusion.panels, f32[8,128,4,128]{3,2,1,0:T(4,128)} %shard_map.20.old), custom_call_target="tpu_custom_call", output_to_operand_aliasing={{}: (2, {})} | custom-call | bytes 1572864 | tf_op jit(solution)/shard_map/place/pallas_call | solution.py:146
  (55 shorter events, 0.1 us)
Async XLA Ops:
  2.3 9.4 %collective-permute-start = (bf16[992,128]{1,0:T(8,128)(2,1)}, bf16[992,128]{1,0:T(8,128)(2,1)S(1)}, u32[]{:S(2)}, u32[]{:S(2)}) collective-permute-start(bf16[992,128]{1,0:T(8,128)(2,1)} %get-tuple-element.7.refs_1_.refs_9_), channel_id=1, source_target_pairs={{0,2},{1,3},{2,0},{3,1},{4,6},{5,7},{6,4},{7,5},{8,10},{9,11},{10,... | collective-permute-start | bytes 761864 | tf_op jit(solution)/shard_map/ppermute | solution.py:185
  5.4 8.1 %collective-permute-start.21 = (bf16[992,128]{1,0:T(8,128)(2,1)}, bf16[992,128]{1,0:T(8,128)(2,1)S(1)}, u32[]{:S(2)}, u32[]{:S(2)}) collective-permute-start(bf16[992,128]{1,0:T(8,128)(2,1)} %get-tuple-element.7.refs_1_.refs_9_), channel_id=1, source_target_pairs={{0,16},{1,17},{2,18},{3,19},{4,20},{5,21},{6,22},{7,23},{8,24},{9,... | collective-permute-start | bytes 761864 | tf_op jit(solution)/shard_map/ppermute | solution.py:185
  6.9 8.1 %collective-permute-start.10 = (bf16[992,128]{1,0:T(8,128)(2,1)}, bf16[992,128]{1,0:T(8,128)(2,1)}, u32[]{:S(2)}, u32[]{:S(2)}) collective-permute-start(bf16[992,128]{1,0:T(8,128)(2,1)} %get-tuple-element.7.refs_1_.refs_9_), channel_id=1, source_target_pairs={{0,1},{1,0},{2,4},{3,5},{4,2},{5,3},{6,7},{7,6},{8,9},{9,8},{10,12... | collective-permute-start | bytes 761864 | tf_op jit(solution)/shard_map/ppermute | solution.py:185
  8.4 8.1 %collective-permute-start.19 = (bf16[992,128]{1,0:T(8,128)(2,1)}, bf16[992,128]{1,0:T(8,128)(2,1)S(1)}, u32[]{:S(2)}, u32[]{:S(2)}) collective-permute-start(bf16[992,128]{1,0:T(8,128)(2,1)} %get-tuple-element.7.refs_1_.refs_9_), channel_id=1, source_target_pairs={{0,8},{1,9},{2,10},{3,11},{4,12},{5,13},{6,14},{7,15},{8,0},{9,1},... | collective-permute-start | bytes 761864 | tf_op jit(solution)/shard_map/ppermute | solution.py:185
  8.4 8.1 %collective-permute-start.26 = (bf16[992,128]{1,0:T(8,128)(2,1)}, bf16[992,128]{1,0:T(8,128)(2,1)S(1)}, u32[]{:S(2)}, u32[]{:S(2)}) collective-permute-start(bf16[992,128]{1,0:T(8,128)(2,1)} %get-tuple-element.7.refs_1_.refs_9_), channel_id=1, source_target_pairs={{0,8},{1,9},{2,3},{3,2},{4,5},{5,4},{6,14},{7,15},{8,0},{9,1},{10,... | collective-permute-start | bytes 761864 | tf_op jit(solution)/shard_map/ppermute | solution.py:185
  11.7 33.2 %copy-start.1 = (bf16[992,128]{1,0:T(8,128)(2,1)}, bf16[992,128]{1,0:T(8,128)(2,1)S(1)}, u32[]{:S(2)}) copy-start(bf16[992,128]{1,0:T(8,128)(2,1)S(1)} %collective-permute-done.refs_1_.refs_11_) | copy-start | bytes 761860
  11.7 7.7 %collective-permute-start.1 = (bf16[1008,128]{1,0:T(8,128)(2,1)}, bf16[1008,128]{1,0:T(8,128)(2,1)S(1)}, u32[]{:S(2)}, u32[]{:S(2)}) collective-permute-start(bf16[1008,128]{1,0:T(8,128)(2,1)} %get-tuple-element.8.refs_2_.refs_10_), channel_id=1, source_target_pairs={{0,2},{1,3},{2,0},{3,1},{4,6},{5,7},{6,4},{7,5},{8,10},{9,11},{10,... | collective-permute-start | bytes 774152 | tf_op jit(solution)/shard_map/ppermute | solution.py:185
  13.5 45.8 %copy-start.11 = (bf16[992,128]{1,0:T(8,128)(2,1)}, bf16[992,128]{1,0:T(8,128)(2,1)S(1)}, u32[]{:S(2)}) copy-start(bf16[992,128]{1,0:T(8,128)(2,1)S(1)} %collective-permute-done.21.refs_5_) | copy-start | bytes 761860
  13.5 7.1 %collective-permute-start.22 = (bf16[1008,128]{1,0:T(8,128)(2,1)}, bf16[1008,128]{1,0:T(8,128)(2,1)S(1)}, u32[]{:S(2)}, u32[]{:S(2)}) collective-permute-start(bf16[1008,128]{1,0:T(8,128)(2,1)} %get-tuple-element.8.refs_2_.refs_10_), channel_id=1, source_target_pairs={{0,16},{1,17},{2,18},{3,19},{4,20},{5,21},{6,22},{7,23},{8,24},{9,... | collective-permute-start | bytes 774152 | tf_op jit(solution)/shard_map/ppermute | solution.py:185
  15.0 9.1 %collective-permute-start.12 = (bf16[1008,128]{1,0:T(8,128)(2,1)}, bf16[1008,128]{1,0:T(8,128)(2,1)S(1)}, u32[]{:S(2)}, u32[]{:S(2)}) collective-permute-start(bf16[1008,128]{1,0:T(8,128)(2,1)} %get-tuple-element.8.refs_2_.refs_10_), channel_id=1, source_target_pairs={{0,1},{1,0},{2,4},{3,5},{4,2},{5,3},{6,7},{7,6},{8,9},{9,8},{10,12... | collective-permute-start | bytes 774152 | tf_op jit(solution)/shard_map/ppermute | solution.py:185
  16.5 42.7 %copy-start.12 = (bf16[992,128]{1,0:T(8,128)(2,1)}, bf16[992,128]{1,0:T(8,128)(2,1)S(1)}, u32[]{:S(2)}) copy-start(bf16[992,128]{1,0:T(8,128)(2,1)S(1)} %collective-permute-done.19.refs_3_) | copy-start | bytes 761860
  16.5 7.6 %collective-permute-start.20 = (bf16[1008,128]{1,0:T(8,128)(2,1)}, bf16[1008,128]{1,0:T(8,128)(2,1)S(1)}, u32[]{:S(2)}, u32[]{:S(2)}) collective-permute-start(bf16[1008,128]{1,0:T(8,128)(2,1)} %get-tuple-element.8.refs_2_.refs_10_), channel_id=1, source_target_pairs={{0,8},{1,9},{2,10},{3,11},{4,12},{5,13},{6,14},{7,15},{8,0},{9,1},... | collective-permute-start | bytes 774152 | tf_op jit(solution)/shard_map/ppermute | solution.py:185
  16.5 13.6 %copy-start.16 = (bf16[992,128]{1,0:T(8,128)(2,1)}, bf16[992,128]{1,0:T(8,128)(2,1)S(1)}, u32[]{:S(2)}) copy-start(bf16[992,128]{1,0:T(8,128)(2,1)S(1)} %collective-permute-done.26.refs_15_) | copy-start | bytes 761860
  16.5 11.0 %collective-permute-start.8 = (bf16[992,128]{1,0:T(8,128)(2,1)S(1)}, bf16[992,128]{1,0:T(8,128)(2,1)}, u32[]{:S(2)}, u32[]{:S(2)}) collective-permute-start(bf16[992,128]{1,0:T(8,128)(2,1)S(1)} %collective-permute-done.refs_1_.refs_11_), channel_id=1, source_target_pairs={{0,1},{1,0},{2,4},{3,5},{4,2},{5,3},{6,7},{7,6},{8,9},{9,8},{10,12... | collective-permute-start | bytes 761864 | tf_op jit(solution)/shard_map/ppermute | solution.py:185
  19.4 25.5 %copy-start = (bf16[1008,128]{1,0:T(8,128)(2,1)}, bf16[1008,128]{1,0:T(8,128)(2,1)S(1)}, u32[]{:S(2)}) copy-start(bf16[1008,128]{1,0:T(8,128)(2,1)S(1)} %collective-permute-done.1.refs_2_.refs_12_) | copy-start | bytes 774148
  19.4 9.4 %collective-permute-start.11 = (bf16[992,128]{1,0:T(8,128)(2,1)}, bf16[992,128]{1,0:T(8,128)(2,1)S(1)}, u32[]{:S(2)}, u32[]{:S(2)}) collective-permute-start(bf16[992,128]{1,0:T(8,128)(2,1)} %collective-permute-done.10.refs_13_), channel_id=1, source_target_pairs={{0,8},{1,9},{2,3},{3,2},{4,5},{5,4},{6,14},{7,15},{8,0},{9,1},{10,... | collective-permute-start | bytes 761864 | tf_op jit(solution)/shard_map/ppermute | solution.py:185
  20.6 38.6 %copy-start.5 = (bf16[1008,128]{1,0:T(8,128)(2,1)}, bf16[1008,128]{1,0:T(8,128)(2,1)S(1)}, u32[]{:S(2)}) copy-start(bf16[1008,128]{1,0:T(8,128)(2,1)S(1)} %collective-permute-done.22.refs_6_) | copy-start | bytes 774148
  20.6 8.9 %collective-permute-start.4 = (bf16[992,128]{1,0:T(8,128)(2,1)S(1)}, bf16[992,128]{1,0:T(8,128)(2,1)}, u32[]{:S(2)}, u32[]{:S(2)}) collective-permute-start(bf16[992,128]{1,0:T(8,128)(2,1)S(1)} %collective-permute-done.refs_1_.refs_11_), channel_id=1, source_target_pairs={{0,16},{1,17},{2,18},{3,19},{4,20},{5,21},{6,22},{7,23},{8,24},{9,... | collective-permute-start | bytes 761864 | tf_op jit(solution)/shard_map/ppermute | solution.py:185
  24.1 11.4 %copy-start.15 = (bf16[1008,128]{1,0:T(8,128)(2,1)}, bf16[1008,128]{1,0:T(8,128)(2,1)S(1)}, u32[]{:S(2)}) copy-start(bf16[1008,128]{1,0:T(8,128)(2,1)S(1)} %collective-permute-done.12.refs_14_) | copy-start | bytes 774148
  24.1 5.5 %collective-permute-start.2 = (bf16[992,128]{1,0:T(8,128)(2,1)S(1)}, bf16[992,128]{1,0:T(8,128)(2,1)}, u32[]{:S(2)}, u32[]{:S(2)}) collective-permute-start(bf16[992,128]{1,0:T(8,128)(2,1)S(1)} %collective-permute-done.refs_1_.refs_11_), channel_id=1, source_target_pairs={{0,8},{1,9},{2,10},{3,11},{4,12},{5,13},{6,14},{7,15},{8,0},{9,1},... | collective-permute-start | bytes 761864 | tf_op jit(solution)/shard_map/ppermute | solution.py:185
  24.1 35.1 %copy-start.6 = (bf16[1008,128]{1,0:T(8,128)(2,1)}, bf16[1008,128]{1,0:T(8,128)(2,1)S(1)}, u32[]{:S(2)}) copy-start(bf16[1008,128]{1,0:T(8,128)(2,1)S(1)} %collective-permute-done.20.refs_4_) | copy-start | bytes 774148
  24.1 8.7 %collective-permute-start.9 = (bf16[1008,128]{1,0:T(8,128)(2,1)S(1)}, bf16[1008,128]{1,0:T(8,128)(2,1)S(1)}, u32[]{:S(2)}, u32[]{:S(2)}) collective-permute-start(bf16[1008,128]{1,0:T(8,128)(2,1)S(1)} %collective-permute-done.1.refs_2_.refs_12_), channel_id=1, source_target_pairs={{0,1},{1,0},{2,4},{3,5},{4,2},{5,3},{6,7},{7,6},{8,9},{9,8},{10,12... | collective-permute-start | bytes 774152 | tf_op jit(solution)/shard_map/ppermute | solution.py:185
  27.5 6.8 %collective-permute-start.16 = (bf16[1008,128]{1,0:T(8,128)(2,1)S(1)}, bf16[1008,128]{1,0:T(8,128)(2,1)}, u32[]{:S(2)}, u32[]{:S(2)}) collective-permute-start(bf16[1008,128]{1,0:T(8,128)(2,1)S(1)} %collective-permute-done.12.refs_14_), channel_id=1, source_target_pairs={{0,2},{1,3},{2,0},{3,1},{4,6},{5,7},{6,4},{7,5},{8,10},{9,11},{10,... | collective-permute-start | bytes 774152 | tf_op jit(solution)/shard_map/ppermute | solution.py:185
  28.8 0.7 copy-start.14
  28.8 6.7 %collective-permute-start.5 = (bf16[1008,128]{1,0:T(8,128)(2,1)S(1)}, bf16[1008,128]{1,0:T(8,128)(2,1)S(1)}, u32[]{:S(2)}, u32[]{:S(2)}) collective-permute-start(bf16[1008,128]{1,0:T(8,128)(2,1)S(1)} %collective-permute-done.1.refs_2_.refs_12_), channel_id=1, source_target_pairs={{0,16},{1,17},{2,18},{3,19},{4,20},{5,21},{6,22},{7,23},{8,24},{9,... | collective-permute-start | bytes 774152 | tf_op jit(solution)/shard_map/ppermute | solution.py:185
  29.5 6.0 %collective-permute-start.13 = (bf16[1008,128]{1,0:T(8,128)(2,1)S(1)}, bf16[1008,128]{1,0:T(8,128)(2,1)S(1)}, u32[]{:S(2)}, u32[]{:S(2)}) collective-permute-start(bf16[1008,128]{1,0:T(8,128)(2,1)S(1)} %collective-permute-done.12.refs_14_), channel_id=1, source_target_pairs={{0,8},{1,9},{2,3},{3,2},{4,5},{5,4},{6,14},{7,15},{8,0},{9,1},{10,... | collective-permute-start | bytes 774152 | tf_op jit(solution)/shard_map/ppermute | solution.py:185
  29.5 6.6 %collective-permute-start.3 = (bf16[1008,128]{1,0:T(8,128)(2,1)S(1)}, bf16[1008,128]{1,0:T(8,128)(2,1)S(1)}, u32[]{:S(2)}, u32[]{:S(2)}) collective-permute-start(bf16[1008,128]{1,0:T(8,128)(2,1)S(1)} %collective-permute-done.1.refs_2_.refs_12_), channel_id=1, source_target_pairs={{0,8},{1,9},{2,10},{3,11},{4,12},{5,13},{6,14},{7,15},{8,0},{9,1},... | collective-permute-start | bytes 774152 | tf_op jit(solution)/shard_map/ppermute | solution.py:185
  32.8 12.1 %copy-start.9 = (bf16[1008,128]{1,0:T(8,128)(2,1)}, bf16[1008,128]{1,0:T(8,128)(2,1)S(1)}, u32[]{:S(2)}) copy-start(bf16[1008,128]{1,0:T(8,128)(2,1)S(1)} %collective-permute-done.9.refs_10_.refs_12_) | copy-start | bytes 774148
  32.8 3.5 %collective-permute-start.15 = (bf16[992,128]{1,0:T(8,128)(2,1)}, bf16[992,128]{1,0:T(8,128)(2,1)S(1)}, u32[]{:S(2)}, u32[]{:S(2)}) collective-permute-start(bf16[992,128]{1,0:T(8,128)(2,1)} %collective-permute-done.8.refs_9_.refs_11_), channel_id=1, source_target_pairs={{0,8},{1,9},{2,3},{3,2},{4,5},{5,4},{6,14},{7,15},{8,0},{9,1},{10,... | collective-permute-start | bytes 761864 | tf_op jit(solution)/shard_map/ppermute | solution.py:185
  34.2 2.8 %collective-permute-start.6 = (bf16[992,128]{1,0:T(8,128)(2,1)}, bf16[992,128]{1,0:T(8,128)(2,1)}, u32[]{:S(2)}, u32[]{:S(2)}) collective-permute-start(bf16[992,128]{1,0:T(8,128)(2,1)} %collective-permute-done.4.refs_5_), channel_id=1, source_target_pairs={{0,8},{1,9},{2,10},{3,11},{4,12},{5,13},{6,14},{7,15},{8,0},{9,1},... | collective-permute-start | bytes 761864 | tf_op jit(solution)/shard_map/ppermute | solution.py:185
  35.5 9.4 %copy-start.2 = (bf16[1008,128]{1,0:T(8,128)(2,1)}, bf16[1008,128]{1,0:T(8,128)(2,1)S(1)}, u32[]{:S(2)}) copy-start(bf16[1008,128]{1,0:T(8,128)(2,1)S(1)} %collective-permute-done.5.refs_6_) | copy-start | bytes 774148
  35.5 2.4 %collective-permute-start.7 = (bf16[1008,128]{1,0:T(8,128)(2,1)S(1)}, bf16[1008,128]{1,0:T(8,128)(2,1)S(1)}, u32[]{:S(2)}, u32[]{:S(2)}) collective-permute-start(bf16[1008,128]{1,0:T(8,128)(2,1)S(1)} %collective-permute-done.5.refs_6_), channel_id=1, source_target_pairs={{0,8},{1,9},{2,10},{3,11},{4,12},{5,13},{6,14},{7,15},{8,0},{9,1},... | collective-permute-start | bytes 774152 | tf_op jit(solution)/shard_map/ppermute | solution.py:185
  35.5 9.4 %copy-start.10 = (bf16[1008,128]{1,0:T(8,128)(2,1)}, bf16[1008,128]{1,0:T(8,128)(2,1)S(1)}, u32[]{:S(2)}) copy-start(bf16[1008,128]{1,0:T(8,128)(2,1)S(1)} %collective-permute-done.13.refs_12_.refs_14_) | copy-start | bytes 774148
  35.6 14.8 %collective-permute-start.17 = (bf16[1008,128]{1,0:T(8,128)(2,1)}, bf16[1008,128]{1,0:T(8,128)(2,1)S(1)}, u32[]{:S(2)}, u32[]{:S(2)}) collective-permute-start(bf16[1008,128]{1,0:T(8,128)(2,1)} %collective-permute-done.16.refs_10_), channel_id=1, source_target_pairs={{0,8},{1,9},{2,4},{3,5},{4,2},{5,3},{6,14},{7,15},{8,0},{9,1},{10,... | collective-permute-start | bytes 774152 | tf_op jit(solution)/shard_map/ppermute | solution.py:185
  36.1 8.8 %copy-start.3 = (bf16[1008,128]{1,0:T(8,128)(2,1)}, bf16[1008,128]{1,0:T(8,128)(2,1)S(1)}, u32[]{:S(2)}) copy-start(bf16[1008,128]{1,0:T(8,128)(2,1)S(1)} %collective-permute-done.3.refs_4_) | copy-start | bytes 774148
  36.1 21.6 %collective-permute-start.27 = (bf16[1008,128]{1,0:T(8,128)(2,1)}, bf16[1008,128]{1,0:T(8,128)(2,1)}, u32[]{:S(2)}, u32[]{:S(2)}) collective-permute-start(bf16[1008,128]{1,0:T(8,128)(2,1)} %get-tuple-element.8.refs_2_.refs_10_), channel_id=1, source_target_pairs={{0,8},{1,9},{2,3},{3,2},{4,5},{5,4},{6,14},{7,15},{8,0},{9,1},{10,... | collective-permute-start | bytes 774152 | tf_op jit(solution)/shard_map/ppermute | solution.py:185
  36.3 0.7 copy-start.13
  36.3 22.9 %collective-permute-start.23 = (bf16[992,128]{1,0:T(8,128)(2,1)S(1)}, bf16[992,128]{1,0:T(8,128)(2,1)}, u32[]{:S(2)}, u32[]{:S(2)}) collective-permute-start(bf16[992,128]{1,0:T(8,128)(2,1)S(1)} %collective-permute-done.21.refs_5_), channel_id=1, source_target_pairs={{0,8},{1,9},{2,10},{3,11},{4,12},{5,13},{6,14},{7,15},{8,0},{9,1},... | collective-permute-start | bytes 761864 | tf_op jit(solution)/shard_map/ppermute | solution.py:185
  37.0 22.2 %collective-permute-start.24 = (bf16[1008,128]{1,0:T(8,128)(2,1)S(1)}, bf16[1008,128]{1,0:T(8,128)(2,1)S(1)}, u32[]{:S(2)}, u32[]{:S(2)}) collective-permute-start(bf16[1008,128]{1,0:T(8,128)(2,1)S(1)} %collective-permute-done.22.refs_6_), channel_id=1, source_target_pairs={{0,8},{1,9},{2,10},{3,11},{4,12},{5,13},{6,14},{7,15},{8,0},{9,1},... | collective-permute-start | bytes 774152 | tf_op jit(solution)/shard_map/ppermute | solution.py:185
  38.0 7.0 %copy-start.4 = (bf16[1008,128]{1,0:T(8,128)(2,1)}, bf16[1008,128]{1,0:T(8,128)(2,1)S(1)}, u32[]{:S(2)}) copy-start(bf16[1008,128]{1,0:T(8,128)(2,1)S(1)} %collective-permute-done.7.refs_8_) | copy-start | bytes 774148
  38.0 28.0 %collective-permute-start.25 = (bf16[992,128]{1,0:T(8,128)(2,1)}, bf16[992,128]{1,0:T(8,128)(2,1)}, u32[]{:S(2)}, u32[]{:S(2)}) collective-permute-start(bf16[992,128]{1,0:T(8,128)(2,1)} %collective-permute-done.10.refs_13_), channel_id=1, source_target_pairs={{0,2},{1,3},{2,0},{3,1},{4,6},{5,7},{6,4},{7,5},{8,10},{9,11},{10,... | collective-permute-start | bytes 761864 | tf_op jit(solution)/shard_map/ppermute | solution.py:185
  50.3 2.7 %copy-start.8 = (bf16[1008,128]{1,0:T(8,128)(2,1)}, bf16[1008,128]{1,0:T(8,128)(2,1)S(1)}, u32[]{:S(2)}) copy-start(bf16[1008,128]{1,0:T(8,128)(2,1)S(1)} %collective-permute-done.17.refs_10_.refs_16_) | copy-start | bytes 774148
  50.4 21.7 %collective-permute-start.14 = (f16[2,128,512]{2,1,0:T(8,128)(2,1)S(1)}, f16[2,128,512]{2,1,0:T(8,128)(2,1)S(1)}, u32[]{:S(2)}, u32[]{:S(2)}) collective-permute-start(f16[2,128,512]{2,1,0:T(8,128)(2,1)S(1)} %convert_element_type.10), channel_id=1, source_target_pairs={{0,2},{1,3},{2,0},{3,1},{4,6},{5,7},{6,4},{7,5},{8,10},{9,11},{10,... | collective-permute-start | bytes 786440 | tf_op jit(solution)/shard_map/ppermute | solution.py:185
  57.7 14.3 %collective-permute-start.18 = (f16[1,128,512]{2,1,0:T(8,128)(2,1)S(1)}, f16[1,128,512]{2,1,0:T(8,128)(2,1)S(1)}, u32[]{:S(2)}, u32[]{:S(2)}) collective-permute-start(f16[1,128,512]{2,1,0:T(8,128)(2,1)S(1)} %convert_element_type.11), channel_id=1, source_target_pairs={{0,2},{1,3},{2,0},{3,1},{4,6},{5,7},{6,4},{7,5},{8,10},{9,11},{10,... | collective-permute-start | bytes 393224 | tf_op jit(solution)/shard_map/ppermute | solution.py:185
  59.3 0.7 copy-start.7

commit v2 on v1

v2 whole, which is shorter than its diff:
```python
import functools

import jax
import jax.numpy as jnp
from jax import lax
from jax.experimental import pallas as pl
from jax.experimental.pallas import tpu as pltpu
from jax.sharding import PartitionSpec as P


AXES = ("grp", "col")
LINE = 4
SCALE = 32768.0


VMEM = pl.BlockSpec(memory_space=pltpu.VMEM)


def unit_kernel(cut, data, first, second):
    squares = jnp.sum(data[...] * data[...], axis=0, keepdims=True)
    scale = lax.rsqrt(squares + 1e-06)
    first[...] = (data[:cut] * scale).astype(jnp.bfloat16)
    second[...] = (data[cut:] * scale).astype(jnp.bfloat16)


def normalize(data, cut):
    features, block = data.shape
    return pl.pallas_call(
        functools.partial(unit_kernel, cut),
        out_shape=[
            jax.ShapeDtypeStruct((cut, block), jnp.bfloat16),
            jax.ShapeDtypeStruct((features - cut, block), jnp.bfloat16),
        ],
        in_specs=[VMEM],
        out_specs=[VMEM, VMEM],
        cost_estimate=pl.CostEstimate(flops=0, bytes_accessed=6 * data.size, transcendentals=0),
        name="normalize",
    )(data)


def shards(descriptors):
    return exchange(descriptors)


def exchange(descriptors):
    ngroups = lax.axis_size("grp")
    ncolumns = lax.axis_size("col")
    block = descriptors.shape[0]
    inner = ncolumns // LINE
    offsets = range(1, inner)
    grp = lax.axis_index("grp")
    col = lax.axis_index("col")
    z, x = col // inner, col % inner
    middle = jnp.logical_or(z == 1, z == 2)

    def mid(zz):
        return zz in (1, 2)

    def send(array, move):
        pairs = []
        for g in range(ngroups):
            for c in range(ncolumns):
                tg, tz, tx = move(g, c // inner, c % inner)
                pairs.append((g * ncolumns + c, (tg * LINE + tz) * inner + tx % inner))
        return lax.ppermute(array, AXES, pairs)

    def line_swap(g, zz, xx):
        return g, zz ^ 1, xx

    def centre_swap(k):
        if k % inner == 0:
            return lambda g, zz, xx: (g, zz ^ 3, xx) if mid(zz) else (g ^ 1, zz, xx)
        return lambda g, zz, xx: (g, zz ^ 3, xx) if mid(zz) else (g, zz, xx - k)

    def shift(k, ends):
        if ends % inner == 0:
            return lambda g, zz, xx: (g, zz, xx - k) if mid(zz) else (g ^ 1, zz, xx)
        return lambda g, zz, xx: (g, zz, xx - (k if mid(zz) else ends))

    def other(j):
        return lambda g, zz, xx: ((g - j) % ngroups, zz, xx)

    def core_swap(g, zz, xx):
        return g ^ 1, zz, xx

    data = descriptors.T
    cut = data.shape[0] // 32 * 16
    unit = normalize(data, cut)
    others = range(2, ngroups, 2)
    halves = (0, 1)
    head, pair = [None, None], [None, None]
    across = [[None, None] for _ in offsets]
    own = {0: unit}
    for j in others:
        own[j] = [None, None]
    for h in halves:
        head[h] = send(unit[h], centre_swap(1))
        pair[h] = send(unit[h], line_swap)
        for k in offsets:
            across[k - 1][h] = send(unit[h], shift(k, k + 1))
        for j in others:
            own[j][h] = send(unit[h], other(j))
    relay, head_pair, end = [None, None], [None, None], {0: pair}
    across_pair = [[None, None] for _ in range(2, inner)]
    centre_across = [[None, None] for _ in offsets]
    for j in others:
        end[j] = [None, None]
    for h in halves:
        relay[h] = send(pair[h], centre_swap(inner - 1))
        for k in offsets:
            centre_across[k - 1][h] = send(head[h], shift(k, 0))
        head_pair[h] = send(head[h], line_swap)
        for k in range(2, inner):
            across_pair[k - 2][h] = send(across[k - 2][h], line_swap)
        for j in others:
            end[j][h] = send(pair[h], other(j))

    def columns_of(parts):
        full = jnp.zeros((ngroups,) + data.shape, jnp.bfloat16)
        for j in sorted(parts):
            for h in halves:
                part = parts[j][h]
                swapped = send(part, core_swap)
                for array, at in ((part, grp + j), (swapped, (grp ^ 1) + j)):
                    start = (at % ngroups, h * cut, 0)
                    full = lax.dynamic_update_slice(full, array[None], start)
        return full

    def slot(dz, k):
        return (z ^ dz) * inner + (x + k) % inner

    def where(for_middle, for_end):
        return jnp.where(middle, slot(*for_middle), slot(*for_end))

    def fourth(block, cols):
        intersection = lax.dot_general(
            jnp.concatenate(block, axis=0),
            cols,
            (((0,), (1,)), ((), ())),
            preferred_element_type=jnp.float32,
        )
        second = intersection * intersection
        return second * second

    def product(block, cols):
        return lax.optimization_barrier(fourth(block, cols))

    def put(out, value, at):
        return lax.dynamic_update_index_in_dim(out, value, at, 0)

    columns = columns_of(own)
    early = [(unit, slot(0, 0)), (pair, slot(1, 0)), (head, where((3, 0), (0, 1)))]
    for k in offsets:
        ends = (0, k + 1) if k + 1 < inner else (3, 0)
        early.append((across[k - 1], where((0, k), ends)))
    out = jnp.zeros((ncolumns, block, ngroups, block), jnp.float32)
    for b, at in early:
        out = put(out, product(b, columns), at)
    end_columns = columns_of(end)
    far_across = []
    for k in offsets:
        source = head_pair if k == 1 else across_pair[k - 2]
        second = send(source[1], centre_swap(0))
        far_across.append([send(relay[0], shift(k, 0)), second])

    def back(blocks):
        panels = [(fourth(b, end_columns) * SCALE).astype(jnp.float16) for b in blocks]
        return send(jnp.stack(panels), line_swap)

    returned = back([relay] + centre_across)
    returned_far = back(far_across)
    late = [(head_pair, where((1, 1), (2, 0))), (relay, where((2, 0), (1, inner - 1)))]
    for k in range(2, inner):
        late.append((across_pair[k - 2], where((1, k), (1, k - 1))))
    late += [(b, where((3, k), (2, k))) for k, b in zip(offsets, centre_across)]
    for b, at in late:
        out = put(out, product(b, columns), at)
    for k, b in zip(offsets, far_across):
        out = put(out, product(b, columns), where((2, k), (3, k)))
    slots = [slot(3, 0)] + [slot(2, k) for k in offsets] + [slot(3, k) for k in offsets]
    panels = [returned[i] for i in range(inner)] + [returned_far[k - 1] for k in offsets]
    for at, panel in zip(slots, panels):
        old = lax.dynamic_index_in_dim(out, at, 0, keepdims=False)
        out = put(out, jnp.where(middle, old, panel.astype(jnp.float32) * (1.0 / SCALE)), at)
    return out.reshape(ncolumns * block, ngroups, block)


def plain(descriptors):
    squares = jnp.sum(descriptors * descriptors, axis=1, keepdims=True)
    unit = (descriptors * lax.rsqrt(squares + 1e-06)).astype(jnp.bfloat16)
    columns = lax.all_gather(unit, "grp", axis=0, tiled=True)
    rows = lax.all_gather(unit, "col", axis=0, tiled=True)
    intersection = jnp.dot(rows, columns.T, preferred_element_type=jnp.float32)
    second = intersection * intersection
    return (second * second).reshape(rows.shape[0], -1, unit.shape[0])


def solution(mesh):
    ngroups, ncolumns = mesh.shape["grp"], mesh.shape["col"]
    fits = ncolumns % (2 * LINE) == 0 and ngroups % 2 == 0
    return jax.shard_map(
        shards if fits else plain,
        mesh=mesh,
        in_specs=(P(AXES, None),),
        out_specs=P("grp", None, "col"),
        check_vma=False,
    )
```

time: 75.8 us -> 69.3 us (0.914)
  Pallas kernels: 24.8 us -> 2.3 us
  waiting for transfers between devices: 15.4 us -> 29.3 us
  matrix products: 0 us -> 5.32 us
  other arithmetic: 4.29 us -> 0.23 us
  local copies, waits for them, and re-layouts: 2.71 us -> 6.32 us
  starting transfers between devices: 28 us -> 25 us
    pallas_call x5 -> x0, Pallas kernels: 22.4 us -> none  [the longest x4 20.1 us: products(): pl.pallas_call(functools.partial(product_kernel, nparts, nblocks, cut, pl...]
    ppermute x28, waiting for transfers between devices: 15.4 us -> 29.3 us  [send(): return lax.ppermute(array, AXES, pairs)]
    dot_general x0 -> x11, matrix products: none -> 5.32 us  [fourth(): lax.dot_general(jnp.concatenate(block, axis=0), cols, (((0,), (1,)), ((),...]
    ppermute x28, starting transfers between devices: 28 us -> 25 us  [send(): return lax.ppermute(array, AXES, pairs)]
    dynamic_update_slice x0 -> x25, local copies, waits for them, and re-layouts: none -> 2.88 us  [the longest x16 2.48 us: columns_of(): full = lax.dynamic_update_slice(full, array[None], start)]
    reshape x0 -> x1, local copies, waits for them, and re-layouts: none -> 2.67 us  [exchange(): return out.reshape(ncolumns * block, ngroups, block)]
    convert_element_type x2 -> x0, other arithmetic: 2.05 us -> none  [back(): return send(panels.astype(jnp.float16), line_swap)]
    unnamed x34 -> x4, local copies, waits for them, and re-layouts: 1.35 us -> 0.01 us
  transfers between devices with their start and end apart: 28 -> 28, of which waited for: 8 -> 11; matrix products, arithmetic and copies ran while one was open for 6% -> 13% of each run, Pallas kernels for 27% -> 0%
where the time goes in v2:
time: 69.3 us; the launch traced here: 69.1 us
  waiting for transfers between devices  29.3 us (42%)
  starting transfers between devices  25 us (36%)
  local copies, waits for them, and re-layouts  6.32 us (9%)
  matrix products  5.32 us (8%)
  Pallas kernels  2.3 us (3%)
    ppermute x28, waiting for transfers between devices, send(): return lax.ppermute(array, AXES, pairs)  29.3 us
    ppermute x28, starting transfers between devices, send(): return lax.ppermute(array, AXES, pairs)  25 us
    dot_general x11, matrix products, fourth(): lax.dot_general(jnp.concatenate(block, axis=0), cols, (((0,), (1,)), ((),...  5.32 us
    reshape x1, local copies, waits for them, and re-layouts, exchange(): return out.reshape(ncolumns * block, ngroups, block)  2.67 us
    dynamic_update_slice x16, local copies, waits for them, and re-layouts, columns_of(): full = lax.dynamic_update_slice(full, array[None], start)  2.48 us
    pallas_call x1, Pallas kernels, normalize(): pl.pallas_call(functools.partial(unit_kernel, cut), out_shape=[jax.ShapeD...  2.3 us
  transfers between devices with their start and end apart: 28, of which 11 were waited for; matrix products, arithmetic and copies ran while one was open for 13% of the time, Pallas kernels for 0%

profile of v2, /device:TPU:0, one launch (start us, length us, event | category | flops | bytes accessed | tf_op | source)
XLA Modules:
  0.0 69.1 jit_solution(16754977895724799308)
XLA Ops:
  0.0 2.3 %normalize.1 = (bf16[992,128]{1,0:T(8,128)(2,1)}, bf16[1008,128]{1,0:T(8,128)(2,1)}) custom-call(f32[2000,128]{1,0:T(8,128)} %bitcast.95), custom_call_target="tpu_custom_call" | custom-call | bytes 1536000 | tf_op jit(solution)/shard_map/normalize/pallas_call | solution.py:28
  2.3 3.1 %collective-permute-start.6 = (bf16[992,128]{1,0:T(8,128)(2,1)}, bf16[992,128]{1,0:T(8,128)(2,1)S(1)}, u32[]{:S(2)}, u32[]{:S(2)}) collective-permute-start(bf16[992,128]{1,0:T(8,128)(2,1)} %get-tuple-element.7), channel_id=1, source_target_pairs={{0,2},{1,3},{2,0},{3,1},{4,6},{5,7},{6,4},{7,5},{8,10},{9,11},{10,... | collective-permute-start | bytes 761864 | tf_op jit(solution)/shard_map/ppermute | solution.py:65
  5.4 1.5 %collective-permute-start.2 = (bf16[992,128]{1,0:T(8,128)(2,1)}, bf16[992,128]{1,0:T(8,128)(2,1)}, u32[]{:S(2)}, u32[]{:S(2)}) collective-permute-start(bf16[992,128]{1,0:T(8,128)(2,1)} %get-tuple-element.7), channel_id=1, source_target_pairs={{0,16},{1,17},{2,18},{3,19},{4,20},{5,21},{6,22},{7,23},{8,24},{9,... | collective-permute-start | bytes 761864 | tf_op jit(solution)/shard_map/ppermute | solution.py:65
  6.9 0.2 collective-permute-start.1
  7.1 0.5 collective-permute-start.4
  7.6 0.3 broadcast.23.clone
  8.1 3.6 %collective-permute-done.6 = bf16[992,128]{1,0:T(8,128)(2,1)S(1)} collective-permute-done((bf16[992,128]{1,0:T(8,128)(2,1)}, bf16[992,128]{1,0:T(8,128)(2,1)S(1)}, u32[]{:S(2)}, u32[]{:S(2)}) %collective-permute-start.6) | collective-permute-done | bytes 253984 | tf_op jit(solution)/shard_map/ppermute | solution.py:65
  11.8 1.7 %collective-permute-start.7 = (bf16[1008,128]{1,0:T(8,128)(2,1)S(1)}, bf16[1008,128]{1,0:T(8,128)(2,1)S(1)}, u32[]{:S(2)}, u32[]{:S(2)}) collective-permute-start(bf16[1008,128]{1,0:T(8,128)(2,1)S(1)} %copy-done), channel_id=1, source_target_pairs={{0,2},{1,3},{2,0},{3,1},{4,6},{5,7},{6,4},{7,5},{8,10},{9,11},{10,... | collective-permute-start | bytes 774152 | tf_op jit(solution)/shard_map/ppermute | solution.py:65
  13.4 0.3 broadcast.23.clone.1
  13.8 1.6 %collective-permute-start.9 = (bf16[1008,128]{1,0:T(8,128)(2,1)S(1)}, bf16[1008,128]{1,0:T(8,128)(2,1)S(1)}, u32[]{:S(2)}, u32[]{:S(2)}) collective-permute-start(bf16[1008,128]{1,0:T(8,128)(2,1)S(1)} %copy-done), channel_id=1, source_target_pairs={{0,1},{1,0},{2,4},{3,5},{4,2},{5,3},{6,7},{7,6},{8,9},{9,8},{10,12... | collective-permute-start | bytes 774152 | tf_op jit(solution)/shard_map/ppermute | solution.py:65
  15.3 1.0 %bitcast_dynamic-update-slice_fusion.22 = bf16[4,2000,128]{2,1,0:T(8,128)(2,1)S(1)} fusion(bf16[4,2000,128]{2,1,0:T(8,128)(2,1)S(1)} %bitcast_dynamic-update-slice_fusion.23, s32[]{:T(128)S(6)} %select_n.191, bf16[992,128]{1,0:T(8,128)(2,1)} %collective-permute-done), kind=kLoop, calls=%fused_computation.75 | loop fusion | bytes 507908 | tf_op jit(solution)/shard_map/dynamic_update_slice | solution.py:126
  16.4 0.6 collective-permute-start.8
  17.0 1.0 %bitcast_dynamic-update-slice_fusion.21 = bf16[4,2000,128]{2,1,0:T(8,128)(2,1)S(1)} fusion(bf16[4,2000,128]{2,1,0:T(8,128)(2,1)S(1)} %bitcast_dynamic-update-slice_fusion.14, s32[]{:T(128)S(6)} %select_n.193, bf16[992,128]{1,0:T(8,128)(2,1)} %collective-permute-done.2), kind=kLoop, calls=%fused_computation.74 | loop fusion | bytes 507908 | tf_op jit(solution)/shard_map/dynamic_update_slice | solution.py:126
  18.0 0.7 %collective-permute-done.3 = bf16[992,128]{1,0:T(8,128)(2,1)S(1)} collective-permute-done((bf16[992,128]{1,0:T(8,128)(2,1)}, bf16[992,128]{1,0:T(8,128)(2,1)S(1)}, u32[]{:S(2)}, u32[]{:S(2)}) %collective-permute-start.3) | collective-permute-done | bytes 253984 | tf_op jit(solution)/shard_map/ppermute | solution.py:65
  18.9 0.8 %collective-permute-done.4 = bf16[1008,128]{1,0:T(8,128)(2,1)S(1)} collective-permute-done((bf16[1008,128]{1,0:T(8,128)(2,1)}, bf16[1008,128]{1,0:T(8,128)(2,1)S(1)}, u32[]{:S(2)}, u32[]{:S(2)}) %collective-permute-start.4) | collective-permute-done | bytes 258080 | tf_op jit(solution)/shard_map/ppermute | solution.py:65
  19.7 0.5 collective-permute-done.20
  20.4 0.4 collective-permute-start.10
  20.9 5.3 %collective-permute-done.8 = bf16[992,128]{1,0:T(8,128)(2,1)S(1)} collective-permute-done((bf16[992,128]{1,0:T(8,128)(2,1)S(1)}, bf16[992,128]{1,0:T(8,128)(2,1)S(1)}, u32[]{:S(2)}, u32[]{:S(2)}) %collective-permute-start.8) | collective-permute-done | bytes 253984 | tf_op jit(solution)/shard_map/ppermute | solution.py:65
  26.2 1.5 %collective-permute-start.14 = (bf16[992,128]{1,0:T(8,128)(2,1)S(1)}, bf16[992,128]{1,0:T(8,128)(2,1)S(1)}, u32[]{:S(2)}, u32[]{:S(2)}) collective-permute-start(bf16[992,128]{1,0:T(8,128)(2,1)S(1)} %collective-permute-done.6), channel_id=1, source_target_pairs={{0,1},{1,0},{2,4},{3,5},{4,2},{5,3},{6,7},{7,6},{8,9},{9,8},{10,12... | collective-permute-start | bytes 761864 | tf_op jit(solution)/shard_map/ppermute | solution.py:65
  27.7 1.7 %collective-permute-start.12 = (bf16[992,128]{1,0:T(8,128)(2,1)S(1)}, bf16[992,128]{1,0:T(8,128)(2,1)S(1)}, u32[]{:S(2)}, u32[]{:S(2)}) collective-permute-start(bf16[992,128]{1,0:T(8,128)(2,1)S(1)} %collective-permute-done.8), channel_id=1, source_target_pairs={{0,2},{1,3},{2,0},{3,1},{4,6},{5,7},{6,4},{7,5},{8,10},{9,11},{10,... | collective-permute-start | bytes 761864 | tf_op jit(solution)/shard_map/ppermute | solution.py:65
  29.4 0.5 fusion.10
  29.9 0.5 fusion.9
  30.5 0.5 fusion.8
  31.0 1.6 %collective-permute-start.22 = (bf16[992,128]{1,0:T(8,128)(2,1)S(1)}, bf16[992,128]{1,0:T(8,128)(2,1)S(1)}, u32[]{:S(2)}, u32[]{:S(2)}) collective-permute-start(bf16[992,128]{1,0:T(8,128)(2,1)S(1)} %collective-permute-done.6), channel_id=1, source_target_pairs={{0,16},{1,17},{2,18},{3,19},{4,20},{5,21},{6,22},{7,23},{8,24},{9,... | collective-permute-start | bytes 761864 | tf_op jit(solution)/shard_map/ppermute | solution.py:65
  32.5 3.7 %collective-permute-start.13 = (bf16[1008,128]{1,0:T(8,128)(2,1)S(1)}, bf16[1008,128]{1,0:T(8,128)(2,1)S(1)}, u32[]{:S(2)}, u32[]{:S(2)}) collective-permute-start(bf16[1008,128]{1,0:T(8,128)(2,1)S(1)} %collective-permute-done.9), channel_id=1, source_target_pairs={{0,2},{1,3},{2,0},{3,1},{4,6},{5,7},{6,4},{7,5},{8,10},{9,11},{10,... | collective-permute-start | bytes 774152 | tf_op jit(solution)/shard_map/ppermute | solution.py:65
  36.2 0.5 fusion.7
  36.7 1.6 %collective-permute-start.15 = (bf16[1008,128]{1,0:T(8,128)(2,1)S(1)}, bf16[1008,128]{1,0:T(8,128)(2,1)S(1)}, u32[]{:S(2)}, u32[]{:S(2)}) collective-permute-start(bf16[1008,128]{1,0:T(8,128)(2,1)S(1)} %collective-permute-done.7), channel_id=1, source_target_pairs={{0,1},{1,0},{2,4},{3,5},{4,2},{5,3},{6,7},{7,6},{8,9},{9,8},{10,12... | collective-permute-start | bytes 774152 | tf_op jit(solution)/shard_map/ppermute | solution.py:65
  38.3 3.0 %collective-permute-done.13 = bf16[1008,128]{1,0:T(8,128)(2,1)S(1)} collective-permute-done((bf16[1008,128]{1,0:T(8,128)(2,1)S(1)}, bf16[1008,128]{1,0:T(8,128)(2,1)S(1)}, u32[]{:S(2)}, u32[]{:S(2)}) %collective-permute-start.13) | collective-permute-done | bytes 258080 | tf_op jit(solution)/shard_map/ppermute | solution.py:65
  41.3 0.5 fusion.6
  41.7 0.2 broadcast_in_dim.79
  42.0 0.6 collective-permute-start.21
  42.6 0.6 collective-permute-done.15
  43.3 0.5 collective-permute-start.24
  43.8 0.5 fusion.5
  44.4 0.5 collective-permute-start.23
  44.9 0.5 fusion.4
  45.7 5.1 %collective-permute-done.24 = bf16[1008,128]{1,0:T(8,128)(2,1)S(1)} collective-permute-done((bf16[1008,128]{1,0:T(8,128)(2,1)S(1)}, bf16[1008,128]{1,0:T(8,128)(2,1)S(1)}, u32[]{:S(2)}, u32[]{:S(2)}) %collective-permute-start.24) | collective-permute-done | bytes 258080 | tf_op jit(solution)/shard_map/ppermute | solution.py:65
  51.0 1.4 %collective-permute-done.25 = bf16[1008,128]{1,0:T(8,128)(2,1)S(1)} collective-permute-done((bf16[1008,128]{1,0:T(8,128)(2,1)S(1)}, bf16[1008,128]{1,0:T(8,128)(2,1)S(1)}, u32[]{:S(2)}, u32[]{:S(2)}) %collective-permute-start.25) | collective-permute-done | bytes 258080 | tf_op jit(solution)/shard_map/ppermute | solution.py:65
  52.4 0.5 fusion.18
  52.9 0.5 fusion.17
  53.5 3.2 %collective-permute-start.26 = (f16[2,128,4,128]{3,1,2,0:T(8,128)(2,1)S(1)}, f16[2,128,4,128]{3,1,2,0:T(8,128)(2,1)S(1)}, u32[]{:S(2)}, u32[]{:S(2)}) collective-permute-start(f16[2,128,4,128]{3,1,2,0:T(8,128)(2,1)S(1)} %pad_maximum_fusion), channel_id=1, source_target_pairs={{0,2},{1,3},{2,0},{3,1},{4,6},{5,7},{6,4},{7,5},{8,10},{9,11},{10,... | collective-permute-start | bytes 786440 | tf_op jit(solution)/shard_map/ppermute | solution.py:65
  56.7 0.5 fusion.3
  57.2 0.5 fusion.19
  57.7 0.1 collective-permute-start.27
  57.8 6.0 %collective-permute-done.26 = f16[2,128,4,128]{3,1,2,0:T(8,128)(2,1)S(1)} collective-permute-done((f16[2,128,4,128]{3,1,2,0:T(8,128)(2,1)S(1)}, f16[2,128,4,128]{3,1,2,0:T(8,128)(2,1)S(1)}, u32[]{:S(2)}, u32[]{:S(2)}) %collective-permute-start.26) | collective-permute-done | bytes 262176 | tf_op jit(solution)/shard_map/ppermute | solution.py:65
  64.0 2.2 %collective-permute-done.27 = f16[1,128,4,128]{3,1,2,0:T(8,128)(2,1)S(1)} collective-permute-done((f16[1,128,4,128]{3,1,2,0:T(8,128)(2,1)S(1)}, f16[1,128,4,128]{3,1,2,0:T(8,128)(2,1)S(1)}, u32[]{:S(2)}, u32[]{:S(2)}) %collective-permute-start.27) | collective-permute-done | bytes 131104 | tf_op jit(solution)/shard_map/ppermute | solution.py:65
  66.2 0.2 copy.2
  66.4 2.7 %copy.3 = f32[1024,4,128]{2,1,0:T(4,128)} copy(f32[1024,4,128]{2,0,1:T(8,128)S(1)} %bitcast.94) | data formatting | bytes 4194304 | tf_op jit(solution)/shard_map/reshape | solution.py:185
  (57 shorter events, 1.5 us)
Async XLA Ops:
  2.3 5.6 %copy-start.1 = (bf16[992,128]{1,0:T(8,128)(2,1)S(1)}, bf16[992,128]{1,0:T(8,128)(2,1)}, u32[]{:S(2)}) copy-start(bf16[992,128]{1,0:T(8,128)(2,1)} %get-tuple-element.7) | copy-start | bytes 761860
  2.3 9.5 %copy-start = (bf16[1008,128]{1,0:T(8,128)(2,1)S(1)}, bf16[1008,128]{1,0:T(8,128)(2,1)}, u32[]{:S(2)}) copy-start(bf16[1008,128]{1,0:T(8,128)(2,1)} %get-tuple-element.8) | copy-start | bytes 774148
  2.3 9.5 %collective-permute-start.6 = (bf16[992,128]{1,0:T(8,128)(2,1)}, bf16[992,128]{1,0:T(8,128)(2,1)S(1)}, u32[]{:S(2)}, u32[]{:S(2)}) collective-permute-start(bf16[992,128]{1,0:T(8,128)(2,1)} %get-tuple-element.7), channel_id=1, source_target_pairs={{0,2},{1,3},{2,0},{3,1},{4,6},{5,7},{6,4},{7,5},{8,10},{9,11},{10,... | collective-permute-start | bytes 761864 | tf_op jit(solution)/shard_map/ppermute | solution.py:65
  5.4 8.4 %collective-permute-start = (bf16[992,128]{1,0:T(8,128)(2,1)}, bf16[992,128]{1,0:T(8,128)(2,1)}, u32[]{:S(2)}, u32[]{:S(2)}) collective-permute-start(bf16[992,128]{1,0:T(8,128)(2,1)} %get-tuple-element.7), channel_id=1, source_target_pairs={{0,8},{1,9},{2,10},{3,11},{4,12},{5,13},{6,14},{7,15},{8,0},{9,1},... | collective-permute-start | bytes 761864 | tf_op jit(solution)/shard_map/ppermute | solution.py:65
  5.4 11.0 %collective-permute-start.2 = (bf16[992,128]{1,0:T(8,128)(2,1)}, bf16[992,128]{1,0:T(8,128)(2,1)}, u32[]{:S(2)}, u32[]{:S(2)}) collective-permute-start(bf16[992,128]{1,0:T(8,128)(2,1)} %get-tuple-element.7), channel_id=1, source_target_pairs={{0,16},{1,17},{2,18},{3,19},{4,20},{5,21},{6,22},{7,23},{8,24},{9,... | collective-permute-start | bytes 761864 | tf_op jit(solution)/shard_map/ppermute | solution.py:65
  6.9 10.1 %collective-permute-start.1 = (bf16[1008,128]{1,0:T(8,128)(2,1)}, bf16[1008,128]{1,0:T(8,128)(2,1)S(1)}, u32[]{:S(2)}, u32[]{:S(2)}) collective-permute-start(bf16[1008,128]{1,0:T(8,128)(2,1)} %get-tuple-element.8), channel_id=1, source_target_pairs={{0,8},{1,9},{2,10},{3,11},{4,12},{5,13},{6,14},{7,15},{8,0},{9,1},... | collective-permute-start | bytes 774152 | tf_op jit(solution)/shard_map/ppermute | solution.py:65
  7.1 12.5 %collective-permute-start.4 = (bf16[1008,128]{1,0:T(8,128)(2,1)}, bf16[1008,128]{1,0:T(8,128)(2,1)S(1)}, u32[]{:S(2)}, u32[]{:S(2)}) collective-permute-start(bf16[1008,128]{1,0:T(8,128)(2,1)} %get-tuple-element.8), channel_id=1, source_target_pairs={{0,16},{1,17},{2,18},{3,19},{4,20},{5,21},{6,22},{7,23},{8,24},{9,... | collective-permute-start | bytes 774152 | tf_op jit(solution)/shard_map/ppermute | solution.py:65
  11.8 8.6 %collective-permute-start.7 = (bf16[1008,128]{1,0:T(8,128)(2,1)S(1)}, bf16[1008,128]{1,0:T(8,128)(2,1)S(1)}, u32[]{:S(2)}, u32[]{:S(2)}) collective-permute-start(bf16[1008,128]{1,0:T(8,128)(2,1)S(1)} %copy-done), channel_id=1, source_target_pairs={{0,2},{1,3},{2,0},{3,1},{4,6},{5,7},{6,4},{7,5},{8,10},{9,11},{10,... | collective-permute-start | bytes 774152 | tf_op jit(solution)/shard_map/ppermute | solution.py:65
  13.8 16.6 %collective-permute-start.9 = (bf16[1008,128]{1,0:T(8,128)(2,1)S(1)}, bf16[1008,128]{1,0:T(8,128)(2,1)S(1)}, u32[]{:S(2)}, u32[]{:S(2)}) collective-permute-start(bf16[1008,128]{1,0:T(8,128)(2,1)S(1)} %copy-done), channel_id=1, source_target_pairs={{0,1},{1,0},{2,4},{3,5},{4,2},{5,3},{6,7},{7,6},{8,9},{9,8},{10,12... | collective-permute-start | bytes 774152 | tf_op jit(solution)/shard_map/ppermute | solution.py:65
  16.4 9.8 %collective-permute-start.8 = (bf16[992,128]{1,0:T(8,128)(2,1)S(1)}, bf16[992,128]{1,0:T(8,128)(2,1)S(1)}, u32[]{:S(2)}, u32[]{:S(2)}) collective-permute-start(bf16[992,128]{1,0:T(8,128)(2,1)S(1)} %copy-done.1), channel_id=1, source_target_pairs={{0,1},{1,0},{2,4},{3,5},{4,2},{5,3},{6,7},{7,6},{8,9},{9,8},{10,12... | collective-permute-start | bytes 761864 | tf_op jit(solution)/shard_map/ppermute | solution.py:65
  17.0 1.7 %collective-permute-start.3 = (bf16[992,128]{1,0:T(8,128)(2,1)}, bf16[992,128]{1,0:T(8,128)(2,1)S(1)}, u32[]{:S(2)}, u32[]{:S(2)}) collective-permute-start(bf16[992,128]{1,0:T(8,128)(2,1)} %collective-permute-done.2), channel_id=1, source_target_pairs={{0,8},{1,9},{2,10},{3,11},{4,12},{5,13},{6,14},{7,15},{8,0},{9,1},... | collective-permute-start | bytes 761864 | tf_op jit(solution)/shard_map/ppermute | solution.py:65
  18.7 1.5 %collective-permute-start.20 = (bf16[992,128]{1,0:T(8,128)(2,1)S(1)}, bf16[992,128]{1,0:T(8,128)(2,1)S(1)}, u32[]{:S(2)}, u32[]{:S(2)}) collective-permute-start(bf16[992,128]{1,0:T(8,128)(2,1)S(1)} %collective-permute-done.6), channel_id=1, source_target_pairs={{0,8},{1,9},{2,10},{3,11},{4,12},{5,13},{6,14},{7,15},{8,0},{9,1},... | collective-permute-start | bytes 761864 | tf_op jit(solution)/shard_map/ppermute | solution.py:65
  19.6 12.9 %collective-permute-start.11 = (bf16[1008,128]{1,0:T(8,128)(2,1)S(1)}, bf16[1008,128]{1,0:T(8,128)(2,1)S(1)}, u32[]{:S(2)}, u32[]{:S(2)}) collective-permute-start(bf16[1008,128]{1,0:T(8,128)(2,1)S(1)} %copy-done), channel_id=1, source_target_pairs={{0,8},{1,9},{2,3},{3,2},{4,5},{5,4},{6,14},{7,15},{8,0},{9,1},{10,... | collective-permute-start | bytes 774152 | tf_op jit(solution)/shard_map/ppermute | solution.py:65
  20.2 7.5 %collective-permute-start.5 = (bf16[1008,128]{1,0:T(8,128)(2,1)S(1)}, bf16[1008,128]{1,0:T(8,128)(2,1)S(1)}, u32[]{:S(2)}, u32[]{:S(2)}) collective-permute-start(bf16[1008,128]{1,0:T(8,128)(2,1)S(1)} %collective-permute-done.4), channel_id=1, source_target_pairs={{0,8},{1,9},{2,10},{3,11},{4,12},{5,13},{6,14},{7,15},{8,0},{9,1},... | collective-permute-start | bytes 774152 | tf_op jit(solution)/shard_map/ppermute | solution.py:65
  20.4 10.5 %collective-permute-start.10 = (bf16[992,128]{1,0:T(8,128)(2,1)S(1)}, bf16[992,128]{1,0:T(8,128)(2,1)S(1)}, u32[]{:S(2)}, u32[]{:S(2)}) collective-permute-start(bf16[992,128]{1,0:T(8,128)(2,1)S(1)} %copy-done.1), channel_id=1, source_target_pairs={{0,8},{1,9},{2,3},{3,2},{4,5},{5,4},{6,14},{7,15},{8,0},{9,1},{10,... | collective-permute-start | bytes 761864 | tf_op jit(solution)/shard_map/ppermute | solution.py:65
  26.2 15.8 %collective-permute-start.14 = (bf16[992,128]{1,0:T(8,128)(2,1)S(1)}, bf16[992,128]{1,0:T(8,128)(2,1)S(1)}, u32[]{:S(2)}, u32[]{:S(2)}) collective-permute-start(bf16[992,128]{1,0:T(8,128)(2,1)S(1)} %collective-permute-done.6), channel_id=1, source_target_pairs={{0,1},{1,0},{2,4},{3,5},{4,2},{5,3},{6,7},{7,6},{8,9},{9,8},{10,12... | collective-permute-start | bytes 761864 | tf_op jit(solution)/shard_map/ppermute | solution.py:65
  27.7 9.0 %collective-permute-start.12 = (bf16[992,128]{1,0:T(8,128)(2,1)S(1)}, bf16[992,128]{1,0:T(8,128)(2,1)S(1)}, u32[]{:S(2)}, u32[]{:S(2)}) collective-permute-start(bf16[992,128]{1,0:T(8,128)(2,1)S(1)} %collective-permute-done.8), channel_id=1, source_target_pairs={{0,2},{1,3},{2,0},{3,1},{4,6},{5,7},{6,4},{7,5},{8,10},{9,11},{10,... | collective-permute-start | bytes 761864 | tf_op jit(solution)/shard_map/ppermute | solution.py:65
  30.4 14.0 %collective-permute-start.16 = (bf16[992,128]{1,0:T(8,128)(2,1)S(1)}, bf16[992,128]{1,0:T(8,128)(2,1)S(1)}, u32[]{:S(2)}, u32[]{:S(2)}) collective-permute-start(bf16[992,128]{1,0:T(8,128)(2,1)S(1)} %collective-permute-done.8), channel_id=1, source_target_pairs={{0,8},{1,9},{2,3},{3,2},{4,5},{5,4},{6,14},{7,15},{8,0},{9,1},{10,... | collective-permute-start | bytes 761864 | tf_op jit(solution)/shard_map/ppermute | solution.py:65
  31.0 13.5 %collective-permute-start.22 = (bf16[992,128]{1,0:T(8,128)(2,1)S(1)}, bf16[992,128]{1,0:T(8,128)(2,1)S(1)}, u32[]{:S(2)}, u32[]{:S(2)}) collective-permute-start(bf16[992,128]{1,0:T(8,128)(2,1)S(1)} %collective-permute-done.6), channel_id=1, source_target_pairs={{0,16},{1,17},{2,18},{3,19},{4,20},{5,21},{6,22},{7,23},{8,24},{9,... | collective-permute-start | bytes 761864 | tf_op jit(solution)/shard_map/ppermute | solution.py:65
  32.5 8.7 %collective-permute-start.13 = (bf16[1008,128]{1,0:T(8,128)(2,1)S(1)}, bf16[1008,128]{1,0:T(8,128)(2,1)S(1)}, u32[]{:S(2)}, u32[]{:S(2)}) collective-permute-start(bf16[1008,128]{1,0:T(8,128)(2,1)S(1)} %collective-permute-done.9), channel_id=1, source_target_pairs={{0,2},{1,3},{2,0},{3,1},{4,6},{5,7},{6,4},{7,5},{8,10},{9,11},{10,... | collective-permute-start | bytes 774152 | tf_op jit(solution)/shard_map/ppermute | solution.py:65
  36.7 6.6 %collective-permute-start.15 = (bf16[1008,128]{1,0:T(8,128)(2,1)S(1)}, bf16[1008,128]{1,0:T(8,128)(2,1)S(1)}, u32[]{:S(2)}, u32[]{:S(2)}) collective-permute-start(bf16[1008,128]{1,0:T(8,128)(2,1)S(1)} %collective-permute-done.7), channel_id=1, source_target_pairs={{0,1},{1,0},{2,4},{3,5},{4,2},{5,3},{6,7},{7,6},{8,9},{9,8},{10,12... | collective-permute-start | bytes 774152 | tf_op jit(solution)/shard_map/ppermute | solution.py:65
  41.3 3.7 %collective-permute-start.17 = (bf16[1008,128]{1,0:T(8,128)(2,1)S(1)}, bf16[1008,128]{1,0:T(8,128)(2,1)S(1)}, u32[]{:S(2)}, u32[]{:S(2)}) collective-permute-start(bf16[1008,128]{1,0:T(8,128)(2,1)S(1)} %collective-permute-done.9), channel_id=1, source_target_pairs={{0,8},{1,9},{2,3},{3,2},{4,5},{5,4},{6,14},{7,15},{8,0},{9,1},{10,... | collective-permute-start | bytes 774152 | tf_op jit(solution)/shard_map/ppermute | solution.py:65
  42.0 3.6 %collective-permute-start.21 = (bf16[1008,128]{1,0:T(8,128)(2,1)S(1)}, bf16[1008,128]{1,0:T(8,128)(2,1)S(1)}, u32[]{:S(2)}, u32[]{:S(2)}) collective-permute-start(bf16[1008,128]{1,0:T(8,128)(2,1)S(1)} %collective-permute-done.7), channel_id=1, source_target_pairs={{0,8},{1,9},{2,10},{3,11},{4,12},{5,13},{6,14},{7,15},{8,0},{9,1},... | collective-permute-start | bytes 774152 | tf_op jit(solution)/shard_map/ppermute | solution.py:65
  43.3 7.6 %collective-permute-start.24 = (bf16[1008,128]{1,0:T(8,128)(2,1)S(1)}, bf16[1008,128]{1,0:T(8,128)(2,1)S(1)}, u32[]{:S(2)}, u32[]{:S(2)}) collective-permute-start(bf16[1008,128]{1,0:T(8,128)(2,1)S(1)} %collective-permute-done.7), channel_id=1, source_target_pairs={{0,16},{1,17},{2,18},{3,19},{4,20},{5,21},{6,22},{7,23},{8,24},{9,... | collective-permute-start | bytes 774152 | tf_op jit(solution)/shard_map/ppermute | solution.py:65
  44.4 12.3 %collective-permute-start.18 = (bf16[992,128]{1,0:T(8,128)(2,1)S(1)}, bf16[992,128]{1,0:T(8,128)(2,1)S(1)}, u32[]{:S(2)}, u32[]{:S(2)}) collective-permute-start(bf16[992,128]{1,0:T(8,128)(2,1)S(1)} %collective-permute-done.14), channel_id=1, source_target_pairs={{0,8},{1,9},{2,3},{3,2},{4,5},{5,4},{6,14},{7,15},{8,0},{9,1},{10,... | collective-permute-start | bytes 761864 | tf_op jit(solution)/shard_map/ppermute | solution.py:65
  44.4 6.4 %collective-permute-start.23 = (bf16[992,128]{1,0:T(8,128)(2,1)S(1)}, bf16[992,128]{1,0:T(8,128)(2,1)S(1)}, u32[]{:S(2)}, u32[]{:S(2)}) collective-permute-start(bf16[992,128]{1,0:T(8,128)(2,1)S(1)} %collective-permute-done.22), channel_id=1, source_target_pairs={{0,8},{1,9},{2,10},{3,11},{4,12},{5,13},{6,14},{7,15},{8,0},{9,1},... | collective-permute-start | bytes 761864 | tf_op jit(solution)/shard_map/ppermute | solution.py:65
  45.5 11.2 %collective-permute-start.19 = (bf16[1008,128]{1,0:T(8,128)(2,1)S(1)}, bf16[1008,128]{1,0:T(8,128)(2,1)S(1)}, u32[]{:S(2)}, u32[]{:S(2)}) collective-permute-start(bf16[1008,128]{1,0:T(8,128)(2,1)S(1)} %collective-permute-done.13), channel_id=1, source_target_pairs={{0,8},{1,9},{2,4},{3,5},{4,2},{5,3},{6,14},{7,15},{8,0},{9,1},{10,... | collective-permute-start | bytes 774152 | tf_op jit(solution)/shard_map/ppermute | solution.py:65
  50.8 1.5 %collective-permute-start.25 = (bf16[1008,128]{1,0:T(8,128)(2,1)S(1)}, bf16[1008,128]{1,0:T(8,128)(2,1)S(1)}, u32[]{:S(2)}, u32[]{:S(2)}) collective-permute-start(bf16[1008,128]{1,0:T(8,128)(2,1)S(1)} %collective-permute-done.24), channel_id=1, source_target_pairs={{0,8},{1,9},{2,10},{3,11},{4,12},{5,13},{6,14},{7,15},{8,0},{9,1},... | collective-permute-start | bytes 774152 | tf_op jit(solution)/shard_map/ppermute | solution.py:65
  53.5 10.4 %collective-permute-start.26 = (f16[2,128,4,128]{3,1,2,0:T(8,128)(2,1)S(1)}, f16[2,128,4,128]{3,1,2,0:T(8,128)(2,1)S(1)}, u32[]{:S(2)}, u32[]{:S(2)}) collective-permute-start(f16[2,128,4,128]{3,1,2,0:T(8,128)(2,1)S(1)} %pad_maximum_fusion), channel_id=1, source_target_pairs={{0,2},{1,3},{2,0},{3,1},{4,6},{5,7},{6,4},{7,5},{8,10},{9,11},{10,... | collective-permute-start | bytes 786440 | tf_op jit(solution)/shard_map/ppermute | solution.py:65
  57.7 8.4 %collective-permute-start.27 = (f16[1,128,4,128]{3,1,2,0:T(8,128)(2,1)S(1)}, f16[1,128,4,128]{3,1,2,0:T(8,128)(2,1)S(1)}, u32[]{:S(2)}, u32[]{:S(2)}) collective-permute-start(f16[1,128,4,128]{3,1,2,0:T(8,128)(2,1)S(1)} %fusion.19), channel_id=1, source_target_pairs={{0,2},{1,3},{2,0},{3,1},{4,6},{5,7},{6,4},{7,5},{8,10},{9,11},{10,... | collective-permute-start | bytes 393224 | tf_op jit(solution)/shard_map/ppermute | solution.py:65

commit v3 on v2

--- a/solution.py
+++ b/solution.py
@@ -34,6 +34,7 @@
         in_specs=[VMEM],
         out_specs=[VMEM, VMEM],
         cost_estimate=pl.CostEstimate(flops=0, bytes_accessed=6 * data.size, transcendentals=0),
+        compiler_params=pltpu.CompilerParams(vmem_limit_bytes=8 * data.size),
         name="normalize",
     )(data)
 
@@ -48,10 +49,32 @@
     block = descriptors.shape[0]
     inner = ncolumns // LINE
     offsets = range(1, inner)
+    others = range(2, ngroups, 2)
+    halves = (0, 1)
     grp = lax.axis_index("grp")
     col = lax.axis_index("col")
     z, x = col // inner, col % inner
     middle = jnp.logical_or(z == 1, z == 2)
+
+    def slot(dz, k):
+        return (z ^ dz) * inner + (x + k) % inner
+
+    def where(for_middle, for_end):
+        return jnp.where(middle, slot(*for_middle), slot(*for_end))
+
+    indices = {("own", j): (grp + j) % ngroups for j in range(0, ngroups, 2)}
+    indices.update({("swapped", j): ((grp ^ 1) + j) % ngroups for j in range(0, ngroups, 2)})
+    indices.update({"unit": slot(0, 0), "pair": slot(1, 0), "head": where((3, 0), (0, 1))})
+    indices.update({"head_pair": where((1, 1), (2, 0)), "relay": where((2, 0), (1, inner - 1))})
+    indices.update({("across", k): where((0, k), (0, k + 1)) for k in range(1, inner - 1)})
+    indices.update({("across_pair", k): where((1, k), (1, k - 1)) for k in range(2, inner)})
+    indices["back", 0] = where((0, inner - 1), (3, 0))
+    indices.update({("back", k): where((3, k), (2, k)) for k in offsets})
+    indices.update({("far", k): where((2, k), (3, k)) for k in offsets})
+    names = list(indices)
+    held = lax.optimization_barrier((descriptors, middle) + tuple(indices[n] for n in names))
+    descriptors, middle = held[:2]
+    at = dict(zip(names, held[2:]))
 
     def mid(zz):
         return zz in (1, 2)
@@ -86,8 +109,6 @@
     data = descriptors.T
     cut = data.shape[0] // 32 * 16
     unit = normalize(data, cut)
-    others = range(2, ngroups, 2)
-    halves = (0, 1)
     head, pair = [None, None], [None, None]
     across = [[None, None] for _ in offsets]
     own = {0: unit}
@@ -121,16 +142,11 @@
             for h in halves:
                 part = parts[j][h]
                 swapped = send(part, core_swap)
-                for array, at in ((part, grp + j), (swapped, (grp ^ 1) + j)):
-                    start = (at % ngroups, h * cut, 0)
-                    full = lax.dynamic_update_slice(full, array[None], start)
+                for array, index in ((part, at["own", j]), (swapped, at["swapped", j])):
+                    full = lax.dynamic_update_slice(
+                        full, array[None], (index, h * cut, 0), allow_negative_indices=False
+                    )
         return full
-
-    def slot(dz, k):
-        return (z ^ dz) * inner + (x + k) % inner
-
-    def where(for_middle, for_end):
-        return jnp.where(middle, slot(*for_middle), slot(*for_end))
 
     def fourth(block, cols):
         intersection = lax.dot_general(
@@ -142,20 +158,22 @@
         second = intersection * intersection
         return second * second
 
-    def product(block, cols):
-        return lax.optimization_barrier(fourth(block, cols))
-
-    def put(out, value, at):
-        return lax.dynamic_update_index_in_dim(out, value, at, 0)
+    def product(block):
+        return lax.optimization_barrier(fourth(block, columns))
+
+    def put(out, value, index):
+        return lax.dynamic_update_index_in_dim(
+            out, value, index, 0, allow_negative_indices=False
+        )
 
     columns = columns_of(own)
-    early = [(unit, slot(0, 0)), (pair, slot(1, 0)), (head, where((3, 0), (0, 1)))]
-    for k in offsets:
-        ends = (0, k + 1) if k + 1 < inner else (3, 0)
-        early.append((across[k - 1], where((0, k), ends)))
     out = jnp.zeros((ncolumns, block, ngroups, block), jnp.float32)
-    for b, at in early:
-        out = put(out, product(b, columns), at)
+    out = put(out, product(unit), at["unit"])
+    out = put(out, product(pair), at["pair"])
+    out = put(out, product(head), at["head"])
+    for k in range(1, inner - 1):
+        out = put(out, product(across[k - 1]), at["across", k])
+    mine = [product(across[-1])]
     end_columns = columns_of(end)
     far_across = []
     for k in offsets:
@@ -169,19 +187,17 @@
 
     returned = back([relay] + centre_across)
     returned_far = back(far_across)
-    late = [(head_pair, where((1, 1), (2, 0))), (relay, where((2, 0), (1, inner - 1)))]
+    out = put(out, product(head_pair), at["head_pair"])
+    out = put(out, product(relay), at["relay"])
     for k in range(2, inner):
-        late.append((across_pair[k - 2], where((1, k), (1, k - 1))))
-    late += [(b, where((3, k), (2, k))) for k, b in zip(offsets, centre_across)]
-    for b, at in late:
-        out = put(out, product(b, columns), at)
-    for k, b in zip(offsets, far_across):
-        out = put(out, product(b, columns), where((2, k), (3, k)))
-    slots = [slot(3, 0)] + [slot(2, k) for k in offsets] + [slot(3, k) for k in offsets]
-    panels = [returned[i] for i in range(inner)] + [returned_far[k - 1] for k in offsets]
-    for at, panel in zip(slots, panels):
-        old = lax.dynamic_index_in_dim(out, at, 0, keepdims=False)
-        out = put(out, jnp.where(middle, old, panel.astype(jnp.float32) * (1.0 / SCALE)), at)
+        out = put(out, product(across_pair[k - 2]), at["across_pair", k])
+    mine += [product(b) for b in centre_across]
+    mine += [product(b) for b in far_across]
+    slots = [at["back", k] for k in range(inner)] + [at["far", k] for k in offsets]
+    panels = [returned[k] for k in range(inner)] + [returned_far[k - 1] for k in offsets]
+    for index, panel, value in zip(slots, panels, mine):
+        theirs = panel.astype(jnp.float32) * (1.0 / SCALE)
+        out = put(out, jnp.where(middle, value, theirs), index)
     return out.reshape(ncolumns * block, ngroups, block)
 
 

time: 69.3 us -> 86.9 us (1.25)
  starting transfers between devices: 25 us -> 42.3 us
  waiting for transfers between devices: 29.3 us -> 32.7 us
  Pallas kernels: 2.3 us -> 0.33 us
    ppermute x28, starting transfers between devices: 25 us -> 42.3 us  [send(): return lax.ppermute(array, AXES, pairs)]
    ppermute x28, waiting for transfers between devices: 29.3 us -> 32.7 us  [send(): return lax.ppermute(array, AXES, pairs)]
    reshape x1 -> x0, local copies, waits for them, and re-layouts: 2.67 us -> none  [exchange(): return out.reshape(ncolumns * block, ngroups, block)]
    unnamed x4, local copies, waits for them, and re-layouts: 0.01 us -> 2.53 us
    pallas_call x1, Pallas kernels: 2.3 us -> 0.33 us  [normalize(): pl.pallas_call(functools.partial(unit_kernel, cut), out_shape=[jax.ShapeD...]
    dynamic_update_slice x25 -> x24, local copies, waits for them, and re-layouts: 2.88 us -> 2.12 us  [the longest x8 1.53 us: put(): lax.dynamic_update_index_in_dim(out, value, index, 0, allow_negative_indi...]
  transfers between devices with their start and end apart: 28 -> 28, of which waited for: 11 -> 10; matrix products, arithmetic and copies ran while one was open for 13% -> 8% of each run, Pallas kernels for 0% -> 0%
where the time goes in v3:
time: 86.9 us; the launch traced here: 86.7 us
  starting transfers between devices  42.3 us (49%)
  waiting for transfers between devices  32.7 us (38%)
  local copies, waits for them, and re-layouts  5.46 us (6%)
  matrix products  5.3 us (6%)
    ppermute x28, starting transfers between devices, send(): return lax.ppermute(array, AXES, pairs)  42.3 us
    ppermute x28, waiting for transfers between devices, send(): return lax.ppermute(array, AXES, pairs)  32.7 us
    dot_general x11, matrix products, fourth(): lax.dot_general(jnp.concatenate(block, axis=0), cols, (((0,), (1,)), ((),...  5.3 us
    unnamed x4, local copies, waits for them, and re-layouts  2.53 us
  transfers between devices with their start and end apart: 28, of which 10 were waited for; matrix products, arithmetic and copies ran while one was open for 8% of the time, Pallas kernels for 0%

profile of v3, /device:TPU:0, one launch (start us, length us, event | category | flops | bytes accessed | tf_op | source)
XLA Modules:
  0.0 86.7 jit_solution(671638689048304965)
XLA Ops:
  0.0 1.2 %copy-done = f32[128,2000]{0,1:T(8,128)S(1)} copy-done((f32[128,2000]{0,1:T(8,128)S(1)}, f32[128,2000]{0,1:T(8,128)}, u32[]{:S(2)}) %copy-start) | copy-done | bytes 1024024
  1.2 0.3 normalize.1
  1.6 3.1 %collective-permute-start.6 = (bf16[992,128]{1,0:T(8,128)(2,1)S(1)}, bf16[992,128]{1,0:T(8,128)(2,1)S(1)}, u32[]{:S(2)}, u32[]{:S(2)}) collective-permute-start(bf16[992,128]{1,0:T(8,128)(2,1)S(1)} %get-tuple-element.22), channel_id=1, source_target_pairs={{0,2},{1,3},{2,0},{3,1},{4,6},{5,7},{6,4},{7,5},{8,10},{9,11},{10,... | collective-permute-start | bytes 761864 | tf_op jit(solution)/shard_map/ppermute | solution.py:88
  4.7 1.9 %collective-permute-start.9 = (bf16[1008,128]{1,0:T(8,128)(2,1)S(1)}, bf16[1008,128]{1,0:T(8,128)(2,1)S(1)}, u32[]{:S(2)}, u32[]{:S(2)}) collective-permute-start(bf16[1008,128]{1,0:T(8,128)(2,1)S(1)} %get-tuple-element.23), channel_id=1, source_target_pairs={{0,1},{1,0},{2,4},{3,5},{4,2},{5,3},{6,7},{7,6},{8,9},{9,8},{10,12... | collective-permute-start | bytes 774152 | tf_op jit(solution)/shard_map/ppermute | solution.py:88
  6.6 0.5 collective-permute-start.1
  7.1 0.3 broadcast.21.clone
  7.4 4.2 %collective-permute-done.6 = bf16[992,128]{1,0:T(8,128)(2,1)S(1)} collective-permute-done((bf16[992,128]{1,0:T(8,128)(2,1)S(1)}, bf16[992,128]{1,0:T(8,128)(2,1)S(1)}, u32[]{:S(2)}, u32[]{:S(2)}) %collective-permute-start.6) | collective-permute-done | bytes 253984 | tf_op jit(solution)/shard_map/ppermute | solution.py:88
  11.7 2.0 %collective-permute-start.2 = (bf16[992,128]{1,0:T(8,128)(2,1)S(1)}, bf16[992,128]{1,0:T(8,128)(2,1)S(1)}, u32[]{:S(2)}, u32[]{:S(2)}) collective-permute-start(bf16[992,128]{1,0:T(8,128)(2,1)S(1)} %get-tuple-element.22), channel_id=1, source_target_pairs={{0,16},{1,17},{2,18},{3,19},{4,20},{5,21},{6,22},{7,23},{8,24},{9,... | collective-permute-start | bytes 761864 | tf_op jit(solution)/shard_map/ppermute | solution.py:88
  13.6 0.3 broadcast.21.clone.1
  14.2 6.5 %collective-permute-done.2 = bf16[992,128]{1,0:T(8,128)(2,1)S(1)} collective-permute-done((bf16[992,128]{1,0:T(8,128)(2,1)S(1)}, bf16[992,128]{1,0:T(8,128)(2,1)S(1)}, u32[]{:S(2)}, u32[]{:S(2)}) %collective-permute-start.2) | collective-permute-done | bytes 253984 | tf_op jit(solution)/shard_map/ppermute | solution.py:88
  20.7 1.6 %collective-permute-start.8 = (bf16[992,128]{1,0:T(8,128)(2,1)S(1)}, bf16[992,128]{1,0:T(8,128)(2,1)S(1)}, u32[]{:S(2)}, u32[]{:S(2)}) collective-permute-start(bf16[992,128]{1,0:T(8,128)(2,1)S(1)} %get-tuple-element.22), channel_id=1, source_target_pairs={{0,1},{1,0},{2,4},{3,5},{4,2},{5,3},{6,7},{7,6},{8,9},{9,8},{10,12... | collective-permute-start | bytes 761864 | tf_op jit(solution)/shard_map/ppermute | solution.py:88
  22.3 1.4 %collective-permute-done.3 = bf16[992,128]{1,0:T(8,128)(2,1)S(1)} collective-permute-done((bf16[992,128]{1,0:T(8,128)(2,1)S(1)}, bf16[992,128]{1,0:T(8,128)(2,1)S(1)}, u32[]{:S(2)}, u32[]{:S(2)}) %collective-permute-start.3) | collective-permute-done | bytes 253984 | tf_op jit(solution)/shard_map/ppermute | solution.py:88
  23.9 0.4 collective-permute-start.15
  24.4 0.9 collective-permute-done.16
  25.5 0.4 collective-permute-start.14
  26.0 1.0 %collective-permute-done.8 = bf16[992,128]{1,0:T(8,128)(2,1)S(1)} collective-permute-done((bf16[992,128]{1,0:T(8,128)(2,1)S(1)}, bf16[992,128]{1,0:T(8,128)(2,1)S(1)}, u32[]{:S(2)}, u32[]{:S(2)}) %collective-permute-start.8) | collective-permute-done | bytes 253984 | tf_op jit(solution)/shard_map/ppermute | solution.py:88
  26.9 1.6 %collective-permute-start.18 = (bf16[992,128]{1,0:T(8,128)(2,1)S(1)}, bf16[992,128]{1,0:T(8,128)(2,1)S(1)}, u32[]{:S(2)}, u32[]{:S(2)}) collective-permute-start(bf16[992,128]{1,0:T(8,128)(2,1)S(1)} %collective-permute-done.6), channel_id=1, source_target_pairs={{0,16},{1,17},{2,18},{3,19},{4,20},{5,21},{6,22},{7,23},{8,24},{9,... | collective-permute-start | bytes 761864 | tf_op jit(solution)/shard_map/ppermute | solution.py:88
  28.6 0.5 collective-permute-start.23
  29.1 0.5 fusion.10
  29.6 0.5 fusion.8
  30.1 0.5 fusion.9
  30.6 1.6 %collective-permute-start.12 = (bf16[992,128]{1,0:T(8,128)(2,1)S(1)}, bf16[992,128]{1,0:T(8,128)(2,1)S(1)}, u32[]{:S(2)}, u32[]{:S(2)}) collective-permute-start(bf16[992,128]{1,0:T(8,128)(2,1)S(1)} %collective-permute-done.6), channel_id=1, source_target_pairs={{0,1},{1,0},{2,4},{3,5},{4,2},{5,3},{6,7},{7,6},{8,9},{9,8},{10,12... | collective-permute-start | bytes 761864 | tf_op jit(solution)/shard_map/ppermute | solution.py:88
  32.2 18.4 %collective-permute-start.10 = (bf16[992,128]{1,0:T(8,128)(2,1)S(1)}, bf16[992,128]{1,0:T(8,128)(2,1)S(1)}, u32[]{:S(2)}, u32[]{:S(2)}) collective-permute-start(bf16[992,128]{1,0:T(8,128)(2,1)S(1)} %collective-permute-done.8), channel_id=1, source_target_pairs={{0,2},{1,3},{2,0},{3,1},{4,6},{5,7},{6,4},{7,5},{8,10},{9,11},{10,... | collective-permute-start | bytes 761864 | tf_op jit(solution)/shard_map/ppermute | solution.py:88
  50.6 0.5 fusion.2
  51.2 1.6 %collective-permute-start.13 = (bf16[1008,128]{1,0:T(8,128)(2,1)S(1)}, bf16[1008,128]{1,0:T(8,128)(2,1)S(1)}, u32[]{:S(2)}, u32[]{:S(2)}) collective-permute-start(bf16[1008,128]{1,0:T(8,128)(2,1)S(1)} %collective-permute-done.7), channel_id=1, source_target_pairs={{0,1},{1,0},{2,4},{3,5},{4,2},{5,3},{6,7},{7,6},{8,9},{9,8},{10,12... | collective-permute-start | bytes 774152 | tf_op jit(solution)/shard_map/ppermute | solution.py:88
  52.7 0.5 fusion.5
  53.2 1.6 %collective-permute-start.20 = (bf16[1008,128]{1,0:T(8,128)(2,1)S(1)}, bf16[1008,128]{1,0:T(8,128)(2,1)S(1)}, u32[]{:S(2)}, u32[]{:S(2)}) collective-permute-start(bf16[1008,128]{1,0:T(8,128)(2,1)S(1)} %collective-permute-done.7), channel_id=1, source_target_pairs={{0,16},{1,17},{2,18},{3,19},{4,20},{5,21},{6,22},{7,23},{8,24},{9,... | collective-permute-start | bytes 774152 | tf_op jit(solution)/shard_map/ppermute | solution.py:88
  54.8 5.0 %collective-permute-done.13 = bf16[1008,128]{1,0:T(8,128)(2,1)S(1)} collective-permute-done((bf16[1008,128]{1,0:T(8,128)(2,1)S(1)}, bf16[1008,128]{1,0:T(8,128)(2,1)S(1)}, u32[]{:S(2)}, u32[]{:S(2)}) %collective-permute-start.13) | collective-permute-done | bytes 258080 | tf_op jit(solution)/shard_map/ppermute | solution.py:88
  59.8 0.5 fusion.6
  60.3 0.3 broadcast_in_dim.76
  61.1 0.5 collective-permute-start.19
  61.5 5.9 %collective-permute-done.11 = bf16[1008,128]{1,0:T(8,128)(2,1)S(1)} collective-permute-done((bf16[1008,128]{1,0:T(8,128)(2,1)S(1)}, bf16[1008,128]{1,0:T(8,128)(2,1)S(1)}, u32[]{:S(2)}, u32[]{:S(2)}) %collective-permute-start.11) | collective-permute-done | bytes 258080 | tf_op jit(solution)/shard_map/ppermute | solution.py:88
  67.5 0.5 fusion.7
  68.0 0.2 copy_dynamic-update-slice_fusion.5
  68.2 0.2 copy_dynamic-update-slice_fusion.4
  68.6 0.5 collective-permute-start.21
  69.4 0.9 collective-permute-done.21
  70.3 0.5 fusion.19
  70.8 5.4 %collective-permute-start.27 = (f16[1,128,4,128]{3,1,2,0:T(8,128)(2,1)S(1)}, f16[1,128,4,128]{3,1,2,0:T(8,128)(2,1)S(1)}, u32[]{:S(2)}, u32[]{:S(2)}) collective-permute-start(f16[1,128,4,128]{3,1,2,0:T(8,128)(2,1)S(1)} %fusion.19), channel_id=1, source_target_pairs={{0,2},{1,3},{2,0},{3,1},{4,6},{5,7},{6,4},{7,5},{8,10},{9,11},{10,... | collective-permute-start | bytes 393224 | tf_op jit(solution)/shard_map/ppermute | solution.py:88
  76.2 0.5 fusion.17
  76.7 0.5 fusion.18
  77.3 0.5 fusion.1
  77.8 2.6 %collective-permute-done.27 = f16[1,128,4,128]{3,1,2,0:T(8,128)(2,1)S(1)} collective-permute-done((f16[1,128,4,128]{3,1,2,0:T(8,128)(2,1)S(1)}, f16[1,128,4,128]{3,1,2,0:T(8,128)(2,1)S(1)}, u32[]{:S(2)}, u32[]{:S(2)}) %collective-permute-start.27) | collective-permute-done | bytes 131104 | tf_op jit(solution)/shard_map/ppermute | solution.py:88
  80.5 4.2 %collective-permute-done.24 = f16[2,128,4,128]{3,1,2,0:T(8,128)(2,1)S(1)} collective-permute-done((f16[2,128,4,128]{3,1,2,0:T(8,128)(2,1)S(1)}, f16[2,128,4,128]{3,1,2,0:T(8,128)(2,1)S(1)}, u32[]{:S(2)}, u32[]{:S(2)}) %collective-permute-start.24) | collective-permute-done | bytes 262176 | tf_op jit(solution)/shard_map/ppermute | solution.py:88
  84.8 0.2 copy_dynamic-update-slice_fusion.2
  85.0 0.2 copy_dynamic-update-slice_fusion.1
  85.2 0.2 copy_dynamic-update-slice_fusion
  85.4 1.3 %copy-done.1 = f32[8,128,4,128]{3,2,1,0:T(4,128)} copy-done((f32[8,128,4,128]{3,2,1,0:T(4,128)}, f32[8,128,4,128]{3,2,1,0:T(4,128)S(1)}, u32[]{:S(2)}) %copy-start.1) | copy-done | bytes 2097176
  (54 shorter events, 2.2 us)
Async XLA Ops:
  0.0 1.2 %copy-start = (f32[128,2000]{0,1:T(8,128)S(1)}, f32[128,2000]{0,1:T(8,128)}, u32[]{:S(2)}) copy-start(f32[128,2000]{0,1:T(8,128)} %param.1) | copy-start | bytes 3072004
  1.6 10.1 %collective-permute-start.6 = (bf16[992,128]{1,0:T(8,128)(2,1)S(1)}, bf16[992,128]{1,0:T(8,128)(2,1)S(1)}, u32[]{:S(2)}, u32[]{:S(2)}) collective-permute-start(bf16[992,128]{1,0:T(8,128)(2,1)S(1)} %get-tuple-element.22), channel_id=1, source_target_pairs={{0,2},{1,3},{2,0},{3,1},{4,6},{5,7},{6,4},{7,5},{8,10},{9,11},{10,... | collective-permute-start | bytes 761864 | tf_op jit(solution)/shard_map/ppermute | solution.py:88
  4.7 20.8 %collective-permute-start.7 = (bf16[1008,128]{1,0:T(8,128)(2,1)S(1)}, bf16[1008,128]{1,0:T(8,128)(2,1)S(1)}, u32[]{:S(2)}, u32[]{:S(2)}) collective-permute-start(bf16[1008,128]{1,0:T(8,128)(2,1)S(1)} %get-tuple-element.23), channel_id=1, source_target_pairs={{0,2},{1,3},{2,0},{3,1},{4,6},{5,7},{6,4},{7,5},{8,10},{9,11},{10,... | collective-permute-start | bytes 774152 | tf_op jit(solution)/shard_map/ppermute | solution.py:88
  4.7 23.8 %collective-permute-start.9 = (bf16[1008,128]{1,0:T(8,128)(2,1)S(1)}, bf16[1008,128]{1,0:T(8,128)(2,1)S(1)}, u32[]{:S(2)}, u32[]{:S(2)}) collective-permute-start(bf16[1008,128]{1,0:T(8,128)(2,1)S(1)} %get-tuple-element.23), channel_id=1, source_target_pairs={{0,1},{1,0},{2,4},{3,5},{4,2},{5,3},{6,7},{7,6},{8,9},{9,8},{10,12... | collective-permute-start | bytes 774152 | tf_op jit(solution)/shard_map/ppermute | solution.py:88
  6.6 7.3 %collective-permute-start = (bf16[992,128]{1,0:T(8,128)(2,1)S(1)}, bf16[992,128]{1,0:T(8,128)(2,1)S(1)}, u32[]{:S(2)}, u32[]{:S(2)}) collective-permute-start(bf16[992,128]{1,0:T(8,128)(2,1)S(1)} %get-tuple-element.22), channel_id=1, source_target_pairs={{0,8},{1,9},{2,10},{3,11},{4,12},{5,13},{6,14},{7,15},{8,0},{9,1},... | collective-permute-start | bytes 761864 | tf_op jit(solution)/shard_map/ppermute | solution.py:88
  6.6 15.6 %collective-permute-start.1 = (bf16[1008,128]{1,0:T(8,128)(2,1)S(1)}, bf16[1008,128]{1,0:T(8,128)(2,1)S(1)}, u32[]{:S(2)}, u32[]{:S(2)}) collective-permute-start(bf16[1008,128]{1,0:T(8,128)(2,1)S(1)} %get-tuple-element.23), channel_id=1, source_target_pairs={{0,8},{1,9},{2,10},{3,11},{4,12},{5,13},{6,14},{7,15},{8,0},{9,1},... | collective-permute-start | bytes 774152 | tf_op jit(solution)/shard_map/ppermute | solution.py:88
  11.7 9.0 %collective-permute-start.2 = (bf16[992,128]{1,0:T(8,128)(2,1)S(1)}, bf16[992,128]{1,0:T(8,128)(2,1)S(1)}, u32[]{:S(2)}, u32[]{:S(2)}) collective-permute-start(bf16[992,128]{1,0:T(8,128)(2,1)S(1)} %get-tuple-element.22), channel_id=1, source_target_pairs={{0,16},{1,17},{2,18},{3,19},{4,20},{5,21},{6,22},{7,23},{8,24},{9,... | collective-permute-start | bytes 761864 | tf_op jit(solution)/shard_map/ppermute | solution.py:88
  13.9 10.0 %collective-permute-start.4 = (bf16[1008,128]{1,0:T(8,128)(2,1)S(1)}, bf16[1008,128]{1,0:T(8,128)(2,1)S(1)}, u32[]{:S(2)}, u32[]{:S(2)}) collective-permute-start(bf16[1008,128]{1,0:T(8,128)(2,1)S(1)} %get-tuple-element.23), channel_id=1, source_target_pairs={{0,16},{1,17},{2,18},{3,19},{4,20},{5,21},{6,22},{7,23},{8,24},{9,... | collective-permute-start | bytes 774152 | tf_op jit(solution)/shard_map/ppermute | solution.py:88
  20.7 6.3 %collective-permute-start.8 = (bf16[992,128]{1,0:T(8,128)(2,1)S(1)}, bf16[992,128]{1,0:T(8,128)(2,1)S(1)}, u32[]{:S(2)}, u32[]{:S(2)}) collective-permute-start(bf16[992,128]{1,0:T(8,128)(2,1)S(1)} %get-tuple-element.22), channel_id=1, source_target_pairs={{0,1},{1,0},{2,4},{3,5},{4,2},{5,3},{6,7},{7,6},{8,9},{9,8},{10,12... | collective-permute-start | bytes 761864 | tf_op jit(solution)/shard_map/ppermute | solution.py:88
  22.2 1.5 %collective-permute-start.3 = (bf16[992,128]{1,0:T(8,128)(2,1)S(1)}, bf16[992,128]{1,0:T(8,128)(2,1)S(1)}, u32[]{:S(2)}, u32[]{:S(2)}) collective-permute-start(bf16[992,128]{1,0:T(8,128)(2,1)S(1)} %collective-permute-done.2), channel_id=1, source_target_pairs={{0,8},{1,9},{2,10},{3,11},{4,12},{5,13},{6,14},{7,15},{8,0},{9,1},... | collective-permute-start | bytes 761864 | tf_op jit(solution)/shard_map/ppermute | solution.py:88
  23.8 1.5 %collective-permute-start.16 = (bf16[992,128]{1,0:T(8,128)(2,1)S(1)}, bf16[992,128]{1,0:T(8,128)(2,1)S(1)}, u32[]{:S(2)}, u32[]{:S(2)}) collective-permute-start(bf16[992,128]{1,0:T(8,128)(2,1)S(1)} %collective-permute-done.6), channel_id=1, source_target_pairs={{0,8},{1,9},{2,10},{3,11},{4,12},{5,13},{6,14},{7,15},{8,0},{9,1},... | collective-permute-start | bytes 761864 | tf_op jit(solution)/shard_map/ppermute | solution.py:88
  23.9 27.2 %collective-permute-start.15 = (bf16[1008,128]{1,0:T(8,128)(2,1)S(1)}, bf16[1008,128]{1,0:T(8,128)(2,1)S(1)}, u32[]{:S(2)}, u32[]{:S(2)}) collective-permute-start(bf16[1008,128]{1,0:T(8,128)(2,1)S(1)} %get-tuple-element.23), channel_id=1, source_target_pairs={{0,8},{1,9},{2,3},{3,2},{4,5},{5,4},{6,14},{7,15},{8,0},{9,1},{10,... | collective-permute-start | bytes 774152 | tf_op jit(solution)/shard_map/ppermute | solution.py:88
  25.3 3.3 %collective-permute-start.5 = (bf16[1008,128]{1,0:T(8,128)(2,1)S(1)}, bf16[1008,128]{1,0:T(8,128)(2,1)S(1)}, u32[]{:S(2)}, u32[]{:S(2)}) collective-permute-start(bf16[1008,128]{1,0:T(8,128)(2,1)S(1)} %collective-permute-done.4), channel_id=1, source_target_pairs={{0,8},{1,9},{2,10},{3,11},{4,12},{5,13},{6,14},{7,15},{8,0},{9,1},... | collective-permute-start | bytes 774152 | tf_op jit(solution)/shard_map/ppermute | solution.py:88
  25.5 25.6 %collective-permute-start.14 = (bf16[992,128]{1,0:T(8,128)(2,1)S(1)}, bf16[992,128]{1,0:T(8,128)(2,1)S(1)}, u32[]{:S(2)}, u32[]{:S(2)}) collective-permute-start(bf16[992,128]{1,0:T(8,128)(2,1)S(1)} %get-tuple-element.22), channel_id=1, source_target_pairs={{0,8},{1,9},{2,3},{3,2},{4,5},{5,4},{6,14},{7,15},{8,0},{9,1},{10,... | collective-permute-start | bytes 761864 | tf_op jit(solution)/shard_map/ppermute | solution.py:88
  26.9 34.0 %collective-permute-start.18 = (bf16[992,128]{1,0:T(8,128)(2,1)S(1)}, bf16[992,128]{1,0:T(8,128)(2,1)S(1)}, u32[]{:S(2)}, u32[]{:S(2)}) collective-permute-start(bf16[992,128]{1,0:T(8,128)(2,1)S(1)} %collective-permute-done.6), channel_id=1, source_target_pairs={{0,16},{1,17},{2,18},{3,19},{4,20},{5,21},{6,22},{7,23},{8,24},{9,... | collective-permute-start | bytes 761864 | tf_op jit(solution)/shard_map/ppermute | solution.py:88
  28.6 2.0 %collective-permute-start.22 = (bf16[992,128]{1,0:T(8,128)(2,1)S(1)}, bf16[992,128]{1,0:T(8,128)(2,1)S(1)}, u32[]{:S(2)}, u32[]{:S(2)}) collective-permute-start(bf16[992,128]{1,0:T(8,128)(2,1)S(1)} %collective-permute-done.8), channel_id=1, source_target_pairs={{0,8},{1,9},{2,3},{3,2},{4,5},{5,4},{6,14},{7,15},{8,0},{9,1},{10,... | collective-permute-start | bytes 761864 | tf_op jit(solution)/shard_map/ppermute | solution.py:88
  28.6 3.6 %collective-permute-start.23 = (bf16[1008,128]{1,0:T(8,128)(2,1)S(1)}, bf16[1008,128]{1,0:T(8,128)(2,1)S(1)}, u32[]{:S(2)}, u32[]{:S(2)}) collective-permute-start(bf16[1008,128]{1,0:T(8,128)(2,1)S(1)} %collective-permute-done.9), channel_id=1, source_target_pairs={{0,8},{1,9},{2,3},{3,2},{4,5},{5,4},{6,14},{7,15},{8,0},{9,1},{10,... | collective-permute-start | bytes 774152 | tf_op jit(solution)/shard_map/ppermute | solution.py:88
  30.6 22.6 %collective-permute-start.12 = (bf16[992,128]{1,0:T(8,128)(2,1)S(1)}, bf16[992,128]{1,0:T(8,128)(2,1)S(1)}, u32[]{:S(2)}, u32[]{:S(2)}) collective-permute-start(bf16[992,128]{1,0:T(8,128)(2,1)S(1)} %collective-permute-done.6), channel_id=1, source_target_pairs={{0,1},{1,0},{2,4},{3,5},{4,2},{5,3},{6,7},{7,6},{8,9},{9,8},{10,12... | collective-permute-start | bytes 761864 | tf_op jit(solution)/shard_map/ppermute | solution.py:88
  32.2 28.9 %collective-permute-start.10 = (bf16[992,128]{1,0:T(8,128)(2,1)S(1)}, bf16[992,128]{1,0:T(8,128)(2,1)S(1)}, u32[]{:S(2)}, u32[]{:S(2)}) collective-permute-start(bf16[992,128]{1,0:T(8,128)(2,1)S(1)} %collective-permute-done.8), channel_id=1, source_target_pairs={{0,2},{1,3},{2,0},{3,1},{4,6},{5,7},{6,4},{7,5},{8,10},{9,11},{10,... | collective-permute-start | bytes 761864 | tf_op jit(solution)/shard_map/ppermute | solution.py:88
  51.1 17.4 %collective-permute-start.17 = (bf16[1008,128]{1,0:T(8,128)(2,1)S(1)}, bf16[1008,128]{1,0:T(8,128)(2,1)S(1)}, u32[]{:S(2)}, u32[]{:S(2)}) collective-permute-start(bf16[1008,128]{1,0:T(8,128)(2,1)S(1)} %collective-permute-done.7), channel_id=1, source_target_pairs={{0,8},{1,9},{2,10},{3,11},{4,12},{5,13},{6,14},{7,15},{8,0},{9,1},... | collective-permute-start | bytes 774152 | tf_op jit(solution)/shard_map/ppermute | solution.py:88
  51.2 8.6 %collective-permute-start.13 = (bf16[1008,128]{1,0:T(8,128)(2,1)S(1)}, bf16[1008,128]{1,0:T(8,128)(2,1)S(1)}, u32[]{:S(2)}, u32[]{:S(2)}) collective-permute-start(bf16[1008,128]{1,0:T(8,128)(2,1)S(1)} %collective-permute-done.7), channel_id=1, source_target_pairs={{0,1},{1,0},{2,4},{3,5},{4,2},{5,3},{6,7},{7,6},{8,9},{9,8},{10,12... | collective-permute-start | bytes 774152 | tf_op jit(solution)/shard_map/ppermute | solution.py:88
  53.2 15.3 %collective-permute-start.20 = (bf16[1008,128]{1,0:T(8,128)(2,1)S(1)}, bf16[1008,128]{1,0:T(8,128)(2,1)S(1)}, u32[]{:S(2)}, u32[]{:S(2)}) collective-permute-start(bf16[1008,128]{1,0:T(8,128)(2,1)S(1)} %collective-permute-done.7), channel_id=1, source_target_pairs={{0,16},{1,17},{2,18},{3,19},{4,20},{5,21},{6,22},{7,23},{8,24},{9,... | collective-permute-start | bytes 774152 | tf_op jit(solution)/shard_map/ppermute | solution.py:88
  59.8 7.7 %collective-permute-start.11 = (bf16[1008,128]{1,0:T(8,128)(2,1)S(1)}, bf16[1008,128]{1,0:T(8,128)(2,1)S(1)}, u32[]{:S(2)}, u32[]{:S(2)}) collective-permute-start(bf16[1008,128]{1,0:T(8,128)(2,1)S(1)} %collective-permute-done.9), channel_id=1, source_target_pairs={{0,2},{1,3},{2,0},{3,1},{4,6},{5,7},{6,4},{7,5},{8,10},{9,11},{10,... | collective-permute-start | bytes 774152 | tf_op jit(solution)/shard_map/ppermute | solution.py:88
  61.0 9.3 %collective-permute-start.25 = (bf16[992,128]{1,0:T(8,128)(2,1)S(1)}, bf16[992,128]{1,0:T(8,128)(2,1)S(1)}, u32[]{:S(2)}, u32[]{:S(2)}) collective-permute-start(bf16[992,128]{1,0:T(8,128)(2,1)S(1)} %collective-permute-done.12), channel_id=1, source_target_pairs={{0,8},{1,9},{2,3},{3,2},{4,5},{5,4},{6,14},{7,15},{8,0},{9,1},{10,... | collective-permute-start | bytes 761864 | tf_op jit(solution)/shard_map/ppermute | solution.py:88
  61.1 8.2 %collective-permute-start.19 = (bf16[992,128]{1,0:T(8,128)(2,1)S(1)}, bf16[992,128]{1,0:T(8,128)(2,1)S(1)}, u32[]{:S(2)}, u32[]{:S(2)}) collective-permute-start(bf16[992,128]{1,0:T(8,128)(2,1)S(1)} %collective-permute-done.18), channel_id=1, source_target_pairs={{0,8},{1,9},{2,10},{3,11},{4,12},{5,13},{6,14},{7,15},{8,0},{9,1},... | collective-permute-start | bytes 761864 | tf_op jit(solution)/shard_map/ppermute | solution.py:88
  68.2 2.2 %collective-permute-start.26 = (bf16[1008,128]{1,0:T(8,128)(2,1)S(1)}, bf16[1008,128]{1,0:T(8,128)(2,1)S(1)}, u32[]{:S(2)}, u32[]{:S(2)}) collective-permute-start(bf16[1008,128]{1,0:T(8,128)(2,1)S(1)} %collective-permute-done.11), channel_id=1, source_target_pairs={{0,8},{1,9},{2,4},{3,5},{4,2},{5,3},{6,14},{7,15},{8,0},{9,1},{10,... | collective-permute-start | bytes 774152 | tf_op jit(solution)/shard_map/ppermute | solution.py:88
  68.6 1.7 %collective-permute-start.21 = (bf16[1008,128]{1,0:T(8,128)(2,1)S(1)}, bf16[1008,128]{1,0:T(8,128)(2,1)S(1)}, u32[]{:S(2)}, u32[]{:S(2)}) collective-permute-start(bf16[1008,128]{1,0:T(8,128)(2,1)S(1)} %collective-permute-done.20), channel_id=1, source_target_pairs={{0,8},{1,9},{2,10},{3,11},{4,12},{5,13},{6,14},{7,15},{8,0},{9,1},... | collective-permute-start | bytes 774152 | tf_op jit(solution)/shard_map/ppermute | solution.py:88
  70.8 9.7 %collective-permute-start.27 = (f16[1,128,4,128]{3,1,2,0:T(8,128)(2,1)S(1)}, f16[1,128,4,128]{3,1,2,0:T(8,128)(2,1)S(1)}, u32[]{:S(2)}, u32[]{:S(2)}) collective-permute-start(f16[1,128,4,128]{3,1,2,0:T(8,128)(2,1)S(1)} %fusion.19), channel_id=1, source_target_pairs={{0,2},{1,3},{2,0},{3,1},{4,6},{5,7},{6,4},{7,5},{8,10},{9,11},{10,... | collective-permute-start | bytes 393224 | tf_op jit(solution)/shard_map/ppermute | solution.py:88
  77.3 7.5 %collective-permute-start.24 = (f16[2,128,4,128]{3,1,2,0:T(8,128)(2,1)S(1)}, f16[2,128,4,128]{3,1,2,0:T(8,128)(2,1)S(1)}, u32[]{:S(2)}, u32[]{:S(2)}) collective-permute-start(f16[2,128,4,128]{3,1,2,0:T(8,128)(2,1)S(1)} %pad_maximum_fusion), channel_id=1, source_target_pairs={{0,2},{1,3},{2,0},{3,1},{4,6},{5,7},{6,4},{7,5},{8,10},{9,11},{10,... | collective-permute-start | bytes 786440 | tf_op jit(solution)/shard_map/ppermute | solution.py:88
  85.4 1.3 %copy-start.1 = (f32[8,128,4,128]{3,2,1,0:T(4,128)}, f32[8,128,4,128]{3,2,1,0:T(4,128)S(1)}, u32[]{:S(2)}) copy-start(f32[8,128,4,128]{3,2,1,0:T(4,128)S(1)} %copy_dynamic-update-slice_fusion) | copy-start | bytes 6291460

commit v4 on v3

--- a/solution.py
+++ b/solution.py
@@ -109,40 +109,49 @@
     data = descriptors.T
     cut = data.shape[0] // 32 * 16
     unit = normalize(data, cut)
-    head, pair = [None, None], [None, None]
-    across = [[None, None] for _ in offsets]
-    own = {0: unit}
-    for j in others:
-        own[j] = [None, None]
+    head, pair, relay, head_pair = ([None, None] for _ in range(4))
+    across, centre_across = ([[None, None] for _ in offsets] for _ in range(2))
+    across_pair = [[None, None] for _ in range(2, inner)]
+    own, end = {0: unit}, {0: pair}
+    for j in others:
+        own[j], end[j] = [None, None], [None, None]
     for h in halves:
         head[h] = send(unit[h], centre_swap(1))
-        pair[h] = send(unit[h], line_swap)
         for k in offsets:
             across[k - 1][h] = send(unit[h], shift(k, k + 1))
+        pair[h] = send(unit[h], line_swap)
+        if h == 0:
+            for j in others:
+                own[j][h] = send(unit[h], other(j))
+    swapped = {("own", 0, h): send(unit[h], core_swap) for h in halves}
+    for h in halves:
         for j in others:
-            own[j][h] = send(unit[h], other(j))
-    relay, head_pair, end = [None, None], [None, None], {0: pair}
-    across_pair = [[None, None] for _ in range(2, inner)]
-    centre_across = [[None, None] for _ in offsets]
-    for j in others:
-        end[j] = [None, None]
-    for h in halves:
+            end[j][h] = send(pair[h], other(j))
         relay[h] = send(pair[h], centre_swap(inner - 1))
         for k in offsets:
             centre_across[k - 1][h] = send(head[h], shift(k, 0))
         head_pair[h] = send(head[h], line_swap)
         for k in range(2, inner):
             across_pair[k - 2][h] = send(across[k - 2][h], line_swap)
-        for j in others:
-            end[j][h] = send(pair[h], other(j))
-
-    def columns_of(parts):
+    for j in others:
+        own[j][1] = send(unit[1], other(j))
+    for j in others:
+        swapped["own", j, 0] = send(own[j][0], core_swap)
+    swapped.update({("end", 0, h): send(pair[h], core_swap) for h in halves})
+    for j in others:
+        swapped["end", j, 0] = send(end[j][0], core_swap)
+    far_across = [[send(head_pair[0] if k == 1 else across_pair[k - 2][0], centre_swap(0)), None] for k in offsets]
+    for j in others:
+        swapped["end", j, 1] = send(end[j][1], core_swap)
+    for k in offsets:
+        far_across[k - 1][1] = send(relay[1], shift(k, 0))
+
+    def columns_of(name, parts):
         full = jnp.zeros((ngroups,) + data.shape, jnp.bfloat16)
         for j in sorted(parts):
             for h in halves:
-                part = parts[j][h]
-                swapped = send(part, core_swap)
-                for array, index in ((part, at["own", j]), (swapped, at["swapped", j])):
+                pieces = ((parts[j][h], at["own", j]), (swapped[name, j, h], at["swapped", j]))
+                for array, index in pieces:
                     full = lax.dynamic_update_slice(
                         full, array[None], (index, h * cut, 0), allow_negative_indices=False
                     )
@@ -166,7 +175,15 @@
             out, value, index, 0, allow_negative_indices=False
         )
 
-    columns = columns_of(own)
+    def back(block):
+        panel = (fourth(block, end_columns) * SCALE).astype(jnp.float16)
+        return send(panel, line_swap)
+
+    end_columns = columns_of("end", end)
+    panels = [back(b) for b in [relay] + centre_across]
+    for j in others:
+        swapped["own", j, 1] = send(own[j][1], core_swap)
+    columns = columns_of("own", own)
     out = jnp.zeros((ncolumns, block, ngroups, block), jnp.float32)
     out = put(out, product(unit), at["unit"])
     out = put(out, product(pair), at["pair"])
@@ -174,27 +191,13 @@
     for k in range(1, inner - 1):
         out = put(out, product(across[k - 1]), at["across", k])
     mine = [product(across[-1])]
-    end_columns = columns_of(end)
-    far_across = []
-    for k in offsets:
-        source = head_pair if k == 1 else across_pair[k - 2]
-        second = send(source[1], centre_swap(0))
-        far_across.append([send(relay[0], shift(k, 0)), second])
-
-    def back(blocks):
-        panels = [(fourth(b, end_columns) * SCALE).astype(jnp.float16) for b in blocks]
-        return send(jnp.stack(panels), line_swap)
-
-    returned = back([relay] + centre_across)
-    returned_far = back(far_across)
+    panels += [back(b) for b in far_across]
     out = put(out, product(head_pair), at["head_pair"])
     out = put(out, product(relay), at["relay"])
     for k in range(2, inner):
         out = put(out, product(across_pair[k - 2]), at["across_pair", k])
-    mine += [product(b) for b in centre_across]
-    mine += [product(b) for b in far_across]
+    mine += [product(b) for b in centre_across + far_across]
     slots = [at["back", k] for k in range(inner)] + [at["far", k] for k in offsets]
-    panels = [returned[k] for k in range(inner)] + [returned_far[k - 1] for k in offsets]
     for index, panel, value in zip(slots, panels, mine):
         theirs = panel.astype(jnp.float32) * (1.0 / SCALE)
         out = put(out, jnp.where(middle, value, theirs), index)

time: 86.9 us -> 86.1 us (level)
  waiting for transfers between devices: 32.7 us -> 25.7 us
  starting transfers between devices: 42.3 us -> 48.6 us
    ppermute x28 -> x29, waiting for transfers between devices: 32.7 us -> 25.7 us  [send(): return lax.ppermute(array, AXES, pairs)]
    ppermute x28 -> x29, starting transfers between devices: 42.3 us -> 48.6 us  [send(): return lax.ppermute(array, AXES, pairs)]
  transfers between devices with their start and end apart: 28 -> 29, of which waited for: 10 -> 9; matrix products, arithmetic and copies ran while one was open for 8% -> 9% of each run, Pallas kernels for 0% -> 0%
where the time goes in v4:
time: 86.1 us; the launch traced here: 85.9 us
  starting transfers between devices  48.6 us (56%)
  waiting for transfers between devices  25.7 us (30%)
  local copies, waits for them, and re-layouts  5.46 us (6%)
  matrix products  5.31 us (6%)
    ppermute x29, starting transfers between devices, send(): return lax.ppermute(array, AXES, pairs)  48.6 us
    ppermute x29, waiting for transfers between devices, send(): return lax.ppermute(array, AXES, pairs)  25.7 us
    dot_general x11, matrix products, fourth(): lax.dot_general(jnp.concatenate(block, axis=0), cols, (((0,), (1,)), ((),...  5.31 us
    unnamed x4, local copies, waits for them, and re-layouts  2.53 us
  transfers between devices with their start and end apart: 29, of which 9 were waited for; matrix products, arithmetic and copies ran while one was open for 9% of the time, Pallas kernels for 0%

profile of v4, /device:TPU:0, one launch (start us, length us, event | category | flops | bytes accessed | tf_op | source)
XLA Modules:
  0.0 85.9 jit_solution(10110139361540842330)
XLA Ops:
  0.0 1.2 %copy-done = f32[128,2000]{0,1:T(8,128)S(1)} copy-done((f32[128,2000]{0,1:T(8,128)S(1)}, f32[128,2000]{0,1:T(8,128)}, u32[]{:S(2)}) %copy-start) | copy-done | bytes 1024024
  1.2 0.3 normalize.1
  1.6 3.1 %collective-permute-start.6 = (bf16[992,128]{1,0:T(8,128)(2,1)S(1)}, bf16[992,128]{1,0:T(8,128)(2,1)S(1)}, u32[]{:S(2)}, u32[]{:S(2)}) collective-permute-start(bf16[992,128]{1,0:T(8,128)(2,1)S(1)} %get-tuple-element.22), channel_id=1, source_target_pairs={{0,2},{1,3},{2,0},{3,1},{4,6},{5,7},{6,4},{7,5},{8,10},{9,11},{10,... | collective-permute-start | bytes 761864 | tf_op jit(solution)/shard_map/ppermute | solution.py:88
  4.7 1.5 %collective-permute-start.8 = (bf16[992,128]{1,0:T(8,128)(2,1)S(1)}, bf16[992,128]{1,0:T(8,128)(2,1)S(1)}, u32[]{:S(2)}, u32[]{:S(2)}) collective-permute-start(bf16[992,128]{1,0:T(8,128)(2,1)S(1)} %get-tuple-element.22), channel_id=1, source_target_pairs={{0,1},{1,0},{2,4},{3,5},{4,2},{5,3},{6,7},{7,6},{8,9},{9,8},{10,12... | collective-permute-start | bytes 761864 | tf_op jit(solution)/shard_map/ppermute | solution.py:88
  6.2 1.7 %collective-permute-start.7 = (bf16[1008,128]{1,0:T(8,128)(2,1)S(1)}, bf16[1008,128]{1,0:T(8,128)(2,1)S(1)}, u32[]{:S(2)}, u32[]{:S(2)}) collective-permute-start(bf16[1008,128]{1,0:T(8,128)(2,1)S(1)} %get-tuple-element.23), channel_id=1, source_target_pairs={{0,2},{1,3},{2,0},{3,1},{4,6},{5,7},{6,4},{7,5},{8,10},{9,11},{10,... | collective-permute-start | bytes 774152 | tf_op jit(solution)/shard_map/ppermute | solution.py:88
  7.8 0.2 collective-permute-start.1
  8.1 0.3 broadcast.17.clone
  8.4 3.3 %collective-permute-done.6 = bf16[992,128]{1,0:T(8,128)(2,1)S(1)} collective-permute-done((bf16[992,128]{1,0:T(8,128)(2,1)S(1)}, bf16[992,128]{1,0:T(8,128)(2,1)S(1)}, u32[]{:S(2)}, u32[]{:S(2)}) %collective-permute-start.6) | collective-permute-done | bytes 253984 | tf_op jit(solution)/shard_map/ppermute | solution.py:88
  11.7 2.0 %collective-permute-start.2 = (bf16[992,128]{1,0:T(8,128)(2,1)S(1)}, bf16[992,128]{1,0:T(8,128)(2,1)S(1)}, u32[]{:S(2)}, u32[]{:S(2)}) collective-permute-start(bf16[992,128]{1,0:T(8,128)(2,1)S(1)} %get-tuple-element.22), channel_id=1, source_target_pairs={{0,16},{1,17},{2,18},{3,19},{4,20},{5,21},{6,22},{7,23},{8,24},{9,... | collective-permute-start | bytes 761864 | tf_op jit(solution)/shard_map/ppermute | solution.py:88
  13.6 0.3 broadcast.17.clone.1
  14.2 6.5 %collective-permute-done.2 = bf16[992,128]{1,0:T(8,128)(2,1)S(1)} collective-permute-done((bf16[992,128]{1,0:T(8,128)(2,1)S(1)}, bf16[992,128]{1,0:T(8,128)(2,1)S(1)}, u32[]{:S(2)}, u32[]{:S(2)}) %collective-permute-start.2) | collective-permute-done | bytes 253984 | tf_op jit(solution)/shard_map/ppermute | solution.py:88
  20.7 1.6 %collective-permute-start.9 = (bf16[1008,128]{1,0:T(8,128)(2,1)S(1)}, bf16[1008,128]{1,0:T(8,128)(2,1)S(1)}, u32[]{:S(2)}, u32[]{:S(2)}) collective-permute-start(bf16[1008,128]{1,0:T(8,128)(2,1)S(1)} %get-tuple-element.23), channel_id=1, source_target_pairs={{0,1},{1,0},{2,4},{3,5},{4,2},{5,3},{6,7},{7,6},{8,9},{9,8},{10,12... | collective-permute-start | bytes 774152 | tf_op jit(solution)/shard_map/ppermute | solution.py:88
  22.3 1.4 %collective-permute-done.3 = bf16[992,128]{1,0:T(8,128)(2,1)S(1)} collective-permute-done((bf16[992,128]{1,0:T(8,128)(2,1)S(1)}, bf16[992,128]{1,0:T(8,128)(2,1)S(1)}, u32[]{:S(2)}, u32[]{:S(2)}) %collective-permute-start.3) | collective-permute-done | bytes 253984 | tf_op jit(solution)/shard_map/ppermute | solution.py:88
  23.9 0.4 collective-permute-start.15
  24.4 0.9 %collective-permute-done.16 = bf16[992,128]{1,0:T(8,128)(2,1)S(1)} collective-permute-done((bf16[992,128]{1,0:T(8,128)(2,1)S(1)}, bf16[992,128]{1,0:T(8,128)(2,1)S(1)}, u32[]{:S(2)}, u32[]{:S(2)}) %collective-permute-start.16) | collective-permute-done | bytes 253984 | tf_op jit(solution)/shard_map/ppermute | solution.py:88
  25.5 0.4 collective-permute-start.14
  26.0 1.6 %collective-permute-start.18 = (bf16[992,128]{1,0:T(8,128)(2,1)S(1)}, bf16[992,128]{1,0:T(8,128)(2,1)S(1)}, u32[]{:S(2)}, u32[]{:S(2)}) collective-permute-start(bf16[992,128]{1,0:T(8,128)(2,1)S(1)} %collective-permute-done.6), channel_id=1, source_target_pairs={{0,16},{1,17},{2,18},{3,19},{4,20},{5,21},{6,22},{7,23},{8,24},{9,... | collective-permute-start | bytes 761864 | tf_op jit(solution)/shard_map/ppermute | solution.py:88
  27.6 0.5 collective-permute-start.24
  28.1 0.5 fusion.10
  28.6 0.5 fusion.8
  29.1 0.5 fusion.9
  29.6 16.1 %collective-permute-start.10 = (bf16[992,128]{1,0:T(8,128)(2,1)S(1)}, bf16[992,128]{1,0:T(8,128)(2,1)S(1)}, u32[]{:S(2)}, u32[]{:S(2)}) collective-permute-start(bf16[992,128]{1,0:T(8,128)(2,1)S(1)} %collective-permute-done.8), channel_id=1, source_target_pairs={{0,2},{1,3},{2,0},{3,1},{4,6},{5,7},{6,4},{7,5},{8,10},{9,11},{10,... | collective-permute-start | bytes 761864 | tf_op jit(solution)/shard_map/ppermute | solution.py:88
  45.7 1.5 %collective-permute-start.12 = (bf16[992,128]{1,0:T(8,128)(2,1)S(1)}, bf16[992,128]{1,0:T(8,128)(2,1)S(1)}, u32[]{:S(2)}, u32[]{:S(2)}) collective-permute-start(bf16[992,128]{1,0:T(8,128)(2,1)S(1)} %collective-permute-done.6), channel_id=1, source_target_pairs={{0,1},{1,0},{2,4},{3,5},{4,2},{5,3},{6,7},{7,6},{8,9},{9,8},{10,12... | collective-permute-start | bytes 761864 | tf_op jit(solution)/shard_map/ppermute | solution.py:88
  47.1 0.5 fusion.3
  47.7 4.0 %collective-permute-start.11 = (bf16[1008,128]{1,0:T(8,128)(2,1)S(1)}, bf16[1008,128]{1,0:T(8,128)(2,1)S(1)}, u32[]{:S(2)}, u32[]{:S(2)}) collective-permute-start(bf16[1008,128]{1,0:T(8,128)(2,1)S(1)} %collective-permute-done.9), channel_id=1, source_target_pairs={{0,2},{1,3},{2,0},{3,1},{4,6},{5,7},{6,4},{7,5},{8,10},{9,11},{10,... | collective-permute-start | bytes 774152 | tf_op jit(solution)/shard_map/ppermute | solution.py:88
  51.7 0.5 fusion.5
  52.2 1.6 %collective-permute-start.20 = (bf16[1008,128]{1,0:T(8,128)(2,1)S(1)}, bf16[1008,128]{1,0:T(8,128)(2,1)S(1)}, u32[]{:S(2)}, u32[]{:S(2)}) collective-permute-start(bf16[1008,128]{1,0:T(8,128)(2,1)S(1)} %collective-permute-done.7), channel_id=1, source_target_pairs={{0,16},{1,17},{2,18},{3,19},{4,20},{5,21},{6,22},{7,23},{8,24},{9,... | collective-permute-start | bytes 774152 | tf_op jit(solution)/shard_map/ppermute | solution.py:88
  53.8 4.7 %collective-permute-done.11 = bf16[1008,128]{1,0:T(8,128)(2,1)S(1)} collective-permute-done((bf16[1008,128]{1,0:T(8,128)(2,1)S(1)}, bf16[1008,128]{1,0:T(8,128)(2,1)S(1)}, u32[]{:S(2)}, u32[]{:S(2)}) %collective-permute-start.11) | collective-permute-done | bytes 258080 | tf_op jit(solution)/shard_map/ppermute | solution.py:88
  58.5 1.5 %collective-permute-start.13 = (bf16[1008,128]{1,0:T(8,128)(2,1)S(1)}, bf16[1008,128]{1,0:T(8,128)(2,1)S(1)}, u32[]{:S(2)}, u32[]{:S(2)}) collective-permute-start(bf16[1008,128]{1,0:T(8,128)(2,1)S(1)} %collective-permute-done.7), channel_id=1, source_target_pairs={{0,1},{1,0},{2,4},{3,5},{4,2},{5,3},{6,7},{7,6},{8,9},{9,8},{10,12... | collective-permute-start | bytes 774152 | tf_op jit(solution)/shard_map/ppermute | solution.py:88
  60.0 0.5 fusion.7
  60.5 0.3 broadcast_in_dim.76
  61.2 0.5 collective-permute-start.19
  61.7 4.7 %collective-permute-done.13 = bf16[1008,128]{1,0:T(8,128)(2,1)S(1)} collective-permute-done((bf16[1008,128]{1,0:T(8,128)(2,1)S(1)}, bf16[1008,128]{1,0:T(8,128)(2,1)S(1)}, u32[]{:S(2)}, u32[]{:S(2)}) %collective-permute-start.13) | collective-permute-done | bytes 258080 | tf_op jit(solution)/shard_map/ppermute | solution.py:88
  66.5 0.5 fusion.6
  67.2 0.2 copy_dynamic-update-slice_fusion.4
  67.5 0.6 collective-permute-start.21
  68.4 0.9 %collective-permute-done.21 = bf16[1008,128]{1,0:T(8,128)(2,1)S(1)} collective-permute-done((bf16[1008,128]{1,0:T(8,128)(2,1)S(1)}, bf16[1008,128]{1,0:T(8,128)(2,1)S(1)}, u32[]{:S(2)}, u32[]{:S(2)}) %collective-permute-start.21) | collective-permute-done | bytes 258080 | tf_op jit(solution)/shard_map/ppermute | solution.py:88
  69.3 0.5 fusion.14
  69.8 7.2 %collective-permute-start.28 = (f16[128,4,128]{2,0,1:T(8,128)(2,1)S(1)}, f16[128,4,128]{2,0,1:T(8,128)(2,1)S(1)}, u32[]{:S(2)}, u32[]{:S(2)}) collective-permute-start(f16[128,4,128]{2,0,1:T(8,128)(2,1)S(1)} %fusion.14), channel_id=1, source_target_pairs={{0,2},{1,3},{2,0},{3,1},{4,6},{5,7},{6,4},{7,5},{8,10},{9,11},{10,... | collective-permute-start | bytes 393224 | tf_op jit(solution)/shard_map/ppermute | solution.py:88
  77.0 0.5 fusion.16
  77.5 0.5 fusion.1
  78.0 0.5 fusion.15
  78.5 2.1 %collective-permute-start.25 = (f16[128,4,128]{2,0,1:T(8,128)(2,1)S(1)}, f16[128,4,128]{2,0,1:T(8,128)(2,1)S(1)}, u32[]{:S(2)}, u32[]{:S(2)}) collective-permute-start(f16[128,4,128]{2,0,1:T(8,128)(2,1)S(1)} %fusion.15), channel_id=1, source_target_pairs={{0,2},{1,3},{2,0},{3,1},{4,6},{5,7},{6,4},{7,5},{8,10},{9,11},{10,... | collective-permute-start | bytes 393224 | tf_op jit(solution)/shard_map/ppermute | solution.py:88
  80.6 2.1 %collective-permute-done.22 = f16[128,4,128]{2,0,1:T(8,128)(2,1)S(1)} collective-permute-done((f16[128,4,128]{2,0,1:T(8,128)(2,1)S(1)}, f16[128,4,128]{2,0,1:T(8,128)(2,1)S(1)}, u32[]{:S(2)}, u32[]{:S(2)}) %collective-permute-start.22) | collective-permute-done | bytes 131104 | tf_op jit(solution)/shard_map/ppermute | solution.py:88
  82.8 0.2 copy_dynamic-update-slice_fusion.2
  83.0 1.2 %collective-permute-done.25 = f16[128,4,128]{2,0,1:T(8,128)(2,1)S(1)} collective-permute-done((f16[128,4,128]{2,0,1:T(8,128)(2,1)S(1)}, f16[128,4,128]{2,0,1:T(8,128)(2,1)S(1)}, u32[]{:S(2)}, u32[]{:S(2)}) %collective-permute-start.25) | collective-permute-done | bytes 131104 | tf_op jit(solution)/shard_map/ppermute | solution.py:88
  84.2 0.2 copy_dynamic-update-slice_fusion.1
  84.6 1.3 %copy-done.1 = f32[8,128,4,128]{3,2,1,0:T(4,128)} copy-done((f32[8,128,4,128]{3,2,1,0:T(4,128)}, f32[8,128,4,128]{3,2,1,0:T(4,128)S(1)}, u32[]{:S(2)}) %copy-start.1) | copy-done | bytes 2097176
  (56 shorter events, 2.4 us)
Async XLA Ops:
  0.0 1.2 %copy-start = (f32[128,2000]{0,1:T(8,128)S(1)}, f32[128,2000]{0,1:T(8,128)}, u32[]{:S(2)}) copy-start(f32[128,2000]{0,1:T(8,128)} %param.1) | copy-start | bytes 3072004
  1.6 10.1 %collective-permute-start.6 = (bf16[992,128]{1,0:T(8,128)(2,1)S(1)}, bf16[992,128]{1,0:T(8,128)(2,1)S(1)}, u32[]{:S(2)}, u32[]{:S(2)}) collective-permute-start(bf16[992,128]{1,0:T(8,128)(2,1)S(1)} %get-tuple-element.22), channel_id=1, source_target_pairs={{0,2},{1,3},{2,0},{3,1},{4,6},{5,7},{6,4},{7,5},{8,10},{9,11},{10,... | collective-permute-start | bytes 761864 | tf_op jit(solution)/shard_map/ppermute | solution.py:88
  4.7 21.3 %collective-permute-start.8 = (bf16[992,128]{1,0:T(8,128)(2,1)S(1)}, bf16[992,128]{1,0:T(8,128)(2,1)S(1)}, u32[]{:S(2)}, u32[]{:S(2)}) collective-permute-start(bf16[992,128]{1,0:T(8,128)(2,1)S(1)} %get-tuple-element.22), channel_id=1, source_target_pairs={{0,1},{1,0},{2,4},{3,5},{4,2},{5,3},{6,7},{7,6},{8,9},{9,8},{10,12... | collective-permute-start | bytes 761864 | tf_op jit(solution)/shard_map/ppermute | solution.py:88
  6.2 7.8 %collective-permute-start = (bf16[992,128]{1,0:T(8,128)(2,1)S(1)}, bf16[992,128]{1,0:T(8,128)(2,1)S(1)}, u32[]{:S(2)}, u32[]{:S(2)}) collective-permute-start(bf16[992,128]{1,0:T(8,128)(2,1)S(1)} %get-tuple-element.22), channel_id=1, source_target_pairs={{0,8},{1,9},{2,10},{3,11},{4,12},{5,13},{6,14},{7,15},{8,0},{9,1},... | collective-permute-start | bytes 761864 | tf_op jit(solution)/shard_map/ppermute | solution.py:88
  6.2 19.3 %collective-permute-start.7 = (bf16[1008,128]{1,0:T(8,128)(2,1)S(1)}, bf16[1008,128]{1,0:T(8,128)(2,1)S(1)}, u32[]{:S(2)}, u32[]{:S(2)}) collective-permute-start(bf16[1008,128]{1,0:T(8,128)(2,1)S(1)} %get-tuple-element.23), channel_id=1, source_target_pairs={{0,2},{1,3},{2,0},{3,1},{4,6},{5,7},{6,4},{7,5},{8,10},{9,11},{10,... | collective-permute-start | bytes 774152 | tf_op jit(solution)/shard_map/ppermute | solution.py:88
  7.8 14.4 %collective-permute-start.1 = (bf16[1008,128]{1,0:T(8,128)(2,1)S(1)}, bf16[1008,128]{1,0:T(8,128)(2,1)S(1)}, u32[]{:S(2)}, u32[]{:S(2)}) collective-permute-start(bf16[1008,128]{1,0:T(8,128)(2,1)S(1)} %get-tuple-element.23), channel_id=1, source_target_pairs={{0,8},{1,9},{2,10},{3,11},{4,12},{5,13},{6,14},{7,15},{8,0},{9,1},... | collective-permute-start | bytes 774152 | tf_op jit(solution)/shard_map/ppermute | solution.py:88
  11.7 9.0 %collective-permute-start.2 = (bf16[992,128]{1,0:T(8,128)(2,1)S(1)}, bf16[992,128]{1,0:T(8,128)(2,1)S(1)}, u32[]{:S(2)}, u32[]{:S(2)}) collective-permute-start(bf16[992,128]{1,0:T(8,128)(2,1)S(1)} %get-tuple-element.22), channel_id=1, source_target_pairs={{0,16},{1,17},{2,18},{3,19},{4,20},{5,21},{6,22},{7,23},{8,24},{9,... | collective-permute-start | bytes 761864 | tf_op jit(solution)/shard_map/ppermute | solution.py:88
  13.9 10.0 %collective-permute-start.4 = (bf16[1008,128]{1,0:T(8,128)(2,1)S(1)}, bf16[1008,128]{1,0:T(8,128)(2,1)S(1)}, u32[]{:S(2)}, u32[]{:S(2)}) collective-permute-start(bf16[1008,128]{1,0:T(8,128)(2,1)S(1)} %get-tuple-element.23), channel_id=1, source_target_pairs={{0,16},{1,17},{2,18},{3,19},{4,20},{5,21},{6,22},{7,23},{8,24},{9,... | collective-permute-start | bytes 774152 | tf_op jit(solution)/shard_map/ppermute | solution.py:88
  20.7 6.9 %collective-permute-start.9 = (bf16[1008,128]{1,0:T(8,128)(2,1)S(1)}, bf16[1008,128]{1,0:T(8,128)(2,1)S(1)}, u32[]{:S(2)}, u32[]{:S(2)}) collective-permute-start(bf16[1008,128]{1,0:T(8,128)(2,1)S(1)} %get-tuple-element.23), channel_id=1, source_target_pairs={{0,1},{1,0},{2,4},{3,5},{4,2},{5,3},{6,7},{7,6},{8,9},{9,8},{10,12... | collective-permute-start | bytes 774152 | tf_op jit(solution)/shard_map/ppermute | solution.py:88
  22.2 1.5 %collective-permute-start.3 = (bf16[992,128]{1,0:T(8,128)(2,1)S(1)}, bf16[992,128]{1,0:T(8,128)(2,1)S(1)}, u32[]{:S(2)}, u32[]{:S(2)}) collective-permute-start(bf16[992,128]{1,0:T(8,128)(2,1)S(1)} %collective-permute-done.2), channel_id=1, source_target_pairs={{0,8},{1,9},{2,10},{3,11},{4,12},{5,13},{6,14},{7,15},{8,0},{9,1},... | collective-permute-start | bytes 761864 | tf_op jit(solution)/shard_map/ppermute | solution.py:88
  23.8 1.5 %collective-permute-start.16 = (bf16[992,128]{1,0:T(8,128)(2,1)S(1)}, bf16[992,128]{1,0:T(8,128)(2,1)S(1)}, u32[]{:S(2)}, u32[]{:S(2)}) collective-permute-start(bf16[992,128]{1,0:T(8,128)(2,1)S(1)} %collective-permute-done.6), channel_id=1, source_target_pairs={{0,8},{1,9},{2,10},{3,11},{4,12},{5,13},{6,14},{7,15},{8,0},{9,1},... | collective-permute-start | bytes 761864 | tf_op jit(solution)/shard_map/ppermute | solution.py:88
  23.9 23.8 %collective-permute-start.15 = (bf16[1008,128]{1,0:T(8,128)(2,1)S(1)}, bf16[1008,128]{1,0:T(8,128)(2,1)S(1)}, u32[]{:S(2)}, u32[]{:S(2)}) collective-permute-start(bf16[1008,128]{1,0:T(8,128)(2,1)S(1)} %get-tuple-element.23), channel_id=1, source_target_pairs={{0,8},{1,9},{2,3},{3,2},{4,5},{5,4},{6,14},{7,15},{8,0},{9,1},{10,... | collective-permute-start | bytes 774152 | tf_op jit(solution)/shard_map/ppermute | solution.py:88
  25.3 2.3 %collective-permute-start.5 = (bf16[1008,128]{1,0:T(8,128)(2,1)S(1)}, bf16[1008,128]{1,0:T(8,128)(2,1)S(1)}, u32[]{:S(2)}, u32[]{:S(2)}) collective-permute-start(bf16[1008,128]{1,0:T(8,128)(2,1)S(1)} %collective-permute-done.4), channel_id=1, source_target_pairs={{0,8},{1,9},{2,10},{3,11},{4,12},{5,13},{6,14},{7,15},{8,0},{9,1},... | collective-permute-start | bytes 774152 | tf_op jit(solution)/shard_map/ppermute | solution.py:88
  25.5 22.2 %collective-permute-start.14 = (bf16[992,128]{1,0:T(8,128)(2,1)S(1)}, bf16[992,128]{1,0:T(8,128)(2,1)S(1)}, u32[]{:S(2)}, u32[]{:S(2)}) collective-permute-start(bf16[992,128]{1,0:T(8,128)(2,1)S(1)} %get-tuple-element.22), channel_id=1, source_target_pairs={{0,8},{1,9},{2,3},{3,2},{4,5},{5,4},{6,14},{7,15},{8,0},{9,1},{10,... | collective-permute-start | bytes 761864 | tf_op jit(solution)/shard_map/ppermute | solution.py:88
  26.0 35.2 %collective-permute-start.18 = (bf16[992,128]{1,0:T(8,128)(2,1)S(1)}, bf16[992,128]{1,0:T(8,128)(2,1)S(1)}, u32[]{:S(2)}, u32[]{:S(2)}) collective-permute-start(bf16[992,128]{1,0:T(8,128)(2,1)S(1)} %collective-permute-done.6), channel_id=1, source_target_pairs={{0,16},{1,17},{2,18},{3,19},{4,20},{5,21},{6,22},{7,23},{8,24},{9,... | collective-permute-start | bytes 761864 | tf_op jit(solution)/shard_map/ppermute | solution.py:88
  27.6 2.0 %collective-permute-start.23 = (bf16[992,128]{1,0:T(8,128)(2,1)S(1)}, bf16[992,128]{1,0:T(8,128)(2,1)S(1)}, u32[]{:S(2)}, u32[]{:S(2)}) collective-permute-start(bf16[992,128]{1,0:T(8,128)(2,1)S(1)} %collective-permute-done.8), channel_id=1, source_target_pairs={{0,8},{1,9},{2,3},{3,2},{4,5},{5,4},{6,14},{7,15},{8,0},{9,1},{10,... | collective-permute-start | bytes 761864 | tf_op jit(solution)/shard_map/ppermute | solution.py:88
  27.6 18.1 %collective-permute-start.24 = (bf16[1008,128]{1,0:T(8,128)(2,1)S(1)}, bf16[1008,128]{1,0:T(8,128)(2,1)S(1)}, u32[]{:S(2)}, u32[]{:S(2)}) collective-permute-start(bf16[1008,128]{1,0:T(8,128)(2,1)S(1)} %collective-permute-done.9), channel_id=1, source_target_pairs={{0,8},{1,9},{2,3},{3,2},{4,5},{5,4},{6,14},{7,15},{8,0},{9,1},{10,... | collective-permute-start | bytes 774152 | tf_op jit(solution)/shard_map/ppermute | solution.py:88
  29.6 22.6 %collective-permute-start.10 = (bf16[992,128]{1,0:T(8,128)(2,1)S(1)}, bf16[992,128]{1,0:T(8,128)(2,1)S(1)}, u32[]{:S(2)}, u32[]{:S(2)}) collective-permute-start(bf16[992,128]{1,0:T(8,128)(2,1)S(1)} %collective-permute-done.8), channel_id=1, source_target_pairs={{0,2},{1,3},{2,0},{3,1},{4,6},{5,7},{6,4},{7,5},{8,10},{9,11},{10,... | collective-permute-start | bytes 761864 | tf_op jit(solution)/shard_map/ppermute | solution.py:88
  45.7 15.6 %collective-permute-start.12 = (bf16[992,128]{1,0:T(8,128)(2,1)S(1)}, bf16[992,128]{1,0:T(8,128)(2,1)S(1)}, u32[]{:S(2)}, u32[]{:S(2)}) collective-permute-start(bf16[992,128]{1,0:T(8,128)(2,1)S(1)} %collective-permute-done.6), channel_id=1, source_target_pairs={{0,1},{1,0},{2,4},{3,5},{4,2},{5,3},{6,7},{7,6},{8,9},{9,8},{10,12... | collective-permute-start | bytes 761864 | tf_op jit(solution)/shard_map/ppermute | solution.py:88
  47.6 19.8 %collective-permute-start.17 = (bf16[1008,128]{1,0:T(8,128)(2,1)S(1)}, bf16[1008,128]{1,0:T(8,128)(2,1)S(1)}, u32[]{:S(2)}, u32[]{:S(2)}) collective-permute-start(bf16[1008,128]{1,0:T(8,128)(2,1)S(1)} %collective-permute-done.7), channel_id=1, source_target_pairs={{0,8},{1,9},{2,10},{3,11},{4,12},{5,13},{6,14},{7,15},{8,0},{9,1},... | collective-permute-start | bytes 774152 | tf_op jit(solution)/shard_map/ppermute | solution.py:88
  47.7 10.8 %collective-permute-start.11 = (bf16[1008,128]{1,0:T(8,128)(2,1)S(1)}, bf16[1008,128]{1,0:T(8,128)(2,1)S(1)}, u32[]{:S(2)}, u32[]{:S(2)}) collective-permute-start(bf16[1008,128]{1,0:T(8,128)(2,1)S(1)} %collective-permute-done.9), channel_id=1, source_target_pairs={{0,2},{1,3},{2,0},{3,1},{4,6},{5,7},{6,4},{7,5},{8,10},{9,11},{10,... | collective-permute-start | bytes 774152 | tf_op jit(solution)/shard_map/ppermute | solution.py:88
  52.2 15.4 %collective-permute-start.20 = (bf16[1008,128]{1,0:T(8,128)(2,1)S(1)}, bf16[1008,128]{1,0:T(8,128)(2,1)S(1)}, u32[]{:S(2)}, u32[]{:S(2)}) collective-permute-start(bf16[1008,128]{1,0:T(8,128)(2,1)S(1)} %collective-permute-done.7), channel_id=1, source_target_pairs={{0,16},{1,17},{2,18},{3,19},{4,20},{5,21},{6,22},{7,23},{8,24},{9,... | collective-permute-start | bytes 774152 | tf_op jit(solution)/shard_map/ppermute | solution.py:88
  58.5 8.0 %collective-permute-start.13 = (bf16[1008,128]{1,0:T(8,128)(2,1)S(1)}, bf16[1008,128]{1,0:T(8,128)(2,1)S(1)}, u32[]{:S(2)}, u32[]{:S(2)}) collective-permute-start(bf16[1008,128]{1,0:T(8,128)(2,1)S(1)} %collective-permute-done.7), channel_id=1, source_target_pairs={{0,1},{1,0},{2,4},{3,5},{4,2},{5,3},{6,7},{7,6},{8,9},{9,8},{10,12... | collective-permute-start | bytes 774152 | tf_op jit(solution)/shard_map/ppermute | solution.py:88
  61.2 8.1 %collective-permute-start.26 = (bf16[992,128]{1,0:T(8,128)(2,1)S(1)}, bf16[992,128]{1,0:T(8,128)(2,1)S(1)}, u32[]{:S(2)}, u32[]{:S(2)}) collective-permute-start(bf16[992,128]{1,0:T(8,128)(2,1)S(1)} %collective-permute-done.10), channel_id=1, source_target_pairs={{0,8},{1,9},{2,4},{3,5},{4,2},{5,3},{6,14},{7,15},{8,0},{9,1},{10,... | collective-permute-start | bytes 761864 | tf_op jit(solution)/shard_map/ppermute | solution.py:88
  61.2 7.0 %collective-permute-start.19 = (bf16[992,128]{1,0:T(8,128)(2,1)S(1)}, bf16[992,128]{1,0:T(8,128)(2,1)S(1)}, u32[]{:S(2)}, u32[]{:S(2)}) collective-permute-start(bf16[992,128]{1,0:T(8,128)(2,1)S(1)} %collective-permute-done.18), channel_id=1, source_target_pairs={{0,8},{1,9},{2,10},{3,11},{4,12},{5,13},{6,14},{7,15},{8,0},{9,1},... | collective-permute-start | bytes 761864 | tf_op jit(solution)/shard_map/ppermute | solution.py:88
  67.2 2.2 %collective-permute-start.27 = (bf16[1008,128]{1,0:T(8,128)(2,1)S(1)}, bf16[1008,128]{1,0:T(8,128)(2,1)S(1)}, u32[]{:S(2)}, u32[]{:S(2)}) collective-permute-start(bf16[1008,128]{1,0:T(8,128)(2,1)S(1)} %collective-permute-done.13), channel_id=1, source_target_pairs={{0,8},{1,9},{2,3},{3,2},{4,5},{5,4},{6,14},{7,15},{8,0},{9,1},{10,... | collective-permute-start | bytes 774152 | tf_op jit(solution)/shard_map/ppermute | solution.py:88
  67.5 1.7 %collective-permute-start.21 = (bf16[1008,128]{1,0:T(8,128)(2,1)S(1)}, bf16[1008,128]{1,0:T(8,128)(2,1)S(1)}, u32[]{:S(2)}, u32[]{:S(2)}) collective-permute-start(bf16[1008,128]{1,0:T(8,128)(2,1)S(1)} %collective-permute-done.20), channel_id=1, source_target_pairs={{0,8},{1,9},{2,10},{3,11},{4,12},{5,13},{6,14},{7,15},{8,0},{9,1},... | collective-permute-start | bytes 774152 | tf_op jit(solution)/shard_map/ppermute | solution.py:88
  69.8 14.6 %collective-permute-start.28 = (f16[128,4,128]{2,0,1:T(8,128)(2,1)S(1)}, f16[128,4,128]{2,0,1:T(8,128)(2,1)S(1)}, u32[]{:S(2)}, u32[]{:S(2)}) collective-permute-start(f16[128,4,128]{2,0,1:T(8,128)(2,1)S(1)} %fusion.14), channel_id=1, source_target_pairs={{0,2},{1,3},{2,0},{3,1},{4,6},{5,7},{6,4},{7,5},{8,10},{9,11},{10,... | collective-permute-start | bytes 393224 | tf_op jit(solution)/shard_map/ppermute | solution.py:88
  77.5 5.3 %collective-permute-start.22 = (f16[128,4,128]{2,0,1:T(8,128)(2,1)S(1)}, f16[128,4,128]{2,0,1:T(8,128)(2,1)S(1)}, u32[]{:S(2)}, u32[]{:S(2)}) collective-permute-start(f16[128,4,128]{2,0,1:T(8,128)(2,1)S(1)} %fusion.16), channel_id=1, source_target_pairs={{0,2},{1,3},{2,0},{3,1},{4,6},{5,7},{6,4},{7,5},{8,10},{9,11},{10,... | collective-permute-start | bytes 393224 | tf_op jit(solution)/shard_map/ppermute | solution.py:88
  78.5 5.6 %collective-permute-start.25 = (f16[128,4,128]{2,0,1:T(8,128)(2,1)S(1)}, f16[128,4,128]{2,0,1:T(8,128)(2,1)S(1)}, u32[]{:S(2)}, u32[]{:S(2)}) collective-permute-start(f16[128,4,128]{2,0,1:T(8,128)(2,1)S(1)} %fusion.15), channel_id=1, source_target_pairs={{0,2},{1,3},{2,0},{3,1},{4,6},{5,7},{6,4},{7,5},{8,10},{9,11},{10,... | collective-permute-start | bytes 393224 | tf_op jit(solution)/shard_map/ppermute | solution.py:88
  84.6 1.3 %copy-start.1 = (f32[8,128,4,128]{3,2,1,0:T(4,128)}, f32[8,128,4,128]{3,2,1,0:T(4,128)S(1)}, u32[]{:S(2)}) copy-start(f32[8,128,4,128]{3,2,1,0:T(4,128)S(1)} %copy_dynamic-update-slice_fusion) | copy-start | bytes 6291460

commit v5 on v4

--- a/solution.py
+++ b/solution.py
@@ -16,8 +16,20 @@
 VMEM = pl.BlockSpec(memory_space=pltpu.VMEM)
 
 
-def unit_kernel(cut, data, first, second):
-    squares = jnp.sum(data[...] * data[...], axis=0, keepdims=True)
+def unit_kernel(cut, chunks, source, first, second, data, sems):
+    size = data.shape[0] // chunks
+
+    def load(i):
+        span = pl.ds(i * size, size)
+        return pltpu.make_async_copy(source.at[span], data.at[span], sems.at[i])
+
+    for i in range(chunks):
+        load(i).start()
+    squares = jnp.zeros((1, data.shape[1]), jnp.float32)
+    for i in range(chunks):
+        load(i).wait()
+        part = data[i * size : (i + 1) * size]
+        squares += jnp.sum(part * part, axis=0, keepdims=True)
     scale = lax.rsqrt(squares + 1e-06)
     first[...] = (data[:cut] * scale).astype(jnp.bfloat16)
     second[...] = (data[cut:] * scale).astype(jnp.bfloat16)
@@ -25,16 +37,21 @@
 
 def normalize(data, cut):
     features, block = data.shape
+    chunks = next(n for n in (5, 4, 3, 2, 1) if features % (8 * n) == 0)
     return pl.pallas_call(
-        functools.partial(unit_kernel, cut),
+        functools.partial(unit_kernel, cut, chunks),
         out_shape=[
             jax.ShapeDtypeStruct((cut, block), jnp.bfloat16),
             jax.ShapeDtypeStruct((features - cut, block), jnp.bfloat16),
         ],
-        in_specs=[VMEM],
+        in_specs=[pl.BlockSpec(memory_space=pltpu.HBM)],
         out_specs=[VMEM, VMEM],
+        scratch_shapes=[
+            pltpu.VMEM((features, block), jnp.float32),
+            pltpu.SemaphoreType.DMA((chunks,)),
+        ],
         cost_estimate=pl.CostEstimate(flops=0, bytes_accessed=6 * data.size, transcendentals=0),
-        compiler_params=pltpu.CompilerParams(vmem_limit_bytes=8 * data.size),
+        compiler_params=pltpu.CompilerParams(vmem_limit_bytes=16 * data.size),
         name="normalize",
     )(data)
 
@@ -120,9 +137,8 @@
         for k in offsets:
             across[k - 1][h] = send(unit[h], shift(k, k + 1))
         pair[h] = send(unit[h], line_swap)
-        if h == 0:
-            for j in others:
-                own[j][h] = send(unit[h], other(j))
+        for j in others:
+            own[j][h] = send(unit[h], other(j))
     swapped = {("own", 0, h): send(unit[h], core_swap) for h in halves}
     for h in halves:
         for j in others:
@@ -134,13 +150,14 @@
         for k in range(2, inner):
             across_pair[k - 2][h] = send(across[k - 2][h], line_swap)
     for j in others:
-        own[j][1] = send(unit[1], other(j))
-    for j in others:
-        swapped["own", j, 0] = send(own[j][0], core_swap)
+        swapped.update({("own", j, h): send(own[j][h], core_swap) for h in halves})
     swapped.update({("end", 0, h): send(pair[h], core_swap) for h in halves})
     for j in others:
         swapped["end", j, 0] = send(end[j][0], core_swap)
-    far_across = [[send(head_pair[0] if k == 1 else across_pair[k - 2][0], centre_swap(0)), None] for k in offsets]
+    far_across = [[None, None] for _ in offsets]
+    for k in offsets:
+        source = head_pair if k == 1 else across_pair[k - 2]
+        far_across[k - 1][0] = send(source[0], centre_swap(0))
     for j in others:
         swapped["end", j, 1] = send(end[j][1], core_swap)
     for k in offsets:
@@ -179,10 +196,6 @@
         panel = (fourth(block, end_columns) * SCALE).astype(jnp.float16)
         return send(panel, line_swap)
 
-    end_columns = columns_of("end", end)
-    panels = [back(b) for b in [relay] + centre_across]
-    for j in others:
-        swapped["own", j, 1] = send(own[j][1], core_swap)
     columns = columns_of("own", own)
     out = jnp.zeros((ncolumns, block, ngroups, block), jnp.float32)
     out = put(out, product(unit), at["unit"])
@@ -191,12 +204,15 @@
     for k in range(1, inner - 1):
         out = put(out, product(across[k - 1]), at["across", k])
     mine = [product(across[-1])]
-    panels += [back(b) for b in far_across]
+    end_columns = columns_of("end", end)
+    panels = [back(b) for b in [relay] + centre_across]
     out = put(out, product(head_pair), at["head_pair"])
     out = put(out, product(relay), at["relay"])
     for k in range(2, inner):
         out = put(out, product(across_pair[k - 2]), at["across_pair", k])
-    mine += [product(b) for b in centre_across + far_across]
+    mine += [product(b) for b in centre_across]
+    panels += [back(b) for b in far_across]
+    mine += [product(b) for b in far_across]
     slots = [at["back", k] for k in range(inner)] + [at["far", k] for k in offsets]
     for index, panel, value in zip(slots, panels, mine):
         theirs = panel.astype(jnp.float32) * (1.0 / SCALE)

time: 86.1 us -> 87.5 us (1.016)
  Pallas kernels: 0.33 us -> 1.69 us
    pallas_call x1, Pallas kernels: 0.33 us -> 1.69 us  [normalize(): pl.pallas_call(functools.partial(unit_kernel, cut, chunks), out_shape=[ja...]
where the time goes in v5:
time: 87.5 us; the launch traced here: 87.3 us
  starting transfers between devices  48.6 us (56%)
  waiting for transfers between devices  25.7 us (29%)
  local copies, waits for them, and re-layouts  5.46 us (6%)
  matrix products  5.32 us (6%)
  Pallas kernels  1.69 us (2%)
    ppermute x29, starting transfers between devices, send(): return lax.ppermute(array, AXES, pairs)  48.6 us
    ppermute x29, waiting for transfers between devices, send(): return lax.ppermute(array, AXES, pairs)  25.7 us
    dot_general x11, matrix products, fourth(): lax.dot_general(jnp.concatenate(block, axis=0), cols, (((0,), (1,)), ((),...  5.32 us
    unnamed x4, local copies, waits for them, and re-layouts  2.53 us
  transfers between devices with their start and end apart: 29, of which 9 were waited for; matrix products, arithmetic and copies ran while one was open for 9% of the time, Pallas kernels for 0%

profile of v5, /device:TPU:0, one launch (start us, length us, event | category | flops | bytes accessed | tf_op | source)
XLA Modules:
  0.0 87.3 jit_solution(567304005871568700)
XLA Ops:
  0.0 1.2 %copy-done = f32[128,2000]{0,1:T(8,128)S(1)} copy-done((f32[128,2000]{0,1:T(8,128)S(1)}, f32[128,2000]{0,1:T(8,128)}, u32[]{:S(2)}) %copy-start) | copy-done | bytes 1024024
  1.2 1.7 %normalize.1 = (bf16[992,128]{1,0:T(8,128)(2,1)S(1)}, bf16[1008,128]{1,0:T(8,128)(2,1)S(1)}) custom-call(f32[2000,128]{1,0:T(8,128)S(1)} %bitcast.83), custom_call_target="tpu_custom_call" | custom-call | bytes 1536000 | tf_op jit(solution)/shard_map/normalize/pallas_call | solution.py:41
  2.9 3.1 %collective-permute-start.6 = (bf16[992,128]{1,0:T(8,128)(2,1)S(1)}, bf16[992,128]{1,0:T(8,128)(2,1)S(1)}, u32[]{:S(2)}, u32[]{:S(2)}) collective-permute-start(bf16[992,128]{1,0:T(8,128)(2,1)S(1)} %get-tuple-element.22), channel_id=1, source_target_pairs={{0,2},{1,3},{2,0},{3,1},{4,6},{5,7},{6,4},{7,5},{8,10},{9,11},{10,... | collective-permute-start | bytes 761864 | tf_op jit(solution)/shard_map/ppermute | solution.py:105
  6.0 1.5 %collective-permute-start.8 = (bf16[992,128]{1,0:T(8,128)(2,1)S(1)}, bf16[992,128]{1,0:T(8,128)(2,1)S(1)}, u32[]{:S(2)}, u32[]{:S(2)}) collective-permute-start(bf16[992,128]{1,0:T(8,128)(2,1)S(1)} %get-tuple-element.22), channel_id=1, source_target_pairs={{0,1},{1,0},{2,4},{3,5},{4,2},{5,3},{6,7},{7,6},{8,9},{9,8},{10,12... | collective-permute-start | bytes 761864 | tf_op jit(solution)/shard_map/ppermute | solution.py:105
  7.5 1.7 %collective-permute-start.7 = (bf16[1008,128]{1,0:T(8,128)(2,1)S(1)}, bf16[1008,128]{1,0:T(8,128)(2,1)S(1)}, u32[]{:S(2)}, u32[]{:S(2)}) collective-permute-start(bf16[1008,128]{1,0:T(8,128)(2,1)S(1)} %get-tuple-element.23), channel_id=1, source_target_pairs={{0,2},{1,3},{2,0},{3,1},{4,6},{5,7},{6,4},{7,5},{8,10},{9,11},{10,... | collective-permute-start | bytes 774152 | tf_op jit(solution)/shard_map/ppermute | solution.py:105
  9.2 0.2 collective-permute-start.1
  9.4 0.3 broadcast.17.clone
  9.7 3.3 %collective-permute-done.6 = bf16[992,128]{1,0:T(8,128)(2,1)S(1)} collective-permute-done((bf16[992,128]{1,0:T(8,128)(2,1)S(1)}, bf16[992,128]{1,0:T(8,128)(2,1)S(1)}, u32[]{:S(2)}, u32[]{:S(2)}) %collective-permute-start.6) | collective-permute-done | bytes 253984 | tf_op jit(solution)/shard_map/ppermute | solution.py:105
  13.0 2.0 %collective-permute-start.2 = (bf16[992,128]{1,0:T(8,128)(2,1)S(1)}, bf16[992,128]{1,0:T(8,128)(2,1)S(1)}, u32[]{:S(2)}, u32[]{:S(2)}) collective-permute-start(bf16[992,128]{1,0:T(8,128)(2,1)S(1)} %get-tuple-element.22), channel_id=1, source_target_pairs={{0,16},{1,17},{2,18},{3,19},{4,20},{5,21},{6,22},{7,23},{8,24},{9,... | collective-permute-start | bytes 761864 | tf_op jit(solution)/shard_map/ppermute | solution.py:105
  15.0 0.3 broadcast.17.clone.1
  15.5 6.5 %collective-permute-done.2 = bf16[992,128]{1,0:T(8,128)(2,1)S(1)} collective-permute-done((bf16[992,128]{1,0:T(8,128)(2,1)S(1)}, bf16[992,128]{1,0:T(8,128)(2,1)S(1)}, u32[]{:S(2)}, u32[]{:S(2)}) %collective-permute-start.2) | collective-permute-done | bytes 253984 | tf_op jit(solution)/shard_map/ppermute | solution.py:105
  22.0 1.6 %collective-permute-start.9 = (bf16[1008,128]{1,0:T(8,128)(2,1)S(1)}, bf16[1008,128]{1,0:T(8,128)(2,1)S(1)}, u32[]{:S(2)}, u32[]{:S(2)}) collective-permute-start(bf16[1008,128]{1,0:T(8,128)(2,1)S(1)} %get-tuple-element.23), channel_id=1, source_target_pairs={{0,1},{1,0},{2,4},{3,5},{4,2},{5,3},{6,7},{7,6},{8,9},{9,8},{10,12... | collective-permute-start | bytes 774152 | tf_op jit(solution)/shard_map/ppermute | solution.py:105
  23.7 1.4 %collective-permute-done.3 = bf16[992,128]{1,0:T(8,128)(2,1)S(1)} collective-permute-done((bf16[992,128]{1,0:T(8,128)(2,1)S(1)}, bf16[992,128]{1,0:T(8,128)(2,1)S(1)}, u32[]{:S(2)}, u32[]{:S(2)}) %collective-permute-start.3) | collective-permute-done | bytes 253984 | tf_op jit(solution)/shard_map/ppermute | solution.py:105
  25.3 0.4 collective-permute-start.15
  25.8 0.9 collective-permute-done.16
  26.8 0.4 collective-permute-start.14
  27.3 1.6 %collective-permute-start.18 = (bf16[992,128]{1,0:T(8,128)(2,1)S(1)}, bf16[992,128]{1,0:T(8,128)(2,1)S(1)}, u32[]{:S(2)}, u32[]{:S(2)}) collective-permute-start(bf16[992,128]{1,0:T(8,128)(2,1)S(1)} %collective-permute-done.6), channel_id=1, source_target_pairs={{0,16},{1,17},{2,18},{3,19},{4,20},{5,21},{6,22},{7,23},{8,24},{9,... | collective-permute-start | bytes 761864 | tf_op jit(solution)/shard_map/ppermute | solution.py:105
  28.9 0.5 collective-permute-start.24
  29.5 0.5 fusion.10
  30.0 0.5 fusion.8
  30.5 0.5 fusion.9
  31.0 16.1 %collective-permute-start.10 = (bf16[992,128]{1,0:T(8,128)(2,1)S(1)}, bf16[992,128]{1,0:T(8,128)(2,1)S(1)}, u32[]{:S(2)}, u32[]{:S(2)}) collective-permute-start(bf16[992,128]{1,0:T(8,128)(2,1)S(1)} %collective-permute-done.8), channel_id=1, source_target_pairs={{0,2},{1,3},{2,0},{3,1},{4,6},{5,7},{6,4},{7,5},{8,10},{9,11},{10,... | collective-permute-start | bytes 761864 | tf_op jit(solution)/shard_map/ppermute | solution.py:105
  47.0 1.5 %collective-permute-start.12 = (bf16[992,128]{1,0:T(8,128)(2,1)S(1)}, bf16[992,128]{1,0:T(8,128)(2,1)S(1)}, u32[]{:S(2)}, u32[]{:S(2)}) collective-permute-start(bf16[992,128]{1,0:T(8,128)(2,1)S(1)} %collective-permute-done.6), channel_id=1, source_target_pairs={{0,1},{1,0},{2,4},{3,5},{4,2},{5,3},{6,7},{7,6},{8,9},{9,8},{10,12... | collective-permute-start | bytes 761864 | tf_op jit(solution)/shard_map/ppermute | solution.py:105
  48.5 0.5 fusion.3
  49.1 4.0 %collective-permute-start.11 = (bf16[1008,128]{1,0:T(8,128)(2,1)S(1)}, bf16[1008,128]{1,0:T(8,128)(2,1)S(1)}, u32[]{:S(2)}, u32[]{:S(2)}) collective-permute-start(bf16[1008,128]{1,0:T(8,128)(2,1)S(1)} %collective-permute-done.9), channel_id=1, source_target_pairs={{0,2},{1,3},{2,0},{3,1},{4,6},{5,7},{6,4},{7,5},{8,10},{9,11},{10,... | collective-permute-start | bytes 774152 | tf_op jit(solution)/shard_map/ppermute | solution.py:105
  53.1 0.5 fusion.5
  53.5 1.6 %collective-permute-start.20 = (bf16[1008,128]{1,0:T(8,128)(2,1)S(1)}, bf16[1008,128]{1,0:T(8,128)(2,1)S(1)}, u32[]{:S(2)}, u32[]{:S(2)}) collective-permute-start(bf16[1008,128]{1,0:T(8,128)(2,1)S(1)} %collective-permute-done.7), channel_id=1, source_target_pairs={{0,16},{1,17},{2,18},{3,19},{4,20},{5,21},{6,22},{7,23},{8,24},{9,... | collective-permute-start | bytes 774152 | tf_op jit(solution)/shard_map/ppermute | solution.py:105
  55.1 4.7 %collective-permute-done.11 = bf16[1008,128]{1,0:T(8,128)(2,1)S(1)} collective-permute-done((bf16[1008,128]{1,0:T(8,128)(2,1)S(1)}, bf16[1008,128]{1,0:T(8,128)(2,1)S(1)}, u32[]{:S(2)}, u32[]{:S(2)}) %collective-permute-start.11) | collective-permute-done | bytes 258080 | tf_op jit(solution)/shard_map/ppermute | solution.py:105
  59.9 1.5 %collective-permute-start.13 = (bf16[1008,128]{1,0:T(8,128)(2,1)S(1)}, bf16[1008,128]{1,0:T(8,128)(2,1)S(1)}, u32[]{:S(2)}, u32[]{:S(2)}) collective-permute-start(bf16[1008,128]{1,0:T(8,128)(2,1)S(1)} %collective-permute-done.7), channel_id=1, source_target_pairs={{0,1},{1,0},{2,4},{3,5},{4,2},{5,3},{6,7},{7,6},{8,9},{9,8},{10,12... | collective-permute-start | bytes 774152 | tf_op jit(solution)/shard_map/ppermute | solution.py:105
  61.4 0.5 fusion.7
  61.9 0.3 broadcast_in_dim.76
  62.6 0.5 collective-permute-start.19
  63.1 4.7 %collective-permute-done.13 = bf16[1008,128]{1,0:T(8,128)(2,1)S(1)} collective-permute-done((bf16[1008,128]{1,0:T(8,128)(2,1)S(1)}, bf16[1008,128]{1,0:T(8,128)(2,1)S(1)}, u32[]{:S(2)}, u32[]{:S(2)}) %collective-permute-start.13) | collective-permute-done | bytes 258080 | tf_op jit(solution)/shard_map/ppermute | solution.py:105
  67.8 0.5 fusion.6
  68.6 0.2 copy_dynamic-update-slice_fusion.4
  68.9 0.6 collective-permute-start.21
  69.8 0.9 collective-permute-done.21
  70.7 0.5 fusion.14
  71.2 7.2 %collective-permute-start.28 = (f16[128,4,128]{2,0,1:T(8,128)(2,1)S(1)}, f16[128,4,128]{2,0,1:T(8,128)(2,1)S(1)}, u32[]{:S(2)}, u32[]{:S(2)}) collective-permute-start(f16[128,4,128]{2,0,1:T(8,128)(2,1)S(1)} %fusion.14), channel_id=1, source_target_pairs={{0,2},{1,3},{2,0},{3,1},{4,6},{5,7},{6,4},{7,5},{8,10},{9,11},{10,... | collective-permute-start | bytes 393224 | tf_op jit(solution)/shard_map/ppermute | solution.py:105
  78.3 0.5 fusion.16
  78.9 0.5 fusion.1
  79.4 0.5 fusion.15
  79.9 2.1 %collective-permute-start.25 = (f16[128,4,128]{2,0,1:T(8,128)(2,1)S(1)}, f16[128,4,128]{2,0,1:T(8,128)(2,1)S(1)}, u32[]{:S(2)}, u32[]{:S(2)}) collective-permute-start(f16[128,4,128]{2,0,1:T(8,128)(2,1)S(1)} %fusion.15), channel_id=1, source_target_pairs={{0,2},{1,3},{2,0},{3,1},{4,6},{5,7},{6,4},{7,5},{8,10},{9,11},{10,... | collective-permute-start | bytes 393224 | tf_op jit(solution)/shard_map/ppermute | solution.py:105
  82.0 2.1 %collective-permute-done.22 = f16[128,4,128]{2,0,1:T(8,128)(2,1)S(1)} collective-permute-done((f16[128,4,128]{2,0,1:T(8,128)(2,1)S(1)}, f16[128,4,128]{2,0,1:T(8,128)(2,1)S(1)}, u32[]{:S(2)}, u32[]{:S(2)}) %collective-permute-start.22) | collective-permute-done | bytes 131104 | tf_op jit(solution)/shard_map/ppermute | solution.py:105
  84.1 0.2 copy_dynamic-update-slice_fusion.2
  84.3 1.2 %collective-permute-done.25 = f16[128,4,128]{2,0,1:T(8,128)(2,1)S(1)} collective-permute-done((f16[128,4,128]{2,0,1:T(8,128)(2,1)S(1)}, f16[128,4,128]{2,0,1:T(8,128)(2,1)S(1)}, u32[]{:S(2)}, u32[]{:S(2)}) %collective-permute-start.25) | collective-permute-done | bytes 131104 | tf_op jit(solution)/shard_map/ppermute | solution.py:105
  85.8 0.2 copy_dynamic-update-slice_fusion
  86.0 1.3 %copy-done.1 = f32[8,128,4,128]{3,2,1,0:T(4,128)} copy-done((f32[8,128,4,128]{3,2,1,0:T(4,128)}, f32[8,128,4,128]{3,2,1,0:T(4,128)S(1)}, u32[]{:S(2)}) %copy-start.1) | copy-done | bytes 2097176
  (56 shorter events, 2.4 us)
Async XLA Ops:
  0.0 1.2 %copy-start = (f32[128,2000]{0,1:T(8,128)S(1)}, f32[128,2000]{0,1:T(8,128)}, u32[]{:S(2)}) copy-start(f32[128,2000]{0,1:T(8,128)} %param.1) | copy-start | bytes 3072004
  2.9 10.1 %collective-permute-start.6 = (bf16[992,128]{1,0:T(8,128)(2,1)S(1)}, bf16[992,128]{1,0:T(8,128)(2,1)S(1)}, u32[]{:S(2)}, u32[]{:S(2)}) collective-permute-start(bf16[992,128]{1,0:T(8,128)(2,1)S(1)} %get-tuple-element.22), channel_id=1, source_target_pairs={{0,2},{1,3},{2,0},{3,1},{4,6},{5,7},{6,4},{7,5},{8,10},{9,11},{10,... | collective-permute-start | bytes 761864 | tf_op jit(solution)/shard_map/ppermute | solution.py:105
  6.0 21.3 %collective-permute-start.8 = (bf16[992,128]{1,0:T(8,128)(2,1)S(1)}, bf16[992,128]{1,0:T(8,128)(2,1)S(1)}, u32[]{:S(2)}, u32[]{:S(2)}) collective-permute-start(bf16[992,128]{1,0:T(8,128)(2,1)S(1)} %get-tuple-element.22), channel_id=1, source_target_pairs={{0,1},{1,0},{2,4},{3,5},{4,2},{5,3},{6,7},{7,6},{8,9},{9,8},{10,12... | collective-permute-start | bytes 761864 | tf_op jit(solution)/shard_map/ppermute | solution.py:105
  7.5 7.8 %collective-permute-start = (bf16[992,128]{1,0:T(8,128)(2,1)S(1)}, bf16[992,128]{1,0:T(8,128)(2,1)S(1)}, u32[]{:S(2)}, u32[]{:S(2)}) collective-permute-start(bf16[992,128]{1,0:T(8,128)(2,1)S(1)} %get-tuple-element.22), channel_id=1, source_target_pairs={{0,8},{1,9},{2,10},{3,11},{4,12},{5,13},{6,14},{7,15},{8,0},{9,1},... | collective-permute-start | bytes 761864 | tf_op jit(solution)/shard_map/ppermute | solution.py:105
  7.5 19.3 %collective-permute-start.7 = (bf16[1008,128]{1,0:T(8,128)(2,1)S(1)}, bf16[1008,128]{1,0:T(8,128)(2,1)S(1)}, u32[]{:S(2)}, u32[]{:S(2)}) collective-permute-start(bf16[1008,128]{1,0:T(8,128)(2,1)S(1)} %get-tuple-element.23), channel_id=1, source_target_pairs={{0,2},{1,3},{2,0},{3,1},{4,6},{5,7},{6,4},{7,5},{8,10},{9,11},{10,... | collective-permute-start | bytes 774152 | tf_op jit(solution)/shard_map/ppermute | solution.py:105
  9.2 14.4 %collective-permute-start.1 = (bf16[1008,128]{1,0:T(8,128)(2,1)S(1)}, bf16[1008,128]{1,0:T(8,128)(2,1)S(1)}, u32[]{:S(2)}, u32[]{:S(2)}) collective-permute-start(bf16[1008,128]{1,0:T(8,128)(2,1)S(1)} %get-tuple-element.23), channel_id=1, source_target_pairs={{0,8},{1,9},{2,10},{3,11},{4,12},{5,13},{6,14},{7,15},{8,0},{9,1},... | collective-permute-start | bytes 774152 | tf_op jit(solution)/shard_map/ppermute | solution.py:105
  13.0 9.0 %collective-permute-start.2 = (bf16[992,128]{1,0:T(8,128)(2,1)S(1)}, bf16[992,128]{1,0:T(8,128)(2,1)S(1)}, u32[]{:S(2)}, u32[]{:S(2)}) collective-permute-start(bf16[992,128]{1,0:T(8,128)(2,1)S(1)} %get-tuple-element.22), channel_id=1, source_target_pairs={{0,16},{1,17},{2,18},{3,19},{4,20},{5,21},{6,22},{7,23},{8,24},{9,... | collective-permute-start | bytes 761864 | tf_op jit(solution)/shard_map/ppermute | solution.py:105
  15.3 10.0 %collective-permute-start.4 = (bf16[1008,128]{1,0:T(8,128)(2,1)S(1)}, bf16[1008,128]{1,0:T(8,128)(2,1)S(1)}, u32[]{:S(2)}, u32[]{:S(2)}) collective-permute-start(bf16[1008,128]{1,0:T(8,128)(2,1)S(1)} %get-tuple-element.23), channel_id=1, source_target_pairs={{0,16},{1,17},{2,18},{3,19},{4,20},{5,21},{6,22},{7,23},{8,24},{9,... | collective-permute-start | bytes 774152 | tf_op jit(solution)/shard_map/ppermute | solution.py:105
  22.0 6.9 %collective-permute-start.9 = (bf16[1008,128]{1,0:T(8,128)(2,1)S(1)}, bf16[1008,128]{1,0:T(8,128)(2,1)S(1)}, u32[]{:S(2)}, u32[]{:S(2)}) collective-permute-start(bf16[1008,128]{1,0:T(8,128)(2,1)S(1)} %get-tuple-element.23), channel_id=1, source_target_pairs={{0,1},{1,0},{2,4},{3,5},{4,2},{5,3},{6,7},{7,6},{8,9},{9,8},{10,12... | collective-permute-start | bytes 774152 | tf_op jit(solution)/shard_map/ppermute | solution.py:105
  23.6 1.5 %collective-permute-start.3 = (bf16[992,128]{1,0:T(8,128)(2,1)S(1)}, bf16[992,128]{1,0:T(8,128)(2,1)S(1)}, u32[]{:S(2)}, u32[]{:S(2)}) collective-permute-start(bf16[992,128]{1,0:T(8,128)(2,1)S(1)} %collective-permute-done.2), channel_id=1, source_target_pairs={{0,8},{1,9},{2,10},{3,11},{4,12},{5,13},{6,14},{7,15},{8,0},{9,1},... | collective-permute-start | bytes 761864 | tf_op jit(solution)/shard_map/ppermute | solution.py:105
  25.1 1.5 %collective-permute-start.16 = (bf16[992,128]{1,0:T(8,128)(2,1)S(1)}, bf16[992,128]{1,0:T(8,128)(2,1)S(1)}, u32[]{:S(2)}, u32[]{:S(2)}) collective-permute-start(bf16[992,128]{1,0:T(8,128)(2,1)S(1)} %collective-permute-done.6), channel_id=1, source_target_pairs={{0,8},{1,9},{2,10},{3,11},{4,12},{5,13},{6,14},{7,15},{8,0},{9,1},... | collective-permute-start | bytes 761864 | tf_op jit(solution)/shard_map/ppermute | solution.py:105
  25.3 23.8 %collective-permute-start.15 = (bf16[1008,128]{1,0:T(8,128)(2,1)S(1)}, bf16[1008,128]{1,0:T(8,128)(2,1)S(1)}, u32[]{:S(2)}, u32[]{:S(2)}) collective-permute-start(bf16[1008,128]{1,0:T(8,128)(2,1)S(1)} %get-tuple-element.23), channel_id=1, source_target_pairs={{0,8},{1,9},{2,3},{3,2},{4,5},{5,4},{6,14},{7,15},{8,0},{9,1},{10,... | collective-permute-start | bytes 774152 | tf_op jit(solution)/shard_map/ppermute | solution.py:105
  26.7 2.3 %collective-permute-start.5 = (bf16[1008,128]{1,0:T(8,128)(2,1)S(1)}, bf16[1008,128]{1,0:T(8,128)(2,1)S(1)}, u32[]{:S(2)}, u32[]{:S(2)}) collective-permute-start(bf16[1008,128]{1,0:T(8,128)(2,1)S(1)} %collective-permute-done.4), channel_id=1, source_target_pairs={{0,8},{1,9},{2,10},{3,11},{4,12},{5,13},{6,14},{7,15},{8,0},{9,1},... | collective-permute-start | bytes 774152 | tf_op jit(solution)/shard_map/ppermute | solution.py:105
  26.8 22.2 %collective-permute-start.14 = (bf16[992,128]{1,0:T(8,128)(2,1)S(1)}, bf16[992,128]{1,0:T(8,128)(2,1)S(1)}, u32[]{:S(2)}, u32[]{:S(2)}) collective-permute-start(bf16[992,128]{1,0:T(8,128)(2,1)S(1)} %get-tuple-element.22), channel_id=1, source_target_pairs={{0,8},{1,9},{2,3},{3,2},{4,5},{5,4},{6,14},{7,15},{8,0},{9,1},{10,... | collective-permute-start | bytes 761864 | tf_op jit(solution)/shard_map/ppermute | solution.py:105
  27.3 35.2 %collective-permute-start.18 = (bf16[992,128]{1,0:T(8,128)(2,1)S(1)}, bf16[992,128]{1,0:T(8,128)(2,1)S(1)}, u32[]{:S(2)}, u32[]{:S(2)}) collective-permute-start(bf16[992,128]{1,0:T(8,128)(2,1)S(1)} %collective-permute-done.6), channel_id=1, source_target_pairs={{0,16},{1,17},{2,18},{3,19},{4,20},{5,21},{6,22},{7,23},{8,24},{9,... | collective-permute-start | bytes 761864 | tf_op jit(solution)/shard_map/ppermute | solution.py:105
  28.9 2.0 %collective-permute-start.23 = (bf16[992,128]{1,0:T(8,128)(2,1)S(1)}, bf16[992,128]{1,0:T(8,128)(2,1)S(1)}, u32[]{:S(2)}, u32[]{:S(2)}) collective-permute-start(bf16[992,128]{1,0:T(8,128)(2,1)S(1)} %collective-permute-done.8), channel_id=1, source_target_pairs={{0,8},{1,9},{2,3},{3,2},{4,5},{5,4},{6,14},{7,15},{8,0},{9,1},{10,... | collective-permute-start | bytes 761864 | tf_op jit(solution)/shard_map/ppermute | solution.py:105
  28.9 18.1 %collective-permute-start.24 = (bf16[1008,128]{1,0:T(8,128)(2,1)S(1)}, bf16[1008,128]{1,0:T(8,128)(2,1)S(1)}, u32[]{:S(2)}, u32[]{:S(2)}) collective-permute-start(bf16[1008,128]{1,0:T(8,128)(2,1)S(1)} %collective-permute-done.9), channel_id=1, source_target_pairs={{0,8},{1,9},{2,3},{3,2},{4,5},{5,4},{6,14},{7,15},{8,0},{9,1},{10,... | collective-permute-start | bytes 774152 | tf_op jit(solution)/shard_map/ppermute | solution.py:105
  31.0 22.6 %collective-permute-start.10 = (bf16[992,128]{1,0:T(8,128)(2,1)S(1)}, bf16[992,128]{1,0:T(8,128)(2,1)S(1)}, u32[]{:S(2)}, u32[]{:S(2)}) collective-permute-start(bf16[992,128]{1,0:T(8,128)(2,1)S(1)} %collective-permute-done.8), channel_id=1, source_target_pairs={{0,2},{1,3},{2,0},{3,1},{4,6},{5,7},{6,4},{7,5},{8,10},{9,11},{10,... | collective-permute-start | bytes 761864 | tf_op jit(solution)/shard_map/ppermute | solution.py:105
  47.0 15.6 %collective-permute-start.12 = (bf16[992,128]{1,0:T(8,128)(2,1)S(1)}, bf16[992,128]{1,0:T(8,128)(2,1)S(1)}, u32[]{:S(2)}, u32[]{:S(2)}) collective-permute-start(bf16[992,128]{1,0:T(8,128)(2,1)S(1)} %collective-permute-done.6), channel_id=1, source_target_pairs={{0,1},{1,0},{2,4},{3,5},{4,2},{5,3},{6,7},{7,6},{8,9},{9,8},{10,12... | collective-permute-start | bytes 761864 | tf_op jit(solution)/shard_map/ppermute | solution.py:105
  49.0 19.8 %collective-permute-start.17 = (bf16[1008,128]{1,0:T(8,128)(2,1)S(1)}, bf16[1008,128]{1,0:T(8,128)(2,1)S(1)}, u32[]{:S(2)}, u32[]{:S(2)}) collective-permute-start(bf16[1008,128]{1,0:T(8,128)(2,1)S(1)} %collective-permute-done.7), channel_id=1, source_target_pairs={{0,8},{1,9},{2,10},{3,11},{4,12},{5,13},{6,14},{7,15},{8,0},{9,1},... | collective-permute-start | bytes 774152 | tf_op jit(solution)/shard_map/ppermute | solution.py:105
  49.1 10.8 %collective-permute-start.11 = (bf16[1008,128]{1,0:T(8,128)(2,1)S(1)}, bf16[1008,128]{1,0:T(8,128)(2,1)S(1)}, u32[]{:S(2)}, u32[]{:S(2)}) collective-permute-start(bf16[1008,128]{1,0:T(8,128)(2,1)S(1)} %collective-permute-done.9), channel_id=1, source_target_pairs={{0,2},{1,3},{2,0},{3,1},{4,6},{5,7},{6,4},{7,5},{8,10},{9,11},{10,... | collective-permute-start | bytes 774152 | tf_op jit(solution)/shard_map/ppermute | solution.py:105
  53.5 15.4 %collective-permute-start.20 = (bf16[1008,128]{1,0:T(8,128)(2,1)S(1)}, bf16[1008,128]{1,0:T(8,128)(2,1)S(1)}, u32[]{:S(2)}, u32[]{:S(2)}) collective-permute-start(bf16[1008,128]{1,0:T(8,128)(2,1)S(1)} %collective-permute-done.7), channel_id=1, source_target_pairs={{0,16},{1,17},{2,18},{3,19},{4,20},{5,21},{6,22},{7,23},{8,24},{9,... | collective-permute-start | bytes 774152 | tf_op jit(solution)/shard_map/ppermute | solution.py:105
  59.9 8.0 %collective-permute-start.13 = (bf16[1008,128]{1,0:T(8,128)(2,1)S(1)}, bf16[1008,128]{1,0:T(8,128)(2,1)S(1)}, u32[]{:S(2)}, u32[]{:S(2)}) collective-permute-start(bf16[1008,128]{1,0:T(8,128)(2,1)S(1)} %collective-permute-done.7), channel_id=1, source_target_pairs={{0,1},{1,0},{2,4},{3,5},{4,2},{5,3},{6,7},{7,6},{8,9},{9,8},{10,12... | collective-permute-start | bytes 774152 | tf_op jit(solution)/shard_map/ppermute | solution.py:105
  62.5 8.1 %collective-permute-start.26 = (bf16[992,128]{1,0:T(8,128)(2,1)S(1)}, bf16[992,128]{1,0:T(8,128)(2,1)S(1)}, u32[]{:S(2)}, u32[]{:S(2)}) collective-permute-start(bf16[992,128]{1,0:T(8,128)(2,1)S(1)} %collective-permute-done.10), channel_id=1, source_target_pairs={{0,8},{1,9},{2,4},{3,5},{4,2},{5,3},{6,14},{7,15},{8,0},{9,1},{10,... | collective-permute-start | bytes 761864 | tf_op jit(solution)/shard_map/ppermute | solution.py:105
  62.6 7.0 %collective-permute-start.19 = (bf16[992,128]{1,0:T(8,128)(2,1)S(1)}, bf16[992,128]{1,0:T(8,128)(2,1)S(1)}, u32[]{:S(2)}, u32[]{:S(2)}) collective-permute-start(bf16[992,128]{1,0:T(8,128)(2,1)S(1)} %collective-permute-done.18), channel_id=1, source_target_pairs={{0,8},{1,9},{2,10},{3,11},{4,12},{5,13},{6,14},{7,15},{8,0},{9,1},... | collective-permute-start | bytes 761864 | tf_op jit(solution)/shard_map/ppermute | solution.py:105
  68.5 2.2 %collective-permute-start.27 = (bf16[1008,128]{1,0:T(8,128)(2,1)S(1)}, bf16[1008,128]{1,0:T(8,128)(2,1)S(1)}, u32[]{:S(2)}, u32[]{:S(2)}) collective-permute-start(bf16[1008,128]{1,0:T(8,128)(2,1)S(1)} %collective-permute-done.13), channel_id=1, source_target_pairs={{0,8},{1,9},{2,3},{3,2},{4,5},{5,4},{6,14},{7,15},{8,0},{9,1},{10,... | collective-permute-start | bytes 774152 | tf_op jit(solution)/shard_map/ppermute | solution.py:105
  68.9 1.7 %collective-permute-start.21 = (bf16[1008,128]{1,0:T(8,128)(2,1)S(1)}, bf16[1008,128]{1,0:T(8,128)(2,1)S(1)}, u32[]{:S(2)}, u32[]{:S(2)}) collective-permute-start(bf16[1008,128]{1,0:T(8,128)(2,1)S(1)} %collective-permute-done.20), channel_id=1, source_target_pairs={{0,8},{1,9},{2,10},{3,11},{4,12},{5,13},{6,14},{7,15},{8,0},{9,1},... | collective-permute-start | bytes 774152 | tf_op jit(solution)/shard_map/ppermute | solution.py:105
  71.2 14.6 %collective-permute-start.28 = (f16[128,4,128]{2,0,1:T(8,128)(2,1)S(1)}, f16[128,4,128]{2,0,1:T(8,128)(2,1)S(1)}, u32[]{:S(2)}, u32[]{:S(2)}) collective-permute-start(f16[128,4,128]{2,0,1:T(8,128)(2,1)S(1)} %fusion.14), channel_id=1, source_target_pairs={{0,2},{1,3},{2,0},{3,1},{4,6},{5,7},{6,4},{7,5},{8,10},{9,11},{10,... | collective-permute-start | bytes 393224 | tf_op jit(solution)/shard_map/ppermute | solution.py:105
  78.8 5.2 %collective-permute-start.22 = (f16[128,4,128]{2,0,1:T(8,128)(2,1)S(1)}, f16[128,4,128]{2,0,1:T(8,128)(2,1)S(1)}, u32[]{:S(2)}, u32[]{:S(2)}) collective-permute-start(f16[128,4,128]{2,0,1:T(8,128)(2,1)S(1)} %fusion.16), channel_id=1, source_target_pairs={{0,2},{1,3},{2,0},{3,1},{4,6},{5,7},{6,4},{7,5},{8,10},{9,11},{10,... | collective-permute-start | bytes 393224 | tf_op jit(solution)/shard_map/ppermute | solution.py:105
  79.9 5.6 %collective-permute-start.25 = (f16[128,4,128]{2,0,1:T(8,128)(2,1)S(1)}, f16[128,4,128]{2,0,1:T(8,128)(2,1)S(1)}, u32[]{:S(2)}, u32[]{:S(2)}) collective-permute-start(f16[128,4,128]{2,0,1:T(8,128)(2,1)S(1)} %fusion.15), channel_id=1, source_target_pairs={{0,2},{1,3},{2,0},{3,1},{4,6},{5,7},{6,4},{7,5},{8,10},{9,11},{10,... | collective-permute-start | bytes 393224 | tf_op jit(solution)/shard_map/ppermute | solution.py:105
  86.0 1.3 %copy-start.1 = (f32[8,128,4,128]{3,2,1,0:T(4,128)}, f32[8,128,4,128]{3,2,1,0:T(4,128)S(1)}, u32[]{:S(2)}) copy-start(f32[8,128,4,128]{3,2,1,0:T(4,128)S(1)} %copy_dynamic-update-slice_fusion) | copy-start | bytes 6291460

commit v6 on v4

--- a/solution.py
+++ b/solution.py
@@ -39,6 +39,34 @@
     )(data)
 
 
+def store_kernel(count, slots, *refs):
+    panels, out, sems = refs[:count], refs[count], refs[count + 1]
+
+    def copy(i):
+        return pltpu.make_async_copy(panels[i], out.at[slots[i]], sems.at[i])
+
+    for i in range(count):
+        copy(i).start()
+    for i in range(count):
+        copy(i).wait()
+
+
+def store(panels, slots, length):
+    count, shape = len(panels), panels[0].shape
+    size = count * panels[0].size
+    return pl.pallas_call(
+        functools.partial(store_kernel, count),
+        out_shape=jax.ShapeDtypeStruct((length,) + shape, panels[0].dtype),
+        in_specs=[pl.BlockSpec(memory_space=pltpu.SMEM)]
+        + [pl.BlockSpec(memory_space=pl.ANY)] * count,
+        out_specs=pl.BlockSpec(memory_space=pltpu.HBM),
+        scratch_shapes=[pltpu.SemaphoreType.DMA((count,))],
+        cost_estimate=pl.CostEstimate(flops=0, bytes_accessed=8 * size, transcendentals=0),
+        compiler_params=pltpu.CompilerParams(vmem_limit_bytes=2**20),
+        name="store",
+    )(slots, *panels)
+
+
 def shards(descriptors):
     return exchange(descriptors)
 
@@ -72,9 +100,16 @@
     indices.update({("back", k): where((3, k), (2, k)) for k in offsets})
     indices.update({("far", k): where((2, k), (3, k)) for k in offsets})
     names = list(indices)
-    held = lax.optimization_barrier((descriptors, middle) + tuple(indices[n] for n in names))
-    descriptors, middle = held[:2]
-    at = dict(zip(names, held[2:]))
+    data = descriptors.T
+    cut = data.shape[0] // 32 * 16
+    unit = normalize(data, cut)
+    stored = ["unit", "pair", "head"] + [("across", k) for k in range(1, inner - 1)]
+    stored += ["head_pair", "relay"] + [("across_pair", k) for k in range(2, inner)]
+    stored += [("back", k) for k in range(inner)]
+    slots = jnp.stack([indices[n] for n in stored])
+    held = lax.optimization_barrier((*unit, middle, slots, *(indices[n] for n in names)))
+    unit, middle, slots = list(held[:2]), held[2], held[3]
+    at = dict(zip(names, held[4:]))
 
     def mid(zz):
         return zz in (1, 2)
@@ -106,27 +141,29 @@
     def core_swap(g, zz, xx):
         return g ^ 1, zz, xx
 
-    data = descriptors.T
-    cut = data.shape[0] // 32 * 16
-    unit = normalize(data, cut)
+    def other_core(j):
+        return lambda g, zz, xx: (((g ^ 1) - j) % ngroups, zz, xx)
+
     head, pair, relay, head_pair = ([None, None] for _ in range(4))
     across, centre_across = ([[None, None] for _ in offsets] for _ in range(2))
     across_pair = [[None, None] for _ in range(2, inner)]
-    own, end = {0: unit}, {0: pair}
-    for j in others:
-        own[j], end[j] = [None, None], [None, None]
+    quarter = unit[1].shape[0] // 32 * 16
+    own = {0: [(0, unit[0]), (cut, unit[1])]}
+    end = {0: []}
+    for j in others:
+        own[j], end[j] = [], []
     for h in halves:
         head[h] = send(unit[h], centre_swap(1))
+        pair[h] = send(unit[h], line_swap)
         for k in offsets:
             across[k - 1][h] = send(unit[h], shift(k, k + 1))
-        pair[h] = send(unit[h], line_swap)
-        if h == 0:
-            for j in others:
-                own[j][h] = send(unit[h], other(j))
+        for j in others:
+            own[j].append((h * cut, send(unit[h] if h == 0 else unit[1][:quarter], other(j))))
     swapped = {("own", 0, h): send(unit[h], core_swap) for h in halves}
     for h in halves:
+        end[0].append((h * cut, pair[h]))
         for j in others:
-            end[j][h] = send(pair[h], other(j))
+            end[j].append((h * cut, send(pair[h], other(j))))
         relay[h] = send(pair[h], centre_swap(inner - 1))
         for k in offsets:
             centre_across[k - 1][h] = send(head[h], shift(k, 0))
@@ -134,26 +171,37 @@
         for k in range(2, inner):
             across_pair[k - 2][h] = send(across[k - 2][h], line_swap)
     for j in others:
-        own[j][1] = send(unit[1], other(j))
-    for j in others:
-        swapped["own", j, 0] = send(own[j][0], core_swap)
-    swapped.update({("end", 0, h): send(pair[h], core_swap) for h in halves})
-    for j in others:
-        swapped["end", j, 0] = send(end[j][0], core_swap)
-    far_across = [[send(head_pair[0] if k == 1 else across_pair[k - 2][0], centre_swap(0)), None] for k in offsets]
-    for j in others:
-        swapped["end", j, 1] = send(end[j][1], core_swap)
+        own[j].append((cut + quarter, send(unit[1][quarter:], other(j))))
+        swapped["own", j, 2] = send(unit[1][quarter:], other_core(j))
+
+    def swap_cores(name, parts, j, i):
+        swapped[name, j, i] = send(parts[j][i][1], core_swap)
+
+    for j in others:
+        swap_cores("own", own, j, 0)
+        swap_cores("own", own, j, 1)
+    swap_cores("end", end, 0, 0)
+    swap_cores("end", end, 0, 1)
+    for j in others:
+        swap_cores("end", end, j, 0)
+    far_across = [[None, None] for _ in offsets]
+    for k in offsets:
+        source = head_pair if k == 1 else across_pair[k - 2]
+        far_across[k - 1][0] = send(source[0], centre_swap(0))
+    for j in others:
+        swap_cores("end", end, j, 1)
     for k in offsets:
         far_across[k - 1][1] = send(relay[1], shift(k, 0))
 
-    def columns_of(name, parts):
-        full = jnp.zeros((ngroups,) + data.shape, jnp.bfloat16)
+    def place(full, name, parts, last):
         for j in sorted(parts):
-            for h in halves:
-                pieces = ((parts[j][h], at["own", j]), (swapped[name, j, h], at["swapped", j]))
+            for i, (row, part) in enumerate(parts[j]):
+                if (name == "own" and i == 2) != last:
+                    continue
+                pieces = ((part, at["own", j]), (swapped[name, j, i], at["swapped", j]))
                 for array, index in pieces:
                     full = lax.dynamic_update_slice(
-                        full, array[None], (index, h * cut, 0), allow_negative_indices=False
+                        full, array[None], (index, row, 0), allow_negative_indices=False
                     )
         return full
 
@@ -179,28 +227,29 @@
         panel = (fourth(block, end_columns) * SCALE).astype(jnp.float16)
         return send(panel, line_swap)
 
-    end_columns = columns_of("end", end)
+    empty = jnp.zeros((ngroups,) + data.shape, jnp.bfloat16)
+    columns = place(empty, "own", own, False)
+    end_columns = place(empty, "end", end, False)
     panels = [back(b) for b in [relay] + centre_across]
-    for j in others:
-        swapped["own", j, 1] = send(own[j][1], core_swap)
-    columns = columns_of("own", own)
-    out = jnp.zeros((ncolumns, block, ngroups, block), jnp.float32)
-    out = put(out, product(unit), at["unit"])
-    out = put(out, product(pair), at["pair"])
-    out = put(out, product(head), at["head"])
-    for k in range(1, inner - 1):
-        out = put(out, product(across[k - 1]), at["across", k])
+    columns = place(columns, "own", own, True)
+    ready = [(product(unit), "unit"), (product(pair), "pair"), (product(head), "head")]
+    ready += [(product(across[k - 1]), ("across", k)) for k in range(1, inner - 1)]
     mine = [product(across[-1])]
+    ready += [(product(relay), "relay")]
     panels += [back(b) for b in far_across]
-    out = put(out, product(head_pair), at["head_pair"])
-    out = put(out, product(relay), at["relay"])
-    for k in range(2, inner):
-        out = put(out, product(across_pair[k - 2]), at["across_pair", k])
-    mine += [product(b) for b in centre_across + far_across]
-    slots = [at["back", k] for k in range(inner)] + [at["far", k] for k in offsets]
-    for index, panel, value in zip(slots, panels, mine):
-        theirs = panel.astype(jnp.float32) * (1.0 / SCALE)
-        out = put(out, jnp.where(middle, value, theirs), index)
+    ready += [(product(head_pair), "head_pair")]
+    ready += [(product(across_pair[k - 2]), ("across_pair", k)) for k in range(2, inner)]
+    mine += [product(b) for b in centre_across]
+    mine += [product(b) for b in far_across]
+    merged = [
+        jnp.where(middle, value, panel.astype(jnp.float32) * (1.0 / SCALE))
+        for value, panel in zip(mine, panels)
+    ]
+    ready += [(value, ("back", k)) for k, value in enumerate(merged[:inner])]
+    ready.sort(key=lambda item: stored.index(item[1]))
+    out = store([value for value, _ in ready], slots, ncolumns)
+    for k in offsets:
+        out = put(out, merged[inner + k - 1], at["far", k])
     return out.reshape(ncolumns * block, ngroups, block)
 
 

time: 86.1 us -> 89.2 us (1.036)
  waiting for transfers between devices: 25.7 us -> 34.7 us
  starting transfers between devices: 48.6 us -> 41 us
  local copies, waits for them, and re-layouts: 5.46 us -> 2.47 us
  other arithmetic: 0.1 us -> 2.94 us
  Pallas kernels: 0.33 us -> 2.15 us
    ppermute x29 -> x31, waiting for transfers between devices: 25.7 us -> 34.7 us  [send(): return lax.ppermute(array, AXES, pairs)]
    ppermute x29 -> x31, starting transfers between devices: 48.6 us -> 41 us  [send(): return lax.ppermute(array, AXES, pairs)]
    pallas_call x0 -> x1, Pallas kernels: none -> 1.83 us  [store(): pl.pallas_call(functools.partial(store_kernel, count), out_shape=jax.Shap...]
    dynamic_update_slice x24 -> x18, local copies, waits for them, and re-layouts: 2.13 us -> 0.61 us  [place(): lax.dynamic_update_slice(full, array[None], (index, row, 0), allow_negati...]
    mul x0 -> x8, other arithmetic: none -> 1.38 us  [fourth(): return second * second]
    unnamed x4 -> x2, local copies, waits for them, and re-layouts: 2.53 us -> 1.22 us
  transfers between devices with their start and end apart: 29 -> 31, of which waited for: 9 -> 13; matrix products, arithmetic and copies ran while one was open for 9% -> 10% of each run, Pallas kernels for 0% -> 2%
where the time goes in v6:
time: 89.2 us; the launch traced here: 89 us
  starting transfers between devices  41 us (46%)
  waiting for transfers between devices  34.7 us (39%)
  matrix products  5.24 us (6%)
  other arithmetic  2.94 us (3%)
  local copies, waits for them, and re-layouts  2.47 us (3%)
  Pallas kernels  2.15 us (2%)
    ppermute x31, starting transfers between devices, send(): return lax.ppermute(array, AXES, pairs)  41 us
    ppermute x31, waiting for transfers between devices, send(): return lax.ppermute(array, AXES, pairs)  34.7 us
    dot_general x11, matrix products, fourth(): lax.dot_general(jnp.concatenate(block, axis=0), cols, (((0,), (1,)), ((),...  5.24 us
    pallas_call x1, Pallas kernels, store(): pl.pallas_call(functools.partial(store_kernel, count), out_shape=jax.Shap...  1.83 us
  transfers between devices with their start and end apart: 31, of which 13 were waited for; matrix products, arithmetic and copies ran while one was open for 10% of the time, Pallas kernels for 2%

profile of v6, /device:TPU:0, one launch (start us, length us, event | category | flops | bytes accessed | tf_op | source)
XLA Modules:
  0.0 89.0 jit_solution(1361870830523596931)
XLA Ops:
  0.0 1.2 %copy-done = f32[128,2000]{0,1:T(8,128)S(1)} copy-done((f32[128,2000]{0,1:T(8,128)S(1)}, f32[128,2000]{0,1:T(8,128)}, u32[]{:S(2)}) %copy-start) | copy-done | bytes 1024024
  1.2 0.3 normalize.1
  1.7 3.1 %collective-permute-start.8 = (bf16[992,128]{1,0:T(8,128)(2,1)S(1)}, bf16[992,128]{1,0:T(8,128)(2,1)S(1)}, u32[]{:S(2)}, u32[]{:S(2)}) collective-permute-start(bf16[992,128]{1,0:T(8,128)(2,1)S(1)} %get-tuple-element.19), channel_id=1, source_target_pairs={{0,2},{1,3},{2,0},{3,1},{4,6},{5,7},{6,4},{7,5},{8,10},{9,11},{10,... | collective-permute-start | bytes 761864 | tf_op jit(solution)/shard_map/ppermute | solution.py:123
  4.8 1.9 %collective-permute-start.11 = (bf16[1008,128]{1,0:T(8,128)(2,1)S(1)}, bf16[1008,128]{1,0:T(8,128)(2,1)S(1)}, u32[]{:S(2)}, u32[]{:S(2)}) collective-permute-start(bf16[1008,128]{1,0:T(8,128)(2,1)S(1)} %get-tuple-element.20), channel_id=1, source_target_pairs={{0,1},{1,0},{2,4},{3,5},{4,2},{5,3},{6,7},{7,6},{8,9},{9,8},{10,12... | collective-permute-start | bytes 774152 | tf_op jit(solution)/shard_map/ppermute | solution.py:123
  6.8 0.3 broadcast_in_dim.61.clone
  7.2 4.5 %collective-permute-done.8 = bf16[992,128]{1,0:T(8,128)(2,1)S(1)} collective-permute-done((bf16[992,128]{1,0:T(8,128)(2,1)S(1)}, bf16[992,128]{1,0:T(8,128)(2,1)S(1)}, u32[]{:S(2)}, u32[]{:S(2)}) %collective-permute-start.8) | collective-permute-done | bytes 253984 | tf_op jit(solution)/shard_map/ppermute | solution.py:123
  11.7 0.3 broadcast_in_dim.61.clone.1
  12.1 2.0 %collective-permute-start.2 = (bf16[992,128]{1,0:T(8,128)(2,1)S(1)}, bf16[992,128]{1,0:T(8,128)(2,1)S(1)}, u32[]{:S(2)}, u32[]{:S(2)}) collective-permute-start(bf16[992,128]{1,0:T(8,128)(2,1)S(1)} %get-tuple-element.19), channel_id=1, source_target_pairs={{0,16},{1,17},{2,18},{3,19},{4,20},{5,21},{6,22},{7,23},{8,24},{9,... | collective-permute-start | bytes 761864 | tf_op jit(solution)/shard_map/ppermute | solution.py:123
  14.2 6.7 %collective-permute-done.2 = bf16[992,128]{1,0:T(8,128)(2,1)S(1)} collective-permute-done((bf16[992,128]{1,0:T(8,128)(2,1)S(1)}, bf16[992,128]{1,0:T(8,128)(2,1)S(1)}, u32[]{:S(2)}, u32[]{:S(2)}) %collective-permute-start.2) | collective-permute-done | bytes 253984 | tf_op jit(solution)/shard_map/ppermute | solution.py:123
  20.9 1.7 %collective-permute-start.4 = (bf16[496,128]{1,0:T(8,128)(2,1)S(1)}, bf16[496,128]{1,0:T(8,128)(2,1)S(1)}, u32[]{:S(2)}, u32[]{:S(2)}) collective-permute-start(bf16[496,128]{1,0:T(8,128)(2,1)S(1)} %slice.7), channel_id=1, source_target_pairs={{0,16},{1,17},{2,18},{3,19},{4,20},{5,21},{6,22},{7,23},{8,24},{9,... | collective-permute-start | bytes 380936 | tf_op jit(solution)/shard_map/ppermute | solution.py:123
  22.7 3.4 %collective-permute-done.4 = bf16[496,128]{1,0:T(8,128)(2,1)S(1)} collective-permute-done((bf16[496,128]{1,0:T(8,128)(2,1)S(1)}, bf16[496,128]{1,0:T(8,128)(2,1)S(1)}, u32[]{:S(2)}, u32[]{:S(2)}) %collective-permute-start.4) | collective-permute-done | bytes 127008 | tf_op jit(solution)/shard_map/ppermute | solution.py:123
  26.1 1.5 %collective-permute-start.6 = (bf16[512,128]{1,0:T(8,128)(2,1)S(1)}, bf16[512,128]{1,0:T(8,128)(2,1)S(1)}, u32[]{:S(2)}, u32[]{:S(2)}) collective-permute-start(bf16[512,128]{1,0:T(8,128)(2,1)S(1)} %slice.8), channel_id=1, source_target_pairs={{0,16},{1,17},{2,18},{3,19},{4,20},{5,21},{6,22},{7,23},{8,24},{9,... | collective-permute-start | bytes 393224 | tf_op jit(solution)/shard_map/ppermute | solution.py:123
  27.7 1.3 %collective-permute-done.5 = bf16[496,128]{1,0:T(8,128)(2,1)S(1)} collective-permute-done((bf16[496,128]{1,0:T(8,128)(2,1)S(1)}, bf16[496,128]{1,0:T(8,128)(2,1)S(1)}, u32[]{:S(2)}, u32[]{:S(2)}) %collective-permute-start.5) | collective-permute-done | bytes 127008 | tf_op jit(solution)/shard_map/ppermute | solution.py:123
  28.9 0.3 collective-permute-start.7
  29.2 1.8 %collective-permute-done.6 = bf16[512,128]{1,0:T(8,128)(2,1)S(1)} collective-permute-done((bf16[512,128]{1,0:T(8,128)(2,1)S(1)}, bf16[512,128]{1,0:T(8,128)(2,1)S(1)}, u32[]{:S(2)}, u32[]{:S(2)}) %collective-permute-start.6) | collective-permute-done | bytes 131104 | tf_op jit(solution)/shard_map/ppermute | solution.py:123
  31.1 3.3 %collective-permute-done.7 = bf16[512,128]{1,0:T(8,128)(2,1)S(1)} collective-permute-done((bf16[512,128]{1,0:T(8,128)(2,1)S(1)}, bf16[512,128]{1,0:T(8,128)(2,1)S(1)}, u32[]{:S(2)}, u32[]{:S(2)}) %collective-permute-start.7) | collective-permute-done | bytes 131104 | tf_op jit(solution)/shard_map/ppermute | solution.py:123
  34.6 0.5 convolution_multiply_fusion.10
  35.1 0.4 collective-permute-start.18
  35.5 0.7 collective-permute-start.20
  36.3 0.5 convolution_multiply_fusion.8
  36.8 1.6 %collective-permute-start.14 = (bf16[992,128]{1,0:T(8,128)(2,1)S(1)}, bf16[992,128]{1,0:T(8,128)(2,1)S(1)}, u32[]{:S(2)}, u32[]{:S(2)}) collective-permute-start(bf16[992,128]{1,0:T(8,128)(2,1)S(1)} %collective-permute-done.8), channel_id=1, source_target_pairs={{0,1},{1,0},{2,4},{3,5},{4,2},{5,3},{6,7},{7,6},{8,9},{9,8},{10,12... | collective-permute-start | bytes 761864 | tf_op jit(solution)/shard_map/ppermute | solution.py:123
  38.4 0.5 convolution_multiply_fusion.5
  39.2 9.5 %collective-permute-start.12 = (bf16[992,128]{1,0:T(8,128)(2,1)S(1)}, bf16[992,128]{1,0:T(8,128)(2,1)S(1)}, u32[]{:S(2)}, u32[]{:S(2)}) collective-permute-start(bf16[992,128]{1,0:T(8,128)(2,1)S(1)} %collective-permute-done.10), channel_id=1, source_target_pairs={{0,2},{1,3},{2,0},{3,1},{4,6},{5,7},{6,4},{7,5},{8,10},{9,11},{10,... | collective-permute-start | bytes 761864 | tf_op jit(solution)/shard_map/ppermute | solution.py:123
  48.8 0.5 convolution_multiply_fusion.9
  49.8 0.6 collective-permute-start.19
  50.4 0.9 collective-permute-done.26
  51.2 6.9 %collective-permute-start.13 = (bf16[1008,128]{1,0:T(8,128)(2,1)S(1)}, bf16[1008,128]{1,0:T(8,128)(2,1)S(1)}, u32[]{:S(2)}, u32[]{:S(2)}) collective-permute-start(bf16[1008,128]{1,0:T(8,128)(2,1)S(1)} %collective-permute-done.11), channel_id=1, source_target_pairs={{0,2},{1,3},{2,0},{3,1},{4,6},{5,7},{6,4},{7,5},{8,10},{9,11},{10,... | collective-permute-start | bytes 774152 | tf_op jit(solution)/shard_map/ppermute | solution.py:123
  58.1 0.5 convolution_multiply_fusion.3
  58.6 0.5 collective-permute-start.22
  59.1 4.4 %collective-permute-done.13 = bf16[1008,128]{1,0:T(8,128)(2,1)S(1)} collective-permute-done((bf16[1008,128]{1,0:T(8,128)(2,1)S(1)}, bf16[1008,128]{1,0:T(8,128)(2,1)S(1)}, u32[]{:S(2)}, u32[]{:S(2)}) %collective-permute-start.13) | collective-permute-done | bytes 258080 | tf_op jit(solution)/shard_map/ppermute | solution.py:123
  63.5 1.4 %collective-permute-start.15 = (bf16[1008,128]{1,0:T(8,128)(2,1)S(1)}, bf16[1008,128]{1,0:T(8,128)(2,1)S(1)}, u32[]{:S(2)}, u32[]{:S(2)}) collective-permute-start(bf16[1008,128]{1,0:T(8,128)(2,1)S(1)} %collective-permute-done.9), channel_id=1, source_target_pairs={{0,1},{1,0},{2,4},{3,5},{4,2},{5,3},{6,7},{7,6},{8,9},{9,8},{10,12... | collective-permute-start | bytes 774152 | tf_op jit(solution)/shard_map/ppermute | solution.py:123
  64.9 0.5 convolution_multiply_fusion.7
  65.7 0.5 collective-permute-start.21
  66.2 3.9 %collective-permute-done.15 = bf16[1008,128]{1,0:T(8,128)(2,1)S(1)} collective-permute-done((bf16[1008,128]{1,0:T(8,128)(2,1)S(1)}, bf16[1008,128]{1,0:T(8,128)(2,1)S(1)}, u32[]{:S(2)}, u32[]{:S(2)}) %collective-permute-start.15) | collective-permute-done | bytes 258080 | tf_op jit(solution)/shard_map/ppermute | solution.py:123
  70.1 0.5 convolution_multiply_fusion.6
  71.1 0.5 collective-permute-start.23
  71.7 1.2 %collective-permute-done.23 = bf16[1008,128]{1,0:T(8,128)(2,1)S(1)} collective-permute-done((bf16[1008,128]{1,0:T(8,128)(2,1)S(1)}, bf16[1008,128]{1,0:T(8,128)(2,1)S(1)}, u32[]{:S(2)}, u32[]{:S(2)}) %collective-permute-start.23) | collective-permute-done | bytes 258080 | tf_op jit(solution)/shard_map/ppermute | solution.py:123
  73.0 0.5 convolution_multiply_fusion.2
  73.7 5.2 %collective-permute-start.27 = (f16[128,4,128]{2,1,0:T(4,128)(2,1)S(1)}, f16[128,4,128]{2,1,0:T(4,128)(2,1)S(1)}, u32[]{:S(2)}, u32[]{:S(2)}) collective-permute-start(f16[128,4,128]{2,1,0:T(4,128)(2,1)S(1)} %fusion.13), channel_id=1, source_target_pairs={{0,2},{1,3},{2,0},{3,1},{4,6},{5,7},{6,4},{7,5},{8,10},{9,11},{10,... | collective-permute-start | bytes 393224 | tf_op jit(solution)/shard_map/ppermute | solution.py:123
  78.8 0.5 convolution_multiply_fusion.4
  79.6 0.5 convolution_multiply_fusion
  80.1 0.2 fusion.11
  80.3 2.1 %collective-permute-start.30 = (f16[128,4,128]{2,1,0:T(4,128)(2,1)S(1)}, f16[128,4,128]{2,1,0:T(4,128)(2,1)S(1)}, u32[]{:S(2)}, u32[]{:S(2)}) collective-permute-start(f16[128,4,128]{2,1,0:T(4,128)(2,1)S(1)} %fusion.11), channel_id=1, source_target_pairs={{0,2},{1,3},{2,0},{3,1},{4,6},{5,7},{6,4},{7,5},{8,10},{9,11},{10,... | collective-permute-start | bytes 393224 | tf_op jit(solution)/shard_map/ppermute | solution.py:123
  82.3 0.5 convolution_multiply_fusion.1
  83.3 2.7 %collective-permute-done.24 = f16[128,4,128]{2,1,0:T(4,128)(2,1)S(1)} collective-permute-done((f16[128,4,128]{2,1,0:T(4,128)(2,1)S(1)}, f16[128,4,128]{2,1,0:T(4,128)(2,1)S(1)}, u32[]{:S(2)}, u32[]{:S(2)}) %collective-permute-start.24) | collective-permute-done | bytes 131104 | tf_op jit(solution)/shard_map/ppermute | solution.py:123
  86.1 1.8 %store.1 = f32[8,128,4,128]{3,2,1,0:T(4,128)} custom-call(s32[7]{0:T(128)S(1)} %stack.31.slots, f32[128,4,128]{2,1,0:T(4,128)S(1)} %copy_multiply_fusion.10.refs_0_, f32[128,4,128]{2,1,0:T(4,128)S(1)} %copy_multiply_fusion.9.refs_1_, f32[128,4,128]{2,1,0:T(4,128)S(1)} %copy_multiply_fusion.8.refs_2_, f32[128,4,128]{2,1,0:T(4,128)S(1)} %copy_multiply_fusion.7.refs_3_, ...), custom_call_target="tpu_custom_call" | custom-call | bytes 3670016 | tf_op jit(solution)/shard_map/store/pallas_call | solution.py:57
  87.9 0.3 collective-permute-done.30
  88.2 0.8 bitcast_dynamic-update-slice_fusion
  (66 shorter events, 3.7 us)
Async XLA Ops:
  0.0 1.2 %copy-start = (f32[128,2000]{0,1:T(8,128)S(1)}, f32[128,2000]{0,1:T(8,128)}, u32[]{:S(2)}) copy-start(f32[128,2000]{0,1:T(8,128)} %param.1) | copy-start | bytes 3072004
  1.7 10.0 %collective-permute-start.8 = (bf16[992,128]{1,0:T(8,128)(2,1)S(1)}, bf16[992,128]{1,0:T(8,128)(2,1)S(1)}, u32[]{:S(2)}, u32[]{:S(2)}) collective-permute-start(bf16[992,128]{1,0:T(8,128)(2,1)S(1)} %get-tuple-element.19), channel_id=1, source_target_pairs={{0,2},{1,3},{2,0},{3,1},{4,6},{5,7},{6,4},{7,5},{8,10},{9,11},{10,... | collective-permute-start | bytes 761864 | tf_op jit(solution)/shard_map/ppermute | solution.py:123
  4.7 34.5 %collective-permute-start.9 = (bf16[1008,128]{1,0:T(8,128)(2,1)S(1)}, bf16[1008,128]{1,0:T(8,128)(2,1)S(1)}, u32[]{:S(2)}, u32[]{:S(2)}) collective-permute-start(bf16[1008,128]{1,0:T(8,128)(2,1)S(1)} %get-tuple-element.20), channel_id=1, source_target_pairs={{0,2},{1,3},{2,0},{3,1},{4,6},{5,7},{6,4},{7,5},{8,10},{9,11},{10,... | collective-permute-start | bytes 774152 | tf_op jit(solution)/shard_map/ppermute | solution.py:123
  4.8 30.7 %collective-permute-start.11 = (bf16[1008,128]{1,0:T(8,128)(2,1)S(1)}, bf16[1008,128]{1,0:T(8,128)(2,1)S(1)}, u32[]{:S(2)}, u32[]{:S(2)}) collective-permute-start(bf16[1008,128]{1,0:T(8,128)(2,1)S(1)} %get-tuple-element.20), channel_id=1, source_target_pairs={{0,1},{1,0},{2,4},{3,5},{4,2},{5,3},{6,7},{7,6},{8,9},{9,8},{10,12... | collective-permute-start | bytes 774152 | tf_op jit(solution)/shard_map/ppermute | solution.py:123
  6.7 28.4 %collective-permute-start.10 = (bf16[992,128]{1,0:T(8,128)(2,1)S(1)}, bf16[992,128]{1,0:T(8,128)(2,1)S(1)}, u32[]{:S(2)}, u32[]{:S(2)}) collective-permute-start(bf16[992,128]{1,0:T(8,128)(2,1)S(1)} %get-tuple-element.19), channel_id=1, source_target_pairs={{0,1},{1,0},{2,4},{3,5},{4,2},{5,3},{6,7},{7,6},{8,9},{9,8},{10,12... | collective-permute-start | bytes 761864 | tf_op jit(solution)/shard_map/ppermute | solution.py:123
  6.8 5.2 %collective-permute-start = (bf16[992,128]{1,0:T(8,128)(2,1)S(1)}, bf16[992,128]{1,0:T(8,128)(2,1)S(1)}, u32[]{:S(2)}, u32[]{:S(2)}) collective-permute-start(bf16[992,128]{1,0:T(8,128)(2,1)S(1)} %get-tuple-element.19), channel_id=1, source_target_pairs={{0,8},{1,9},{2,10},{3,11},{4,12},{5,13},{6,14},{7,15},{8,0},{9,1},... | collective-permute-start | bytes 761864 | tf_op jit(solution)/shard_map/ppermute | solution.py:123
  11.7 10.9 %collective-permute-start.1 = (bf16[1008,128]{1,0:T(8,128)(2,1)S(1)}, bf16[1008,128]{1,0:T(8,128)(2,1)S(1)}, u32[]{:S(2)}, u32[]{:S(2)}) collective-permute-start(bf16[1008,128]{1,0:T(8,128)(2,1)S(1)} %get-tuple-element.20), channel_id=1, source_target_pairs={{0,8},{1,9},{2,10},{3,11},{4,12},{5,13},{6,14},{7,15},{8,0},{9,1},... | collective-permute-start | bytes 774152 | tf_op jit(solution)/shard_map/ppermute | solution.py:123
  12.1 8.8 %collective-permute-start.2 = (bf16[992,128]{1,0:T(8,128)(2,1)S(1)}, bf16[992,128]{1,0:T(8,128)(2,1)S(1)}, u32[]{:S(2)}, u32[]{:S(2)}) collective-permute-start(bf16[992,128]{1,0:T(8,128)(2,1)S(1)} %get-tuple-element.19), channel_id=1, source_target_pairs={{0,16},{1,17},{2,18},{3,19},{4,20},{5,21},{6,22},{7,23},{8,24},{9,... | collective-permute-start | bytes 761864 | tf_op jit(solution)/shard_map/ppermute | solution.py:123
  20.9 5.2 %collective-permute-start.4 = (bf16[496,128]{1,0:T(8,128)(2,1)S(1)}, bf16[496,128]{1,0:T(8,128)(2,1)S(1)}, u32[]{:S(2)}, u32[]{:S(2)}) collective-permute-start(bf16[496,128]{1,0:T(8,128)(2,1)S(1)} %slice.7), channel_id=1, source_target_pairs={{0,16},{1,17},{2,18},{3,19},{4,20},{5,21},{6,22},{7,23},{8,24},{9,... | collective-permute-start | bytes 380936 | tf_op jit(solution)/shard_map/ppermute | solution.py:123
  22.6 5.0 %collective-permute-start.3 = (bf16[992,128]{1,0:T(8,128)(2,1)S(1)}, bf16[992,128]{1,0:T(8,128)(2,1)S(1)}, u32[]{:S(2)}, u32[]{:S(2)}) collective-permute-start(bf16[992,128]{1,0:T(8,128)(2,1)S(1)} %collective-permute-done.2), channel_id=1, source_target_pairs={{0,8},{1,9},{2,10},{3,11},{4,12},{5,13},{6,14},{7,15},{8,0},{9,1},... | collective-permute-start | bytes 761864 | tf_op jit(solution)/shard_map/ppermute | solution.py:123
  26.1 5.0 %collective-permute-start.6 = (bf16[512,128]{1,0:T(8,128)(2,1)S(1)}, bf16[512,128]{1,0:T(8,128)(2,1)S(1)}, u32[]{:S(2)}, u32[]{:S(2)}) collective-permute-start(bf16[512,128]{1,0:T(8,128)(2,1)S(1)} %slice.8), channel_id=1, source_target_pairs={{0,16},{1,17},{2,18},{3,19},{4,20},{5,21},{6,22},{7,23},{8,24},{9,... | collective-permute-start | bytes 393224 | tf_op jit(solution)/shard_map/ppermute | solution.py:123
  27.6 1.3 %collective-permute-start.5 = (bf16[496,128]{1,0:T(8,128)(2,1)S(1)}, bf16[496,128]{1,0:T(8,128)(2,1)S(1)}, u32[]{:S(2)}, u32[]{:S(2)}) collective-permute-start(bf16[496,128]{1,0:T(8,128)(2,1)S(1)} %collective-permute-done.4), channel_id=1, source_target_pairs={{0,8},{1,9},{2,10},{3,11},{4,12},{5,13},{6,14},{7,15},{8,0},{9,1},... | collective-permute-start | bytes 380936 | tf_op jit(solution)/shard_map/ppermute | solution.py:123
  28.9 5.5 %collective-permute-start.7 = (bf16[512,128]{1,0:T(8,128)(2,1)S(1)}, bf16[512,128]{1,0:T(8,128)(2,1)S(1)}, u32[]{:S(2)}, u32[]{:S(2)}) collective-permute-start(bf16[512,128]{1,0:T(8,128)(2,1)S(1)} %slice.8), channel_id=1, source_target_pairs={{0,24},{1,25},{2,26},{3,27},{4,28},{5,29},{6,30},{7,31},{8,16},{9,... | collective-permute-start | bytes 393224 | tf_op jit(solution)/shard_map/ppermute | solution.py:123
  31.0 5.8 %collective-permute-start.17 = (bf16[1008,128]{1,0:T(8,128)(2,1)S(1)}, bf16[1008,128]{1,0:T(8,128)(2,1)S(1)}, u32[]{:S(2)}, u32[]{:S(2)}) collective-permute-start(bf16[1008,128]{1,0:T(8,128)(2,1)S(1)} %get-tuple-element.20), channel_id=1, source_target_pairs={{0,8},{1,9},{2,3},{3,2},{4,5},{5,4},{6,14},{7,15},{8,0},{9,1},{10,... | collective-permute-start | bytes 774152 | tf_op jit(solution)/shard_map/ppermute | solution.py:123
  34.4 2.3 %collective-permute-start.16 = (bf16[992,128]{1,0:T(8,128)(2,1)S(1)}, bf16[992,128]{1,0:T(8,128)(2,1)S(1)}, u32[]{:S(2)}, u32[]{:S(2)}) collective-permute-start(bf16[992,128]{1,0:T(8,128)(2,1)S(1)} %get-tuple-element.19), channel_id=1, source_target_pairs={{0,8},{1,9},{2,3},{3,2},{4,5},{5,4},{6,14},{7,15},{8,0},{9,1},{10,... | collective-permute-start | bytes 761864 | tf_op jit(solution)/shard_map/ppermute | solution.py:123
  35.1 14.6 %collective-permute-start.18 = (bf16[992,128]{1,0:T(8,128)(2,1)S(1)}, bf16[992,128]{1,0:T(8,128)(2,1)S(1)}, u32[]{:S(2)}, u32[]{:S(2)}) collective-permute-start(bf16[992,128]{1,0:T(8,128)(2,1)S(1)} %collective-permute-done.8), channel_id=1, source_target_pairs={{0,8},{1,9},{2,10},{3,11},{4,12},{5,13},{6,14},{7,15},{8,0},{9,1},... | collective-permute-start | bytes 761864 | tf_op jit(solution)/shard_map/ppermute | solution.py:123
  35.5 30.1 %collective-permute-start.20 = (bf16[992,128]{1,0:T(8,128)(2,1)S(1)}, bf16[992,128]{1,0:T(8,128)(2,1)S(1)}, u32[]{:S(2)}, u32[]{:S(2)}) collective-permute-start(bf16[992,128]{1,0:T(8,128)(2,1)S(1)} %collective-permute-done.8), channel_id=1, source_target_pairs={{0,16},{1,17},{2,18},{3,19},{4,20},{5,21},{6,22},{7,23},{8,24},{9,... | collective-permute-start | bytes 761864 | tf_op jit(solution)/shard_map/ppermute | solution.py:123
  36.7 13.1 %collective-permute-start.25 = (bf16[992,128]{1,0:T(8,128)(2,1)S(1)}, bf16[992,128]{1,0:T(8,128)(2,1)S(1)}, u32[]{:S(2)}, u32[]{:S(2)}) collective-permute-start(bf16[992,128]{1,0:T(8,128)(2,1)S(1)} %collective-permute-done.10), channel_id=1, source_target_pairs={{0,8},{1,9},{2,3},{3,2},{4,5},{5,4},{6,14},{7,15},{8,0},{9,1},{10,... | collective-permute-start | bytes 761864 | tf_op jit(solution)/shard_map/ppermute | solution.py:123
  36.8 28.8 %collective-permute-start.14 = (bf16[992,128]{1,0:T(8,128)(2,1)S(1)}, bf16[992,128]{1,0:T(8,128)(2,1)S(1)}, u32[]{:S(2)}, u32[]{:S(2)}) collective-permute-start(bf16[992,128]{1,0:T(8,128)(2,1)S(1)} %collective-permute-done.8), channel_id=1, source_target_pairs={{0,1},{1,0},{2,4},{3,5},{4,2},{5,3},{6,7},{7,6},{8,9},{9,8},{10,12... | collective-permute-start | bytes 761864 | tf_op jit(solution)/shard_map/ppermute | solution.py:123
  39.2 19.4 %collective-permute-start.12 = (bf16[992,128]{1,0:T(8,128)(2,1)S(1)}, bf16[992,128]{1,0:T(8,128)(2,1)S(1)}, u32[]{:S(2)}, u32[]{:S(2)}) collective-permute-start(bf16[992,128]{1,0:T(8,128)(2,1)S(1)} %collective-permute-done.10), channel_id=1, source_target_pairs={{0,2},{1,3},{2,0},{3,1},{4,6},{5,7},{6,4},{7,5},{8,10},{9,11},{10,... | collective-permute-start | bytes 761864 | tf_op jit(solution)/shard_map/ppermute | solution.py:123
  49.6 1.6 %collective-permute-start.26 = (bf16[1008,128]{1,0:T(8,128)(2,1)S(1)}, bf16[1008,128]{1,0:T(8,128)(2,1)S(1)}, u32[]{:S(2)}, u32[]{:S(2)}) collective-permute-start(bf16[1008,128]{1,0:T(8,128)(2,1)S(1)} %collective-permute-done.11), channel_id=1, source_target_pairs={{0,8},{1,9},{2,3},{3,2},{4,5},{5,4},{6,14},{7,15},{8,0},{9,1},{10,... | collective-permute-start | bytes 774152 | tf_op jit(solution)/shard_map/ppermute | solution.py:123
  49.8 21.7 %collective-permute-start.19 = (bf16[1008,128]{1,0:T(8,128)(2,1)S(1)}, bf16[1008,128]{1,0:T(8,128)(2,1)S(1)}, u32[]{:S(2)}, u32[]{:S(2)}) collective-permute-start(bf16[1008,128]{1,0:T(8,128)(2,1)S(1)} %collective-permute-done.9), channel_id=1, source_target_pairs={{0,8},{1,9},{2,10},{3,11},{4,12},{5,13},{6,14},{7,15},{8,0},{9,1},... | collective-permute-start | bytes 774152 | tf_op jit(solution)/shard_map/ppermute | solution.py:123
  51.2 12.3 %collective-permute-start.13 = (bf16[1008,128]{1,0:T(8,128)(2,1)S(1)}, bf16[1008,128]{1,0:T(8,128)(2,1)S(1)}, u32[]{:S(2)}, u32[]{:S(2)}) collective-permute-start(bf16[1008,128]{1,0:T(8,128)(2,1)S(1)} %collective-permute-done.11), channel_id=1, source_target_pairs={{0,2},{1,3},{2,0},{3,1},{4,6},{5,7},{6,4},{7,5},{8,10},{9,11},{10,... | collective-permute-start | bytes 774152 | tf_op jit(solution)/shard_map/ppermute | solution.py:123
  58.6 12.4 %collective-permute-start.22 = (bf16[1008,128]{1,0:T(8,128)(2,1)S(1)}, bf16[1008,128]{1,0:T(8,128)(2,1)S(1)}, u32[]{:S(2)}, u32[]{:S(2)}) collective-permute-start(bf16[1008,128]{1,0:T(8,128)(2,1)S(1)} %collective-permute-done.9), channel_id=1, source_target_pairs={{0,16},{1,17},{2,18},{3,19},{4,20},{5,21},{6,22},{7,23},{8,24},{9,... | collective-permute-start | bytes 774152 | tf_op jit(solution)/shard_map/ppermute | solution.py:123
  63.5 6.6 %collective-permute-start.15 = (bf16[1008,128]{1,0:T(8,128)(2,1)S(1)}, bf16[1008,128]{1,0:T(8,128)(2,1)S(1)}, u32[]{:S(2)}, u32[]{:S(2)}) collective-permute-start(bf16[1008,128]{1,0:T(8,128)(2,1)S(1)} %collective-permute-done.9), channel_id=1, source_target_pairs={{0,1},{1,0},{2,4},{3,5},{4,2},{5,3},{6,7},{7,6},{8,9},{9,8},{10,12... | collective-permute-start | bytes 774152 | tf_op jit(solution)/shard_map/ppermute | solution.py:123
  65.6 14.0 %collective-permute-start.28 = (bf16[992,128]{1,0:T(8,128)(2,1)S(1)}, bf16[992,128]{1,0:T(8,128)(2,1)S(1)}, u32[]{:S(2)}, u32[]{:S(2)}) collective-permute-start(bf16[992,128]{1,0:T(8,128)(2,1)S(1)} %collective-permute-done.12), channel_id=1, source_target_pairs={{0,8},{1,9},{2,4},{3,5},{4,2},{5,3},{6,14},{7,15},{8,0},{9,1},{10,... | collective-permute-start | bytes 761864 | tf_op jit(solution)/shard_map/ppermute | solution.py:123
  65.7 5.9 %collective-permute-start.21 = (bf16[992,128]{1,0:T(8,128)(2,1)S(1)}, bf16[992,128]{1,0:T(8,128)(2,1)S(1)}, u32[]{:S(2)}, u32[]{:S(2)}) collective-permute-start(bf16[992,128]{1,0:T(8,128)(2,1)S(1)} %collective-permute-done.20), channel_id=1, source_target_pairs={{0,8},{1,9},{2,10},{3,11},{4,12},{5,13},{6,14},{7,15},{8,0},{9,1},... | collective-permute-start | bytes 761864 | tf_op jit(solution)/shard_map/ppermute | solution.py:123
  71.0 8.6 %collective-permute-start.29 = (bf16[1008,128]{1,0:T(8,128)(2,1)S(1)}, bf16[1008,128]{1,0:T(8,128)(2,1)S(1)}, u32[]{:S(2)}, u32[]{:S(2)}) collective-permute-start(bf16[1008,128]{1,0:T(8,128)(2,1)S(1)} %collective-permute-done.15), channel_id=1, source_target_pairs={{0,8},{1,9},{2,3},{3,2},{4,5},{5,4},{6,14},{7,15},{8,0},{9,1},{10,... | collective-permute-start | bytes 774152 | tf_op jit(solution)/shard_map/ppermute | solution.py:123
  71.1 1.9 %collective-permute-start.23 = (bf16[1008,128]{1,0:T(8,128)(2,1)S(1)}, bf16[1008,128]{1,0:T(8,128)(2,1)S(1)}, u32[]{:S(2)}, u32[]{:S(2)}) collective-permute-start(bf16[1008,128]{1,0:T(8,128)(2,1)S(1)} %collective-permute-done.22), channel_id=1, source_target_pairs={{0,8},{1,9},{2,10},{3,11},{4,12},{5,13},{6,14},{7,15},{8,0},{9,1},... | collective-permute-start | bytes 774152 | tf_op jit(solution)/shard_map/ppermute | solution.py:123
  73.7 9.5 %collective-permute-start.27 = (f16[128,4,128]{2,1,0:T(4,128)(2,1)S(1)}, f16[128,4,128]{2,1,0:T(4,128)(2,1)S(1)}, u32[]{:S(2)}, u32[]{:S(2)}) collective-permute-start(f16[128,4,128]{2,1,0:T(4,128)(2,1)S(1)} %fusion.13), channel_id=1, source_target_pairs={{0,2},{1,3},{2,0},{3,1},{4,6},{5,7},{6,4},{7,5},{8,10},{9,11},{10,... | collective-permute-start | bytes 393224 | tf_op jit(solution)/shard_map/ppermute | solution.py:123
  79.5 6.5 %collective-permute-start.24 = (f16[128,4,128]{2,1,0:T(4,128)(2,1)S(1)}, f16[128,4,128]{2,1,0:T(4,128)(2,1)S(1)}, u32[]{:S(2)}, u32[]{:S(2)}) collective-permute-start(f16[128,4,128]{2,1,0:T(4,128)(2,1)S(1)} %fusion.15), channel_id=1, source_target_pairs={{0,2},{1,3},{2,0},{3,1},{4,6},{5,7},{6,4},{7,5},{8,10},{9,11},{10,... | collective-permute-start | bytes 393224 | tf_op jit(solution)/shard_map/ppermute | solution.py:123
  80.3 8.0 %collective-permute-start.30 = (f16[128,4,128]{2,1,0:T(4,128)(2,1)S(1)}, f16[128,4,128]{2,1,0:T(4,128)(2,1)S(1)}, u32[]{:S(2)}, u32[]{:S(2)}) collective-permute-start(f16[128,4,128]{2,1,0:T(4,128)(2,1)S(1)} %fusion.11), channel_id=1, source_target_pairs={{0,2},{1,3},{2,0},{3,1},{4,6},{5,7},{6,4},{7,5},{8,10},{9,11},{10,... | collective-permute-start | bytes 393224 | tf_op jit(solution)/shard_map/ppermute | solution.py:123

commit v7 on v6

--- a/solution.py
+++ b/solution.py
@@ -1,5 +1,4 @@
 import functools
-
 import jax
 import jax.numpy as jnp
 from jax import lax
@@ -11,6 +10,15 @@
 AXES = ("grp", "col")
 LINE = 4
 SCALE = 32768.0
+ORDER = (
+    "head0", "pair0", "across0", "own0", "head1", "pair1", "across1", "own1",
+    "unitcore0", "unitcore1",
+    "relay0", "end0", "turn0", "headpair0", "relay1", "end1", "turn1", "headpair1",
+    "own2", "crossed0", "owncore0", "owncore1", "paircore0", "paircore1", "endcore0",
+    "early*", "far0", "endcore1", "far1", "ends*", "relay>", "turn>",
+    "rest*", "unit*", "pair*", "head*", "across*", "relay*", "far>",
+    "headpair*", "turn*", "far*",
+)
 
 
 VMEM = pl.BlockSpec(memory_space=pltpu.VMEM)
@@ -42,29 +50,32 @@
 def store_kernel(count, slots, *refs):
     panels, out, sems = refs[:count], refs[count], refs[count + 1]
 
-    def copy(i):
-        return pltpu.make_async_copy(panels[i], out.at[slots[i]], sems.at[i])
-
-    for i in range(count):
-        copy(i).start()
-    for i in range(count):
-        copy(i).wait()
+    def copy(i, a):
+        return pltpu.make_async_copy(
+            panels[i].at[a], out.at[slots[i], :, a, :], sems.at[i, a]
+        )
+
+    pairs = [(i, a) for i in range(count) for a in range(out.shape[2])]
+    for pair in pairs:
+        copy(*pair).start()
+    for pair in pairs:
+        copy(*pair).wait()
 
 
 def store(panels, slots, length):
-    count, shape = len(panels), panels[0].shape
-    size = count * panels[0].size
+    count, (rows, nparts, size) = len(panels), panels[0].shape
+    total = count * panels[0].size
     return pl.pallas_call(
         functools.partial(store_kernel, count),
-        out_shape=jax.ShapeDtypeStruct((length,) + shape, panels[0].dtype),
+        out_shape=jax.ShapeDtypeStruct((length, rows, nparts, size), panels[0].dtype),
         in_specs=[pl.BlockSpec(memory_space=pltpu.SMEM)]
         + [pl.BlockSpec(memory_space=pl.ANY)] * count,
         out_specs=pl.BlockSpec(memory_space=pltpu.HBM),
-        scratch_shapes=[pltpu.SemaphoreType.DMA((count,))],
-        cost_estimate=pl.CostEstimate(flops=0, bytes_accessed=8 * size, transcendentals=0),
+        scratch_shapes=[pltpu.SemaphoreType.DMA((count, nparts))],
+        cost_estimate=pl.CostEstimate(flops=0, bytes_accessed=8 * total, transcendentals=0),
         compiler_params=pltpu.CompilerParams(vmem_limit_bytes=2**20),
         name="store",
-    )(slots, *panels)
+    )(slots, *[panel.transpose(1, 0, 2) for panel in panels])
 
 
 def shards(descriptors):
@@ -144,65 +155,23 @@
     def other_core(j):
         return lambda g, zz, xx: (((g ^ 1) - j) % ngroups, zz, xx)
 
+    quarter = unit[1].shape[0] // 32 * 16
     head, pair, relay, head_pair = ([None, None] for _ in range(4))
-    across, centre_across = ([[None, None] for _ in offsets] for _ in range(2))
+    across, centre_across, far = ([[None, None] for _ in offsets] for _ in range(3))
     across_pair = [[None, None] for _ in range(2, inner)]
-    quarter = unit[1].shape[0] // 32 * 16
-    own = {0: [(0, unit[0]), (cut, unit[1])]}
-    end = {0: []}
-    for j in others:
-        own[j], end[j] = [], []
-    for h in halves:
-        head[h] = send(unit[h], centre_swap(1))
-        pair[h] = send(unit[h], line_swap)
-        for k in offsets:
-            across[k - 1][h] = send(unit[h], shift(k, k + 1))
-        for j in others:
-            own[j].append((h * cut, send(unit[h] if h == 0 else unit[1][:quarter], other(j))))
-    swapped = {("own", 0, h): send(unit[h], core_swap) for h in halves}
-    for h in halves:
-        end[0].append((h * cut, pair[h]))
-        for j in others:
-            end[j].append((h * cut, send(pair[h], other(j))))
-        relay[h] = send(pair[h], centre_swap(inner - 1))
-        for k in offsets:
-            centre_across[k - 1][h] = send(head[h], shift(k, 0))
-        head_pair[h] = send(head[h], line_swap)
-        for k in range(2, inner):
-            across_pair[k - 2][h] = send(across[k - 2][h], line_swap)
-    for j in others:
-        own[j].append((cut + quarter, send(unit[1][quarter:], other(j))))
-        swapped["own", j, 2] = send(unit[1][quarter:], other_core(j))
-
-    def swap_cores(name, parts, j, i):
-        swapped[name, j, i] = send(parts[j][i][1], core_swap)
-
-    for j in others:
-        swap_cores("own", own, j, 0)
-        swap_cores("own", own, j, 1)
-    swap_cores("end", end, 0, 0)
-    swap_cores("end", end, 0, 1)
-    for j in others:
-        swap_cores("end", end, j, 0)
-    far_across = [[None, None] for _ in offsets]
-    for k in offsets:
-        source = head_pair if k == 1 else across_pair[k - 2]
-        far_across[k - 1][0] = send(source[0], centre_swap(0))
-    for j in others:
-        swap_cores("end", end, j, 1)
-    for k in offsets:
-        far_across[k - 1][1] = send(relay[1], shift(k, 0))
-
-    def place(full, name, parts, last):
-        for j in sorted(parts):
-            for i, (row, part) in enumerate(parts[j]):
-                if (name == "own" and i == 2) != last:
-                    continue
-                pieces = ((part, at["own", j]), (swapped[name, j, i], at["swapped", j]))
-                for array, index in pieces:
-                    full = lax.dynamic_update_slice(
-                        full, array[None], (index, row, 0), allow_negative_indices=False
-                    )
+    own = {j: [None, None, None] for j in others}
+    end = {j: [None, None] for j in others}
+    own_swapped = {j: [None, None, None] for j in range(0, ngroups, 2)}
+    end_swapped = {j: [None, None] for j in range(0, ngroups, 2)}
+    columns = {}
+    values = {}
+    panels = {}
+
+    def place(full, row, part, swapped, j):
+        for array, index in ((part, at["own", j]), (swapped, at["swapped", j])):
+            full = lax.dynamic_update_slice(
+                full, array[None], (index, row, 0), allow_negative_indices=False
+            )
         return full
 
     def fourth(block, cols):
@@ -216,40 +185,128 @@
         return second * second
 
     def product(block):
-        return lax.optimization_barrier(fourth(block, columns))
-
-    def put(out, value, index):
-        return lax.dynamic_update_index_in_dim(
-            out, value, index, 0, allow_negative_indices=False
+        return lax.optimization_barrier(fourth(block, columns["own"]))
+
+    def fill_early():
+        full = jnp.zeros((ngroups,) + data.shape, jnp.bfloat16)
+        for h in halves:
+            full = place(full, h * cut, unit[h], own_swapped[0][h], 0)
+            for j in others:
+                full = place(full, h * cut, own[j][h], own_swapped[j][h], j)
+        columns["own"] = full
+
+    def fill_rest():
+        for j in others:
+            full = columns["own"]
+            columns["own"] = place(full, cut + quarter, own[j][2], own_swapped[j][2], j)
+
+    def fill_end():
+        full = jnp.zeros((ngroups,) + data.shape, jnp.bfloat16)
+        for h in halves:
+            full = place(full, h * cut, pair[h], end_swapped[0][h], 0)
+            for j in others:
+                full = place(full, h * cut, end[j][h], end_swapped[j][h], j)
+        columns["end"] = full
+
+    def piece(i):
+        return (unit[0], unit[1][:quarter], unit[1][quarter:])[i]
+
+    def run(name):
+        what, h = (name[:-1], int(name[-1])) if name[-1].isdigit() else ("", 0)
+        if what == "head":
+            head[h] = send(unit[h], centre_swap(1))
+        elif what == "pair":
+            pair[h] = send(unit[h], line_swap)
+        elif what == "across":
+            for k in offsets:
+                across[k - 1][h] = send(unit[h], shift(k, k + 1))
+        elif what == "own":
+            for j in others:
+                own[j][h] = send(piece(h), other(j))
+        elif what == "crossed":
+            for j in others:
+                own_swapped[j][2] = send(piece(2), other_core(j))
+        elif what == "unitcore":
+            own_swapped[0][h] = send(unit[h], core_swap)
+        elif what == "owncore":
+            for j in others:
+                own_swapped[j][h] = send(own[j][h], core_swap)
+        elif what == "paircore":
+            end_swapped[0][h] = send(pair[h], core_swap)
+        elif what == "endcore":
+            for j in others:
+                end_swapped[j][h] = send(end[j][h], core_swap)
+        elif what == "relay":
+            relay[h] = send(pair[h], centre_swap(inner - 1))
+        elif what == "turn":
+            for k in offsets:
+                centre_across[k - 1][h] = send(head[h], shift(k, 0))
+        elif what == "headpair":
+            head_pair[h] = send(head[h], line_swap)
+            for k in range(2, inner):
+                across_pair[k - 2][h] = send(across[k - 2][h], line_swap)
+        elif what == "end":
+            for j in others:
+                end[j][h] = send(pair[h], other(j))
+        elif what == "far":
+            for k in offsets:
+                source = head_pair if k == 1 else across_pair[k - 2]
+                if h == 0:
+                    far[k - 1][0] = send(source[0], centre_swap(0))
+                else:
+                    far[k - 1][1] = send(relay[1], shift(k, 0))
+        elif name == "early*":
+            fill_early()
+        elif name == "rest*":
+            fill_rest()
+        elif name == "ends*":
+            fill_end()
+        elif name == "unit*":
+            values["unit"] = product(unit)
+        elif name == "pair*":
+            values["pair"] = product(pair)
+        elif name == "head*":
+            values["head"] = product(head)
+        elif name == "across*":
+            for k in range(1, inner - 1):
+                values["across", k] = product(across[k - 1])
+            values["back", 0] = product(across[-1])
+        elif name == "headpair*":
+            values["head_pair"] = product(head_pair)
+            for k in range(2, inner):
+                values["across_pair", k] = product(across_pair[k - 2])
+        elif name == "relay*":
+            values["relay"] = product(relay)
+        elif name == "turn*":
+            for k in offsets:
+                values["back", k] = product(centre_across[k - 1])
+        elif name == "far*":
+            for k in offsets:
+                values["far", k] = product(far[k - 1])
+
+    def panel(block):
+        return (fourth(block, columns["end"]) * SCALE).astype(jnp.float16)
+
+    sources = {
+        "relay>": [(relay, ("back", 0))],
+        "turn>": [(b, ("back", k)) for k, b in zip(offsets, centre_across)],
+        "far>": [(b, ("far", k)) for k, b in zip(offsets, far)],
+    }
+    for name in ORDER:
+        if name in sources:
+            made = [(panel(b), key) for b, key in sources[name]]
+            for value, key in made:
+                panels[key] = send(value, line_swap)
+        else:
+            run(name)
+
+    for key, value in panels.items():
+        values[key] = jnp.where(middle, values[key], value.astype(jnp.float32) * (1.0 / SCALE))
+    out = store([values[key] for key in stored], slots, ncolumns)
+    for k in offsets:
+        out = lax.dynamic_update_index_in_dim(
+            out, values["far", k], at["far", k], 0, allow_negative_indices=False
         )
-
-    def back(block):
-        panel = (fourth(block, end_columns) * SCALE).astype(jnp.float16)
-        return send(panel, line_swap)
-
-    empty = jnp.zeros((ngroups,) + data.shape, jnp.bfloat16)
-    columns = place(empty, "own", own, False)
-    end_columns = place(empty, "end", end, False)
-    panels = [back(b) for b in [relay] + centre_across]
-    columns = place(columns, "own", own, True)
-    ready = [(product(unit), "unit"), (product(pair), "pair"), (product(head), "head")]
-    ready += [(product(across[k - 1]), ("across", k)) for k in range(1, inner - 1)]
-    mine = [product(across[-1])]
-    ready += [(product(relay), "relay")]
-    panels += [back(b) for b in far_across]
-    ready += [(product(head_pair), "head_pair")]
-    ready += [(product(across_pair[k - 2]), ("across_pair", k)) for k in range(2, inner)]
-    mine += [product(b) for b in centre_across]
-    mine += [product(b) for b in far_across]
-    merged = [
-        jnp.where(middle, value, panel.astype(jnp.float32) * (1.0 / SCALE))
-        for value, panel in zip(mine, panels)
-    ]
-    ready += [(value, ("back", k)) for k, value in enumerate(merged[:inner])]
-    ready.sort(key=lambda item: stored.index(item[1]))
-    out = store([value for value, _ in ready], slots, ncolumns)
-    for k in offsets:
-        out = put(out, merged[inner + k - 1], at["far", k])
     return out.reshape(ncolumns * block, ngroups, block)
 
 

time: 89.2 us -> 80.3 us (0.900)
  waiting for transfers between devices: 34.7 us -> 22.1 us
  starting transfers between devices: 41 us -> 46.6 us
  other arithmetic: 2.94 us -> 0.11 us
    ppermute x31, waiting for transfers between devices: 34.7 us -> 22.1 us  [send(): return lax.ppermute(array, AXES, pairs)]
    ppermute x31, starting transfers between devices: 41 us -> 46.6 us  [send(): return lax.ppermute(array, AXES, pairs)]
    mul x8 -> x0, other arithmetic: 1.38 us -> none  [fourth(): return second * second]
  transfers between devices with their start and end apart: 31 -> 31, of which waited for: 13 -> 13; matrix products, arithmetic and copies ran while one was open for 10% -> 8% of each run, Pallas kernels for 2% -> 2%
where the time goes in v7:
time: 80.3 us; the launch traced here: 80.2 us
  starting transfers between devices  46.6 us (58%)
  waiting for transfers between devices  22.1 us (28%)
  matrix products  5.3 us (7%)
  local copies, waits for them, and re-layouts  3.34 us (4%)
  Pallas kernels  2.32 us (3%)
    ppermute x31, starting transfers between devices, send(): return lax.ppermute(array, AXES, pairs)  46.6 us
    ppermute x31, waiting for transfers between devices, send(): return lax.ppermute(array, AXES, pairs)  22.1 us
    dot_general x11, matrix products, fourth(): lax.dot_general(jnp.concatenate(block, axis=0), cols, (((0,), (1,)), ((),...  5.3 us
    pallas_call x1, Pallas kernels, store(): pl.pallas_call(functools.partial(store_kernel, count), out_shape=jax.Shap...  1.99 us
  transfers between devices with their start and end apart: 31, of which 13 were waited for; matrix products, arithmetic and copies ran while one was open for 8% of the time, Pallas kernels for 2%

profile of v7, /device:TPU:0, one launch (start us, length us, event | category | flops | bytes accessed | tf_op | source)
XLA Modules:
  0.0 80.2 jit_solution(477636580926693292)
XLA Ops:
  0.0 1.2 %copy-done = f32[128,2000]{0,1:T(8,128)S(1)} copy-done((f32[128,2000]{0,1:T(8,128)S(1)}, f32[128,2000]{0,1:T(8,128)}, u32[]{:S(2)}) %copy-start) | copy-done | bytes 1024024
  1.2 0.3 normalize.1
  1.7 3.1 %collective-permute-start.8 = (bf16[992,128]{1,0:T(8,128)(2,1)S(1)}, bf16[992,128]{1,0:T(8,128)(2,1)S(1)}, u32[]{:S(2)}, u32[]{:S(2)}) collective-permute-start(bf16[992,128]{1,0:T(8,128)(2,1)S(1)} %get-tuple-element.19), channel_id=1, source_target_pairs={{0,2},{1,3},{2,0},{3,1},{4,6},{5,7},{6,4},{7,5},{8,10},{9,11},{10,... | collective-permute-start | bytes 761864 | tf_op jit(solution)/shard_map/ppermute | solution.py:134
  4.7 1.5 %collective-permute-start.10 = (bf16[992,128]{1,0:T(8,128)(2,1)S(1)}, bf16[992,128]{1,0:T(8,128)(2,1)S(1)}, u32[]{:S(2)}, u32[]{:S(2)}) collective-permute-start(bf16[992,128]{1,0:T(8,128)(2,1)S(1)} %get-tuple-element.19), channel_id=1, source_target_pairs={{0,1},{1,0},{2,4},{3,5},{4,2},{5,3},{6,7},{7,6},{8,9},{9,8},{10,12... | collective-permute-start | bytes 761864 | tf_op jit(solution)/shard_map/ppermute | solution.py:134
  6.2 1.5 %collective-permute-start.1 = (bf16[992,128]{1,0:T(8,128)(2,1)S(1)}, bf16[992,128]{1,0:T(8,128)(2,1)S(1)}, u32[]{:S(2)}, u32[]{:S(2)}) collective-permute-start(bf16[992,128]{1,0:T(8,128)(2,1)S(1)} %get-tuple-element.19), channel_id=1, source_target_pairs={{0,16},{1,17},{2,18},{3,19},{4,20},{5,21},{6,22},{7,23},{8,24},{9,... | collective-permute-start | bytes 761864 | tf_op jit(solution)/shard_map/ppermute | solution.py:134
  7.8 1.7 %collective-permute-start.9 = (bf16[1008,128]{1,0:T(8,128)(2,1)S(1)}, bf16[1008,128]{1,0:T(8,128)(2,1)S(1)}, u32[]{:S(2)}, u32[]{:S(2)}) collective-permute-start(bf16[1008,128]{1,0:T(8,128)(2,1)S(1)} %get-tuple-element.20), channel_id=1, source_target_pairs={{0,2},{1,3},{2,0},{3,1},{4,6},{5,7},{6,4},{7,5},{8,10},{9,11},{10,... | collective-permute-start | bytes 774152 | tf_op jit(solution)/shard_map/ppermute | solution.py:134
  9.4 0.3 broadcast.17.clone
  9.8 1.4 %collective-permute-done.8 = bf16[992,128]{1,0:T(8,128)(2,1)S(1)} collective-permute-done((bf16[992,128]{1,0:T(8,128)(2,1)S(1)}, bf16[992,128]{1,0:T(8,128)(2,1)S(1)}, u32[]{:S(2)}, u32[]{:S(2)}) %collective-permute-start.8) | collective-permute-done | bytes 253984 | tf_op jit(solution)/shard_map/ppermute | solution.py:134
  11.2 0.3 broadcast.17.clone.1
  11.5 2.6 %collective-permute-start.4 = (bf16[496,128]{1,0:T(8,128)(2,1)S(1)}, bf16[496,128]{1,0:T(8,128)(2,1)S(1)}, u32[]{:S(2)}, u32[]{:S(2)}) collective-permute-start(bf16[496,128]{1,0:T(8,128)(2,1)S(1)} %slice.7), channel_id=1, source_target_pairs={{0,16},{1,17},{2,18},{3,19},{4,20},{5,21},{6,22},{7,23},{8,24},{9,... | collective-permute-start | bytes 380936 | tf_op jit(solution)/shard_map/ppermute | solution.py:134
  14.1 0.7 collective-permute-done.1
  14.9 1.4 %collective-permute-done.2 = bf16[992,128]{1,0:T(8,128)(2,1)S(1)} collective-permute-done((bf16[992,128]{1,0:T(8,128)(2,1)S(1)}, bf16[992,128]{1,0:T(8,128)(2,1)S(1)}, u32[]{:S(2)}, u32[]{:S(2)}) %collective-permute-start.2) | collective-permute-done | bytes 253984 | tf_op jit(solution)/shard_map/ppermute | solution.py:134
  16.3 1.5 %collective-permute-start.6 = (bf16[512,128]{1,0:T(8,128)(2,1)S(1)}, bf16[512,128]{1,0:T(8,128)(2,1)S(1)}, u32[]{:S(2)}, u32[]{:S(2)}) collective-permute-start(bf16[512,128]{1,0:T(8,128)(2,1)S(1)} %slice.8), channel_id=1, source_target_pairs={{0,16},{1,17},{2,18},{3,19},{4,20},{5,21},{6,22},{7,23},{8,24},{9,... | collective-permute-start | bytes 393224 | tf_op jit(solution)/shard_map/ppermute | solution.py:134
  18.2 1.0 %collective-permute-start.7 = (bf16[512,128]{1,0:T(8,128)(2,1)S(1)}, bf16[512,128]{1,0:T(8,128)(2,1)S(1)}, u32[]{:S(2)}, u32[]{:S(2)}) collective-permute-start(bf16[512,128]{1,0:T(8,128)(2,1)S(1)} %slice.8), channel_id=1, source_target_pairs={{0,24},{1,25},{2,26},{3,27},{4,28},{5,29},{6,30},{7,31},{8,16},{9,... | collective-permute-start | bytes 393224 | tf_op jit(solution)/shard_map/ppermute | solution.py:134
  19.2 0.9 %collective-permute-start.5 = (bf16[496,128]{1,0:T(8,128)(2,1)S(1)}, bf16[496,128]{1,0:T(8,128)(2,1)S(1)}, u32[]{:S(2)}, u32[]{:S(2)}) collective-permute-start(bf16[496,128]{1,0:T(8,128)(2,1)S(1)} %collective-permute-done.4), channel_id=1, source_target_pairs={{0,8},{1,9},{2,10},{3,11},{4,12},{5,13},{6,14},{7,15},{8,0},{9,1},... | collective-permute-start | bytes 380936 | tf_op jit(solution)/shard_map/ppermute | solution.py:134
  20.1 0.9 %collective-permute-done.5 = bf16[496,128]{1,0:T(8,128)(2,1)S(1)} collective-permute-done((bf16[496,128]{1,0:T(8,128)(2,1)S(1)}, bf16[496,128]{1,0:T(8,128)(2,1)S(1)}, u32[]{:S(2)}, u32[]{:S(2)}) %collective-permute-start.5) | collective-permute-done | bytes 127008 | tf_op jit(solution)/shard_map/ppermute | solution.py:134
  21.0 1.8 %collective-permute-start.11 = (bf16[1008,128]{1,0:T(8,128)(2,1)S(1)}, bf16[1008,128]{1,0:T(8,128)(2,1)S(1)}, u32[]{:S(2)}, u32[]{:S(2)}) collective-permute-start(bf16[1008,128]{1,0:T(8,128)(2,1)S(1)} %get-tuple-element.20), channel_id=1, source_target_pairs={{0,1},{1,0},{2,4},{3,5},{4,2},{5,3},{6,7},{7,6},{8,9},{9,8},{10,12... | collective-permute-start | bytes 774152 | tf_op jit(solution)/shard_map/ppermute | solution.py:134
  23.0 1.0 %collective-permute-done.7 = bf16[512,128]{1,0:T(8,128)(2,1)S(1)} collective-permute-done((bf16[512,128]{1,0:T(8,128)(2,1)S(1)}, bf16[512,128]{1,0:T(8,128)(2,1)S(1)}, u32[]{:S(2)}, u32[]{:S(2)}) %collective-permute-start.7) | collective-permute-done | bytes 131104 | tf_op jit(solution)/shard_map/ppermute | solution.py:134
  24.0 0.8 %collective-permute-start.16 = (bf16[992,128]{1,0:T(8,128)(2,1)S(1)}, bf16[992,128]{1,0:T(8,128)(2,1)S(1)}, u32[]{:S(2)}, u32[]{:S(2)}) collective-permute-start(bf16[992,128]{1,0:T(8,128)(2,1)S(1)} %get-tuple-element.19), channel_id=1, source_target_pairs={{0,8},{1,9},{2,3},{3,2},{4,5},{5,4},{6,14},{7,15},{8,0},{9,1},{10,... | collective-permute-start | bytes 761864 | tf_op jit(solution)/shard_map/ppermute | solution.py:134
  24.8 0.5 fusion.10
  25.4 4.2 %collective-permute-done.11 = bf16[1008,128]{1,0:T(8,128)(2,1)S(1)} collective-permute-done((bf16[1008,128]{1,0:T(8,128)(2,1)S(1)}, bf16[1008,128]{1,0:T(8,128)(2,1)S(1)}, u32[]{:S(2)}, u32[]{:S(2)}) %collective-permute-start.11) | collective-permute-done | bytes 258080 | tf_op jit(solution)/shard_map/ppermute | solution.py:134
  29.8 0.5 fusion.8
  30.3 1.7 %collective-permute-start.12 = (bf16[992,128]{1,0:T(8,128)(2,1)S(1)}, bf16[992,128]{1,0:T(8,128)(2,1)S(1)}, u32[]{:S(2)}, u32[]{:S(2)}) collective-permute-start(bf16[992,128]{1,0:T(8,128)(2,1)S(1)} %collective-permute-done.10), channel_id=1, source_target_pairs={{0,2},{1,3},{2,0},{3,1},{4,6},{5,7},{6,4},{7,5},{8,10},{9,11},{10,... | collective-permute-start | bytes 761864 | tf_op jit(solution)/shard_map/ppermute | solution.py:134
  32.0 0.5 fusion.9
  32.5 1.6 %collective-permute-start.14 = (bf16[992,128]{1,0:T(8,128)(2,1)S(1)}, bf16[992,128]{1,0:T(8,128)(2,1)S(1)}, u32[]{:S(2)}, u32[]{:S(2)}) collective-permute-start(bf16[992,128]{1,0:T(8,128)(2,1)S(1)} %collective-permute-done.8), channel_id=1, source_target_pairs={{0,1},{1,0},{2,4},{3,5},{4,2},{5,3},{6,7},{7,6},{8,9},{9,8},{10,12... | collective-permute-start | bytes 761864 | tf_op jit(solution)/shard_map/ppermute | solution.py:134
  34.1 0.5 fusion.5
  34.9 2.3 %collective-permute-done.19 = bf16[992,128]{1,0:T(8,128)(2,1)S(1)} collective-permute-done((bf16[992,128]{1,0:T(8,128)(2,1)S(1)}, bf16[992,128]{1,0:T(8,128)(2,1)S(1)}, u32[]{:S(2)}, u32[]{:S(2)}) %collective-permute-start.19) | collective-permute-done | bytes 253984 | tf_op jit(solution)/shard_map/ppermute | solution.py:134
  37.2 0.3 collective-permute-start.22
  37.5 13.6 %collective-permute-start.13 = (bf16[1008,128]{1,0:T(8,128)(2,1)S(1)}, bf16[1008,128]{1,0:T(8,128)(2,1)S(1)}, u32[]{:S(2)}, u32[]{:S(2)}) collective-permute-start(bf16[1008,128]{1,0:T(8,128)(2,1)S(1)} %collective-permute-done.11), channel_id=1, source_target_pairs={{0,2},{1,3},{2,0},{3,1},{4,6},{5,7},{6,4},{7,5},{8,10},{9,11},{10,... | collective-permute-start | bytes 774152 | tf_op jit(solution)/shard_map/ppermute | solution.py:134
  51.1 0.5 fusion.3
  51.6 1.6 %collective-permute-start.15 = (bf16[1008,128]{1,0:T(8,128)(2,1)S(1)}, bf16[1008,128]{1,0:T(8,128)(2,1)S(1)}, u32[]{:S(2)}, u32[]{:S(2)}) collective-permute-start(bf16[1008,128]{1,0:T(8,128)(2,1)S(1)} %collective-permute-done.9), channel_id=1, source_target_pairs={{0,1},{1,0},{2,4},{3,5},{4,2},{5,3},{6,7},{7,6},{8,9},{9,8},{10,12... | collective-permute-start | bytes 774152 | tf_op jit(solution)/shard_map/ppermute | solution.py:134
  53.2 2.7 %collective-permute-done.13 = bf16[1008,128]{1,0:T(8,128)(2,1)S(1)} collective-permute-done((bf16[1008,128]{1,0:T(8,128)(2,1)S(1)}, bf16[1008,128]{1,0:T(8,128)(2,1)S(1)}, u32[]{:S(2)}, u32[]{:S(2)}) %collective-permute-start.13) | collective-permute-done | bytes 258080 | tf_op jit(solution)/shard_map/ppermute | solution.py:134
  55.9 0.5 fusion.7
  56.4 0.6 collective-permute-start.28
  57.0 1.1 %collective-permute-done.15 = bf16[1008,128]{1,0:T(8,128)(2,1)S(1)} collective-permute-done((bf16[1008,128]{1,0:T(8,128)(2,1)S(1)}, bf16[1008,128]{1,0:T(8,128)(2,1)S(1)}, u32[]{:S(2)}, u32[]{:S(2)}) %collective-permute-start.15) | collective-permute-done | bytes 258080 | tf_op jit(solution)/shard_map/ppermute | solution.py:134
  58.0 0.5 fusion.6
  58.6 0.5 collective-permute-start.23
  59.3 1.2 %collective-permute-done.23 = bf16[1008,128]{1,0:T(8,128)(2,1)S(1)} collective-permute-done((bf16[1008,128]{1,0:T(8,128)(2,1)S(1)}, bf16[1008,128]{1,0:T(8,128)(2,1)S(1)}, u32[]{:S(2)}, u32[]{:S(2)}) %collective-permute-start.23) | collective-permute-done | bytes 258080 | tf_op jit(solution)/shard_map/ppermute | solution.py:134
  60.6 0.5 fusion.14
  61.0 7.5 %collective-permute-start.30 = (f16[128,4,128]{2,0,1:T(8,128)(2,1)S(1)}, f16[128,4,128]{2,0,1:T(8,128)(2,1)S(1)}, u32[]{:S(2)}, u32[]{:S(2)}) collective-permute-start(f16[128,4,128]{2,0,1:T(8,128)(2,1)S(1)} %fusion.14), channel_id=1, source_target_pairs={{0,2},{1,3},{2,0},{3,1},{4,6},{5,7},{6,4},{7,5},{8,10},{9,11},{10,... | collective-permute-start | bytes 393224 | tf_op jit(solution)/shard_map/ppermute | solution.py:134
  68.5 0.5 fusion.15
  69.1 0.5 fusion.1
  69.6 0.5 fusion.16
  70.1 2.1 %collective-permute-start.24 = (f16[128,4,128]{2,0,1:T(8,128)(2,1)S(1)}, f16[128,4,128]{2,0,1:T(8,128)(2,1)S(1)}, u32[]{:S(2)}, u32[]{:S(2)}) collective-permute-start(f16[128,4,128]{2,0,1:T(8,128)(2,1)S(1)} %fusion.16), channel_id=1, source_target_pairs={{0,2},{1,3},{2,0},{3,1},{4,6},{5,7},{6,4},{7,5},{8,10},{9,11},{10,... | collective-permute-start | bytes 393224 | tf_op jit(solution)/shard_map/ppermute | solution.py:134
  72.2 3.3 %collective-permute-done.27 = f16[128,4,128]{2,0,1:T(8,128)(2,1)S(1)} collective-permute-done((f16[128,4,128]{2,0,1:T(8,128)(2,1)S(1)}, f16[128,4,128]{2,0,1:T(8,128)(2,1)S(1)}, u32[]{:S(2)}, u32[]{:S(2)}) %collective-permute-start.27) | collective-permute-done | bytes 131104 | tf_op jit(solution)/shard_map/ppermute | solution.py:134
  75.5 1.7 %collective-permute-done.24 = f16[128,4,128]{2,0,1:T(8,128)(2,1)S(1)} collective-permute-done((f16[128,4,128]{2,0,1:T(8,128)(2,1)S(1)}, f16[128,4,128]{2,0,1:T(8,128)(2,1)S(1)}, u32[]{:S(2)}, u32[]{:S(2)}) %collective-permute-start.24) | collective-permute-done | bytes 131104 | tf_op jit(solution)/shard_map/ppermute | solution.py:134
  77.2 2.0 %store.1 = f32[8,128,4,128]{3,2,1,0:T(4,128)} custom-call(s32[7]{0:T(128)S(1)} %stack.31.slots, f32[4,128,128]{2,1,0:T(8,128)S(1)} %bitcast.94, f32[4,128,128]{2,1,0:T(8,128)S(1)} %bitcast.96, f32[4,128,128]{2,1,0:T(8,128)S(1)} %bitcast.95, f32[4,128,128]{2,1,0:T(8,128)S(1)} %bitcast.97, f32[4,128,128]{2,1,0:T(8,128)S(1)} %bitcast.98, ...), custom_call_target="tpu_custom_call" | custom-call | bytes 3670016 | tf_op jit(solution)/shard_map/store/pallas_call | solution.py:68
  79.3 0.9 %copy_dynamic-update-slice_fusion = f32[8,128,4,128]{3,2,1,0:T(4,128)} fusion(f32[8,128,4,128]{3,2,1,0:T(4,128)} %store.1, s32[]{:T(128)S(6)} %select_n.106, f32[1,128,4,128]{3,1,2,0:T(8,128)S(1)} %select_bitcast_fusion), kind=kLoop, calls=%fused_computation.46 | loop fusion | bytes 524292 | tf_op jit(solution)/shard_map/jit(dynamic_update_index_in_dim)/dynamic_update_slice | solution.py:307
  (56 shorter events, 2.0 us)
Async XLA Ops:
  0.0 1.2 %copy-start = (f32[128,2000]{0,1:T(8,128)S(1)}, f32[128,2000]{0,1:T(8,128)}, u32[]{:S(2)}) copy-start(f32[128,2000]{0,1:T(8,128)} %param.1) | copy-start | bytes 3072004
  1.7 9.5 %collective-permute-start.8 = (bf16[992,128]{1,0:T(8,128)(2,1)S(1)}, bf16[992,128]{1,0:T(8,128)(2,1)S(1)}, u32[]{:S(2)}, u32[]{:S(2)}) collective-permute-start(bf16[992,128]{1,0:T(8,128)(2,1)S(1)} %get-tuple-element.19), channel_id=1, source_target_pairs={{0,2},{1,3},{2,0},{3,1},{4,6},{5,7},{6,4},{7,5},{8,10},{9,11},{10,... | collective-permute-start | bytes 761864 | tf_op jit(solution)/shard_map/ppermute | solution.py:134
  4.7 20.5 %collective-permute-start.10 = (bf16[992,128]{1,0:T(8,128)(2,1)S(1)}, bf16[992,128]{1,0:T(8,128)(2,1)S(1)}, u32[]{:S(2)}, u32[]{:S(2)}) collective-permute-start(bf16[992,128]{1,0:T(8,128)(2,1)S(1)} %get-tuple-element.19), channel_id=1, source_target_pairs={{0,1},{1,0},{2,4},{3,5},{4,2},{5,3},{6,7},{7,6},{8,9},{9,8},{10,12... | collective-permute-start | bytes 761864 | tf_op jit(solution)/shard_map/ppermute | solution.py:134
  6.2 5.3 %collective-permute-start = (bf16[992,128]{1,0:T(8,128)(2,1)S(1)}, bf16[992,128]{1,0:T(8,128)(2,1)S(1)}, u32[]{:S(2)}, u32[]{:S(2)}) collective-permute-start(bf16[992,128]{1,0:T(8,128)(2,1)S(1)} %get-tuple-element.19), channel_id=1, source_target_pairs={{0,8},{1,9},{2,10},{3,11},{4,12},{5,13},{6,14},{7,15},{8,0},{9,1},... | collective-permute-start | bytes 761864 | tf_op jit(solution)/shard_map/ppermute | solution.py:134
  6.2 8.5 %collective-permute-start.1 = (bf16[992,128]{1,0:T(8,128)(2,1)S(1)}, bf16[992,128]{1,0:T(8,128)(2,1)S(1)}, u32[]{:S(2)}, u32[]{:S(2)}) collective-permute-start(bf16[992,128]{1,0:T(8,128)(2,1)S(1)} %get-tuple-element.19), channel_id=1, source_target_pairs={{0,16},{1,17},{2,18},{3,19},{4,20},{5,21},{6,22},{7,23},{8,24},{9,... | collective-permute-start | bytes 761864 | tf_op jit(solution)/shard_map/ppermute | solution.py:134
  7.8 22.5 %collective-permute-start.9 = (bf16[1008,128]{1,0:T(8,128)(2,1)S(1)}, bf16[1008,128]{1,0:T(8,128)(2,1)S(1)}, u32[]{:S(2)}, u32[]{:S(2)}) collective-permute-start(bf16[1008,128]{1,0:T(8,128)(2,1)S(1)} %get-tuple-element.20), channel_id=1, source_target_pairs={{0,2},{1,3},{2,0},{3,1},{4,6},{5,7},{6,4},{7,5},{8,10},{9,11},{10,... | collective-permute-start | bytes 774152 | tf_op jit(solution)/shard_map/ppermute | solution.py:134
  11.2 8.0 %collective-permute-start.3 = (bf16[1008,128]{1,0:T(8,128)(2,1)S(1)}, bf16[1008,128]{1,0:T(8,128)(2,1)S(1)}, u32[]{:S(2)}, u32[]{:S(2)}) collective-permute-start(bf16[1008,128]{1,0:T(8,128)(2,1)S(1)} %get-tuple-element.20), channel_id=1, source_target_pairs={{0,8},{1,9},{2,10},{3,11},{4,12},{5,13},{6,14},{7,15},{8,0},{9,1},... | collective-permute-start | bytes 774152 | tf_op jit(solution)/shard_map/ppermute | solution.py:134
  11.5 6.7 %collective-permute-start.4 = (bf16[496,128]{1,0:T(8,128)(2,1)S(1)}, bf16[496,128]{1,0:T(8,128)(2,1)S(1)}, u32[]{:S(2)}, u32[]{:S(2)}) collective-permute-start(bf16[496,128]{1,0:T(8,128)(2,1)S(1)} %slice.7), channel_id=1, source_target_pairs={{0,16},{1,17},{2,18},{3,19},{4,20},{5,21},{6,22},{7,23},{8,24},{9,... | collective-permute-start | bytes 380936 | tf_op jit(solution)/shard_map/ppermute | solution.py:134
  14.8 1.5 %collective-permute-start.2 = (bf16[992,128]{1,0:T(8,128)(2,1)S(1)}, bf16[992,128]{1,0:T(8,128)(2,1)S(1)}, u32[]{:S(2)}, u32[]{:S(2)}) collective-permute-start(bf16[992,128]{1,0:T(8,128)(2,1)S(1)} %collective-permute-done.1), channel_id=1, source_target_pairs={{0,8},{1,9},{2,10},{3,11},{4,12},{5,13},{6,14},{7,15},{8,0},{9,1},... | collective-permute-start | bytes 761864 | tf_op jit(solution)/shard_map/ppermute | solution.py:134
  16.3 6.5 %collective-permute-start.6 = (bf16[512,128]{1,0:T(8,128)(2,1)S(1)}, bf16[512,128]{1,0:T(8,128)(2,1)S(1)}, u32[]{:S(2)}, u32[]{:S(2)}) collective-permute-start(bf16[512,128]{1,0:T(8,128)(2,1)S(1)} %slice.8), channel_id=1, source_target_pairs={{0,16},{1,17},{2,18},{3,19},{4,20},{5,21},{6,22},{7,23},{8,24},{9,... | collective-permute-start | bytes 393224 | tf_op jit(solution)/shard_map/ppermute | solution.py:134
  18.2 5.8 %collective-permute-start.7 = (bf16[512,128]{1,0:T(8,128)(2,1)S(1)}, bf16[512,128]{1,0:T(8,128)(2,1)S(1)}, u32[]{:S(2)}, u32[]{:S(2)}) collective-permute-start(bf16[512,128]{1,0:T(8,128)(2,1)S(1)} %slice.8), channel_id=1, source_target_pairs={{0,24},{1,25},{2,26},{3,27},{4,28},{5,29},{6,30},{7,31},{8,16},{9,... | collective-permute-start | bytes 393224 | tf_op jit(solution)/shard_map/ppermute | solution.py:134
  19.2 1.8 %collective-permute-start.5 = (bf16[496,128]{1,0:T(8,128)(2,1)S(1)}, bf16[496,128]{1,0:T(8,128)(2,1)S(1)}, u32[]{:S(2)}, u32[]{:S(2)}) collective-permute-start(bf16[496,128]{1,0:T(8,128)(2,1)S(1)} %collective-permute-done.4), channel_id=1, source_target_pairs={{0,8},{1,9},{2,10},{3,11},{4,12},{5,13},{6,14},{7,15},{8,0},{9,1},... | collective-permute-start | bytes 380936 | tf_op jit(solution)/shard_map/ppermute | solution.py:134
  21.0 8.5 %collective-permute-start.11 = (bf16[1008,128]{1,0:T(8,128)(2,1)S(1)}, bf16[1008,128]{1,0:T(8,128)(2,1)S(1)}, u32[]{:S(2)}, u32[]{:S(2)}) collective-permute-start(bf16[1008,128]{1,0:T(8,128)(2,1)S(1)} %get-tuple-element.20), channel_id=1, source_target_pairs={{0,1},{1,0},{2,4},{3,5},{4,2},{5,3},{6,7},{7,6},{8,9},{9,8},{10,12... | collective-permute-start | bytes 774152 | tf_op jit(solution)/shard_map/ppermute | solution.py:134
  22.8 9.7 %collective-permute-start.17 = (bf16[1008,128]{1,0:T(8,128)(2,1)S(1)}, bf16[1008,128]{1,0:T(8,128)(2,1)S(1)}, u32[]{:S(2)}, u32[]{:S(2)}) collective-permute-start(bf16[1008,128]{1,0:T(8,128)(2,1)S(1)} %get-tuple-element.20), channel_id=1, source_target_pairs={{0,8},{1,9},{2,3},{3,2},{4,5},{5,4},{6,14},{7,15},{8,0},{9,1},{10,... | collective-permute-start | bytes 774152 | tf_op jit(solution)/shard_map/ppermute | solution.py:134
  24.0 8.5 %collective-permute-start.16 = (bf16[992,128]{1,0:T(8,128)(2,1)S(1)}, bf16[992,128]{1,0:T(8,128)(2,1)S(1)}, u32[]{:S(2)}, u32[]{:S(2)}) collective-permute-start(bf16[992,128]{1,0:T(8,128)(2,1)S(1)} %get-tuple-element.19), channel_id=1, source_target_pairs={{0,8},{1,9},{2,3},{3,2},{4,5},{5,4},{6,14},{7,15},{8,0},{9,1},{10,... | collective-permute-start | bytes 761864 | tf_op jit(solution)/shard_map/ppermute | solution.py:134
  25.3 9.3 %collective-permute-start.18 = (bf16[992,128]{1,0:T(8,128)(2,1)S(1)}, bf16[992,128]{1,0:T(8,128)(2,1)S(1)}, u32[]{:S(2)}, u32[]{:S(2)}) collective-permute-start(bf16[992,128]{1,0:T(8,128)(2,1)S(1)} %collective-permute-done.8), channel_id=1, source_target_pairs={{0,8},{1,9},{2,10},{3,11},{4,12},{5,13},{6,14},{7,15},{8,0},{9,1},... | collective-permute-start | bytes 761864 | tf_op jit(solution)/shard_map/ppermute | solution.py:134
  29.5 7.6 %collective-permute-start.19 = (bf16[992,128]{1,0:T(8,128)(2,1)S(1)}, bf16[992,128]{1,0:T(8,128)(2,1)S(1)}, u32[]{:S(2)}, u32[]{:S(2)}) collective-permute-start(bf16[992,128]{1,0:T(8,128)(2,1)S(1)} %collective-permute-done.8), channel_id=1, source_target_pairs={{0,16},{1,17},{2,18},{3,19},{4,20},{5,21},{6,22},{7,23},{8,24},{9,... | collective-permute-start | bytes 761864 | tf_op jit(solution)/shard_map/ppermute | solution.py:134
  30.3 21.4 %collective-permute-start.12 = (bf16[992,128]{1,0:T(8,128)(2,1)S(1)}, bf16[992,128]{1,0:T(8,128)(2,1)S(1)}, u32[]{:S(2)}, u32[]{:S(2)}) collective-permute-start(bf16[992,128]{1,0:T(8,128)(2,1)S(1)} %collective-permute-done.10), channel_id=1, source_target_pairs={{0,2},{1,3},{2,0},{3,1},{4,6},{5,7},{6,4},{7,5},{8,10},{9,11},{10,... | collective-permute-start | bytes 761864 | tf_op jit(solution)/shard_map/ppermute | solution.py:134
  32.4 4.7 %collective-permute-start.25 = (bf16[992,128]{1,0:T(8,128)(2,1)S(1)}, bf16[992,128]{1,0:T(8,128)(2,1)S(1)}, u32[]{:S(2)}, u32[]{:S(2)}) collective-permute-start(bf16[992,128]{1,0:T(8,128)(2,1)S(1)} %collective-permute-done.10), channel_id=1, source_target_pairs={{0,8},{1,9},{2,3},{3,2},{4,5},{5,4},{6,14},{7,15},{8,0},{9,1},{10,... | collective-permute-start | bytes 761864 | tf_op jit(solution)/shard_map/ppermute | solution.py:134
  32.5 23.8 %collective-permute-start.14 = (bf16[992,128]{1,0:T(8,128)(2,1)S(1)}, bf16[992,128]{1,0:T(8,128)(2,1)S(1)}, u32[]{:S(2)}, u32[]{:S(2)}) collective-permute-start(bf16[992,128]{1,0:T(8,128)(2,1)S(1)} %collective-permute-done.8), channel_id=1, source_target_pairs={{0,1},{1,0},{2,4},{3,5},{4,2},{5,3},{6,7},{7,6},{8,9},{9,8},{10,12... | collective-permute-start | bytes 761864 | tf_op jit(solution)/shard_map/ppermute | solution.py:134
  34.6 2.9 %collective-permute-start.26 = (bf16[1008,128]{1,0:T(8,128)(2,1)S(1)}, bf16[1008,128]{1,0:T(8,128)(2,1)S(1)}, u32[]{:S(2)}, u32[]{:S(2)}) collective-permute-start(bf16[1008,128]{1,0:T(8,128)(2,1)S(1)} %collective-permute-done.11), channel_id=1, source_target_pairs={{0,8},{1,9},{2,3},{3,2},{4,5},{5,4},{6,14},{7,15},{8,0},{9,1},{10,... | collective-permute-start | bytes 774152 | tf_op jit(solution)/shard_map/ppermute | solution.py:134
  37.1 22.1 %collective-permute-start.21 = (bf16[1008,128]{1,0:T(8,128)(2,1)S(1)}, bf16[1008,128]{1,0:T(8,128)(2,1)S(1)}, u32[]{:S(2)}, u32[]{:S(2)}) collective-permute-start(bf16[1008,128]{1,0:T(8,128)(2,1)S(1)} %collective-permute-done.9), channel_id=1, source_target_pairs={{0,8},{1,9},{2,10},{3,11},{4,12},{5,13},{6,14},{7,15},{8,0},{9,1},... | collective-permute-start | bytes 774152 | tf_op jit(solution)/shard_map/ppermute | solution.py:134
  37.2 21.4 %collective-permute-start.22 = (bf16[1008,128]{1,0:T(8,128)(2,1)S(1)}, bf16[1008,128]{1,0:T(8,128)(2,1)S(1)}, u32[]{:S(2)}, u32[]{:S(2)}) collective-permute-start(bf16[1008,128]{1,0:T(8,128)(2,1)S(1)} %collective-permute-done.9), channel_id=1, source_target_pairs={{0,16},{1,17},{2,18},{3,19},{4,20},{5,21},{6,22},{7,23},{8,24},{9,... | collective-permute-start | bytes 774152 | tf_op jit(solution)/shard_map/ppermute | solution.py:134
  37.5 18.4 %collective-permute-start.13 = (bf16[1008,128]{1,0:T(8,128)(2,1)S(1)}, bf16[1008,128]{1,0:T(8,128)(2,1)S(1)}, u32[]{:S(2)}, u32[]{:S(2)}) collective-permute-start(bf16[1008,128]{1,0:T(8,128)(2,1)S(1)} %collective-permute-done.11), channel_id=1, source_target_pairs={{0,2},{1,3},{2,0},{3,1},{4,6},{5,7},{6,4},{7,5},{8,10},{9,11},{10,... | collective-permute-start | bytes 774152 | tf_op jit(solution)/shard_map/ppermute | solution.py:134
  51.6 6.4 %collective-permute-start.15 = (bf16[1008,128]{1,0:T(8,128)(2,1)S(1)}, bf16[1008,128]{1,0:T(8,128)(2,1)S(1)}, u32[]{:S(2)}, u32[]{:S(2)}) collective-permute-start(bf16[1008,128]{1,0:T(8,128)(2,1)S(1)} %collective-permute-done.9), channel_id=1, source_target_pairs={{0,1},{1,0},{2,4},{3,5},{4,2},{5,3},{6,7},{7,6},{8,9},{9,8},{10,12... | collective-permute-start | bytes 774152 | tf_op jit(solution)/shard_map/ppermute | solution.py:134
  55.9 3.2 %collective-permute-start.20 = (bf16[992,128]{1,0:T(8,128)(2,1)S(1)}, bf16[992,128]{1,0:T(8,128)(2,1)S(1)}, u32[]{:S(2)}, u32[]{:S(2)}) collective-permute-start(bf16[992,128]{1,0:T(8,128)(2,1)S(1)} %collective-permute-done.19), channel_id=1, source_target_pairs={{0,8},{1,9},{2,10},{3,11},{4,12},{5,13},{6,14},{7,15},{8,0},{9,1},... | collective-permute-start | bytes 761864 | tf_op jit(solution)/shard_map/ppermute | solution.py:134
  56.4 4.1 %collective-permute-start.28 = (bf16[992,128]{1,0:T(8,128)(2,1)S(1)}, bf16[992,128]{1,0:T(8,128)(2,1)S(1)}, u32[]{:S(2)}, u32[]{:S(2)}) collective-permute-start(bf16[992,128]{1,0:T(8,128)(2,1)S(1)} %collective-permute-done.12), channel_id=1, source_target_pairs={{0,8},{1,9},{2,4},{3,5},{4,2},{5,3},{6,14},{7,15},{8,0},{9,1},{10,... | collective-permute-start | bytes 761864 | tf_op jit(solution)/shard_map/ppermute | solution.py:134
  58.5 2.0 %collective-permute-start.29 = (bf16[1008,128]{1,0:T(8,128)(2,1)S(1)}, bf16[1008,128]{1,0:T(8,128)(2,1)S(1)}, u32[]{:S(2)}, u32[]{:S(2)}) collective-permute-start(bf16[1008,128]{1,0:T(8,128)(2,1)S(1)} %collective-permute-done.15), channel_id=1, source_target_pairs={{0,8},{1,9},{2,3},{3,2},{4,5},{5,4},{6,14},{7,15},{8,0},{9,1},{10,... | collective-permute-start | bytes 774152 | tf_op jit(solution)/shard_map/ppermute | solution.py:134
  58.6 1.9 %collective-permute-start.23 = (bf16[1008,128]{1,0:T(8,128)(2,1)S(1)}, bf16[1008,128]{1,0:T(8,128)(2,1)S(1)}, u32[]{:S(2)}, u32[]{:S(2)}) collective-permute-start(bf16[1008,128]{1,0:T(8,128)(2,1)S(1)} %collective-permute-done.22), channel_id=1, source_target_pairs={{0,8},{1,9},{2,10},{3,11},{4,12},{5,13},{6,14},{7,15},{8,0},{9,1},... | collective-permute-start | bytes 774152 | tf_op jit(solution)/shard_map/ppermute | solution.py:134
  61.0 18.2 %collective-permute-start.30 = (f16[128,4,128]{2,0,1:T(8,128)(2,1)S(1)}, f16[128,4,128]{2,0,1:T(8,128)(2,1)S(1)}, u32[]{:S(2)}, u32[]{:S(2)}) collective-permute-start(f16[128,4,128]{2,0,1:T(8,128)(2,1)S(1)} %fusion.14), channel_id=1, source_target_pairs={{0,2},{1,3},{2,0},{3,1},{4,6},{5,7},{6,4},{7,5},{8,10},{9,11},{10,... | collective-permute-start | bytes 393224 | tf_op jit(solution)/shard_map/ppermute | solution.py:134
  69.0 6.4 %collective-permute-start.27 = (f16[128,4,128]{2,0,1:T(8,128)(2,1)S(1)}, f16[128,4,128]{2,0,1:T(8,128)(2,1)S(1)}, u32[]{:S(2)}, u32[]{:S(2)}) collective-permute-start(f16[128,4,128]{2,0,1:T(8,128)(2,1)S(1)} %fusion.15), channel_id=1, source_target_pairs={{0,2},{1,3},{2,0},{3,1},{4,6},{5,7},{6,4},{7,5},{8,10},{9,11},{10,... | collective-permute-start | bytes 393224 | tf_op jit(solution)/shard_map/ppermute | solution.py:134
  70.1 7.1 %collective-permute-start.24 = (f16[128,4,128]{2,0,1:T(8,128)(2,1)S(1)}, f16[128,4,128]{2,0,1:T(8,128)(2,1)S(1)}, u32[]{:S(2)}, u32[]{:S(2)}) collective-permute-start(f16[128,4,128]{2,0,1:T(8,128)(2,1)S(1)} %fusion.16), channel_id=1, source_target_pairs={{0,2},{1,3},{2,0},{3,1},{4,6},{5,7},{6,4},{7,5},{8,10},{9,11},{10,... | collective-permute-start | bytes 393224 | tf_op jit(solution)/shard_map/ppermute | solution.py:134

commit v8 on v7

--- a/solution.py
+++ b/solution.py
@@ -12,20 +12,31 @@
 SCALE = 32768.0
 ORDER = (
     "head0", "pair0", "across0", "own0", "head1", "pair1", "across1", "own1",
-    "unitcore0", "unitcore1",
-    "relay0", "end0", "turn0", "headpair0", "relay1", "end1", "turn1", "headpair1",
-    "own2", "crossed0", "owncore0", "owncore1", "paircore0", "paircore1", "endcore0",
-    "early*", "far0", "endcore1", "far1", "ends*", "relay>", "turn>",
-    "rest*", "unit*", "pair*", "head*", "across*", "relay*", "far>",
-    "headpair*", "turn*", "far*",
+    "unitcore0", "unitcore1", "relay0", "end0", "turn0", "headpair0", "relay1", "end1",
+    "turn1", "headpair1", "own2", "crossed0", "owncore0", "owncore1", "paircore0", "paircore1",
+    "endcore0", "early*", "far0", "far1", "endcore1", "ends*", "relay>", "turn>",
+    "rest*", "unit*", "pair*", "head*", "across*", "relay*", "far>", "headpair*",
+    "turn*", "far*",
 )
 
 
 VMEM = pl.BlockSpec(memory_space=pltpu.VMEM)
 
 
-def unit_kernel(cut, data, first, second):
-    squares = jnp.sum(data[...] * data[...], axis=0, keepdims=True)
+def unit_kernel(cut, chunks, source, first, second, data, sems):
+    size = data.shape[0] // chunks
+
+    def load(i):
+        span = pl.ds(i * size, size)
+        return pltpu.make_async_copy(source.at[span], data.at[span], sems.at[i])
+
+    for i in range(chunks):
+        load(i).start()
+    squares = jnp.zeros((1, data.shape[1]), jnp.float32)
+    for i in range(chunks):
+        load(i).wait()
+        part = data[i * size : (i + 1) * size]
+        squares += jnp.sum(part * part, axis=0, keepdims=True)
     scale = lax.rsqrt(squares + 1e-06)
     first[...] = (data[:cut] * scale).astype(jnp.bfloat16)
     second[...] = (data[cut:] * scale).astype(jnp.bfloat16)
@@ -33,18 +44,23 @@
 
 def normalize(data, cut):
     features, block = data.shape
+    chunks = next(n for n in (5, 4, 3, 2, 1) if features % (8 * n) == 0)
     return pl.pallas_call(
-        functools.partial(unit_kernel, cut),
+        functools.partial(unit_kernel, cut, chunks),
         out_shape=[
             jax.ShapeDtypeStruct((cut, block), jnp.bfloat16),
             jax.ShapeDtypeStruct((features - cut, block), jnp.bfloat16),
         ],
-        in_specs=[VMEM],
+        in_specs=[pl.BlockSpec(memory_space=pltpu.HBM)],
         out_specs=[VMEM, VMEM],
+        scratch_shapes=[
+            pltpu.VMEM((features, block), jnp.float32),
+            pltpu.SemaphoreType.DMA((chunks,)),
+        ],
         cost_estimate=pl.CostEstimate(flops=0, bytes_accessed=6 * data.size, transcendentals=0),
-        compiler_params=pltpu.CompilerParams(vmem_limit_bytes=8 * data.size),
+        compiler_params=pltpu.CompilerParams(vmem_limit_bytes=16 * data.size),
         name="normalize",
-    )(data)
+    )(pltpu.with_memory_space_constraint(data, pltpu.HBM))
 
 
 def store_kernel(count, slots, *refs):
@@ -76,6 +92,22 @@
         compiler_params=pltpu.CompilerParams(vmem_limit_bytes=2**20),
         name="store",
     )(slots, *[panel.transpose(1, 0, 2) for panel in panels])
+
+
+def blank_kernel(*refs):
+    del refs
+
+
+def blank(after, shape, count):
+    return pl.pallas_call(
+        blank_kernel,
+        out_shape=[jax.ShapeDtypeStruct(shape, jnp.bfloat16)] * count,
+        in_specs=[pl.BlockSpec(memory_space=pl.ANY)],
+        out_specs=[pl.BlockSpec(memory_space=pl.ANY)] * count,
+        cost_estimate=pl.CostEstimate(flops=0, bytes_accessed=0, transcendentals=0),
+        compiler_params=pltpu.CompilerParams(vmem_limit_bytes=2**20),
+        name="blank",
+    )(after)
 
 
 def shards(descriptors):
@@ -163,6 +195,7 @@
     end = {j: [None, None] for j in others}
     own_swapped = {j: [None, None, None] for j in range(0, ngroups, 2)}
     end_swapped = {j: [None, None] for j in range(0, ngroups, 2)}
+    blanks = list(blank(unit[0], (ngroups,) + data.shape, 2))
     columns = {}
     values = {}
     panels = {}
@@ -188,7 +221,7 @@
         return lax.optimization_barrier(fourth(block, columns["own"]))
 
     def fill_early():
-        full = jnp.zeros((ngroups,) + data.shape, jnp.bfloat16)
+        full = blanks.pop()
         for h in halves:
             full = place(full, h * cut, unit[h], own_swapped[0][h], 0)
             for j in others:
@@ -201,7 +234,7 @@
             columns["own"] = place(full, cut + quarter, own[j][2], own_swapped[j][2], j)
 
     def fill_end():
-        full = jnp.zeros((ngroups,) + data.shape, jnp.bfloat16)
+        full = blanks.pop()
         for h in halves:
             full = place(full, h * cut, pair[h], end_swapped[0][h], 0)
             for j in others:

time: 80.3 us -> 79.9 us (level)
  local copies, waits for them, and re-layouts: 3.34 us -> 1.58 us
  Pallas kernels: 2.32 us -> 3.45 us
    unnamed x2 -> x0, local copies, waits for them, and re-layouts: 1.22 us -> none
    pallas_call x1 -> x2, Pallas kernels: 0.33 us -> 1.46 us  [the longest x1 1.46 us: normalize(): pl.pallas_call(functools.partial(unit_kernel, cut, chunks), out_shape=[ja...]
  transfers between devices with their start and end apart: 31 -> 31, of which waited for: 13 -> 13; matrix products, arithmetic and copies ran while one was open for 8% -> 7% of each run, Pallas kernels for 2% -> 2%
where the time goes in v8:
time: 79.9 us; the launch traced here: 79.8 us
  starting transfers between devices  46.5 us (58%)
  waiting for transfers between devices  22.4 us (28%)
  matrix products  5.32 us (7%)
  Pallas kernels  3.45 us (4%)
  local copies, waits for them, and re-layouts  1.58 us (2%)
    ppermute x31, starting transfers between devices, send(): return lax.ppermute(array, AXES, pairs)  46.5 us
    ppermute x31, waiting for transfers between devices, send(): return lax.ppermute(array, AXES, pairs)  22.4 us
    dot_general x11, matrix products, fourth(): lax.dot_general(jnp.concatenate(block, axis=0), cols, (((0,), (1,)), ((),...  5.32 us
    pallas_call x1, Pallas kernels, store(): pl.pallas_call(functools.partial(store_kernel, count), out_shape=jax.Shap...  1.99 us
  transfers between devices with their start and end apart: 31, of which 13 were waited for; matrix products, arithmetic and copies ran while one was open for 7% of the time, Pallas kernels for 2%

profile of v8, /device:TPU:0, one launch (start us, length us, event | category | flops | bytes accessed | tf_op | source)
XLA Modules:
  0.0 79.8 jit_solution(7031815103300924612)
XLA Ops:
  0.0 1.5 %normalize.1 = (bf16[992,128]{1,0:T(8,128)(2,1)S(1)}, bf16[1008,128]{1,0:T(8,128)(2,1)S(1)}) custom-call(f32[2000,128]{1,0:T(8,128)} %bitcast.99), custom_call_target="tpu_custom_call" | custom-call | bytes 1536000 | tf_op jit(solution)/shard_map/normalize/pallas_call | solution.py:48
  1.6 3.1 %collective-permute-start.8 = (bf16[992,128]{1,0:T(8,128)(2,1)S(1)}, bf16[992,128]{1,0:T(8,128)(2,1)S(1)}, u32[]{:S(2)}, u32[]{:S(2)}) collective-permute-start(bf16[992,128]{1,0:T(8,128)(2,1)S(1)} %get-tuple-element.21.refs_0_), channel_id=1, source_target_pairs={{0,2},{1,3},{2,0},{3,1},{4,6},{5,7},{6,4},{7,5},{8,10},{9,11},{10,... | collective-permute-start | bytes 761864 | tf_op jit(solution)/shard_map/ppermute | solution.py:166
  4.7 1.5 %collective-permute-start.10 = (bf16[992,128]{1,0:T(8,128)(2,1)S(1)}, bf16[992,128]{1,0:T(8,128)(2,1)S(1)}, u32[]{:S(2)}, u32[]{:S(2)}) collective-permute-start(bf16[992,128]{1,0:T(8,128)(2,1)S(1)} %get-tuple-element.21.refs_0_), channel_id=1, source_target_pairs={{0,1},{1,0},{2,4},{3,5},{4,2},{5,3},{6,7},{7,6},{8,9},{9,8},{10,12... | collective-permute-start | bytes 761864 | tf_op jit(solution)/shard_map/ppermute | solution.py:166
  6.1 1.5 %collective-permute-start.1 = (bf16[992,128]{1,0:T(8,128)(2,1)S(1)}, bf16[992,128]{1,0:T(8,128)(2,1)S(1)}, u32[]{:S(2)}, u32[]{:S(2)}) collective-permute-start(bf16[992,128]{1,0:T(8,128)(2,1)S(1)} %get-tuple-element.21.refs_0_), channel_id=1, source_target_pairs={{0,16},{1,17},{2,18},{3,19},{4,20},{5,21},{6,22},{7,23},{8,24},{9,... | collective-permute-start | bytes 761864 | tf_op jit(solution)/shard_map/ppermute | solution.py:166
  7.7 1.7 %collective-permute-start.9 = (bf16[1008,128]{1,0:T(8,128)(2,1)S(1)}, bf16[1008,128]{1,0:T(8,128)(2,1)S(1)}, u32[]{:S(2)}, u32[]{:S(2)}) collective-permute-start(bf16[1008,128]{1,0:T(8,128)(2,1)S(1)} %get-tuple-element.22), channel_id=1, source_target_pairs={{0,2},{1,3},{2,0},{3,1},{4,6},{5,7},{6,4},{7,5},{8,10},{9,11},{10,... | collective-permute-start | bytes 774152 | tf_op jit(solution)/shard_map/ppermute | solution.py:166
  9.4 1.7 %collective-permute-done.8 = bf16[992,128]{1,0:T(8,128)(2,1)S(1)} collective-permute-done((bf16[992,128]{1,0:T(8,128)(2,1)S(1)}, bf16[992,128]{1,0:T(8,128)(2,1)S(1)}, u32[]{:S(2)}, u32[]{:S(2)}) %collective-permute-start.8) | collective-permute-done | bytes 253984 | tf_op jit(solution)/shard_map/ppermute | solution.py:166
  11.1 2.6 %collective-permute-start.4 = (bf16[496,128]{1,0:T(8,128)(2,1)S(1)}, bf16[496,128]{1,0:T(8,128)(2,1)S(1)}, u32[]{:S(2)}, u32[]{:S(2)}) collective-permute-start(bf16[496,128]{1,0:T(8,128)(2,1)S(1)} %slice.7), channel_id=1, source_target_pairs={{0,16},{1,17},{2,18},{3,19},{4,20},{5,21},{6,22},{7,23},{8,24},{9,... | collective-permute-start | bytes 380936 | tf_op jit(solution)/shard_map/ppermute | solution.py:166
  13.7 1.0 %collective-permute-done.1 = bf16[992,128]{1,0:T(8,128)(2,1)S(1)} collective-permute-done((bf16[992,128]{1,0:T(8,128)(2,1)S(1)}, bf16[992,128]{1,0:T(8,128)(2,1)S(1)}, u32[]{:S(2)}, u32[]{:S(2)}) %collective-permute-start.1) | collective-permute-done | bytes 253984 | tf_op jit(solution)/shard_map/ppermute | solution.py:166
  14.8 1.4 %collective-permute-done.2 = bf16[992,128]{1,0:T(8,128)(2,1)S(1)} collective-permute-done((bf16[992,128]{1,0:T(8,128)(2,1)S(1)}, bf16[992,128]{1,0:T(8,128)(2,1)S(1)}, u32[]{:S(2)}, u32[]{:S(2)}) %collective-permute-start.2) | collective-permute-done | bytes 253984 | tf_op jit(solution)/shard_map/ppermute | solution.py:166
  16.2 1.5 %collective-permute-start.6 = (bf16[512,128]{1,0:T(8,128)(2,1)S(1)}, bf16[512,128]{1,0:T(8,128)(2,1)S(1)}, u32[]{:S(2)}, u32[]{:S(2)}) collective-permute-start(bf16[512,128]{1,0:T(8,128)(2,1)S(1)} %slice.8), channel_id=1, source_target_pairs={{0,16},{1,17},{2,18},{3,19},{4,20},{5,21},{6,22},{7,23},{8,24},{9,... | collective-permute-start | bytes 393224 | tf_op jit(solution)/shard_map/ppermute | solution.py:166
  17.8 1.0 %collective-permute-start.7 = (bf16[512,128]{1,0:T(8,128)(2,1)S(1)}, bf16[512,128]{1,0:T(8,128)(2,1)S(1)}, u32[]{:S(2)}, u32[]{:S(2)}) collective-permute-start(bf16[512,128]{1,0:T(8,128)(2,1)S(1)} %slice.8), channel_id=1, source_target_pairs={{0,24},{1,25},{2,26},{3,27},{4,28},{5,29},{6,30},{7,31},{8,16},{9,... | collective-permute-start | bytes 393224 | tf_op jit(solution)/shard_map/ppermute | solution.py:166
  18.8 0.9 %collective-permute-start.5 = (bf16[496,128]{1,0:T(8,128)(2,1)S(1)}, bf16[496,128]{1,0:T(8,128)(2,1)S(1)}, u32[]{:S(2)}, u32[]{:S(2)}) collective-permute-start(bf16[496,128]{1,0:T(8,128)(2,1)S(1)} %collective-permute-done.4), channel_id=1, source_target_pairs={{0,8},{1,9},{2,10},{3,11},{4,12},{5,13},{6,14},{7,15},{8,0},{9,1},... | collective-permute-start | bytes 380936 | tf_op jit(solution)/shard_map/ppermute | solution.py:166
  19.7 0.9 %collective-permute-done.5 = bf16[496,128]{1,0:T(8,128)(2,1)S(1)} collective-permute-done((bf16[496,128]{1,0:T(8,128)(2,1)S(1)}, bf16[496,128]{1,0:T(8,128)(2,1)S(1)}, u32[]{:S(2)}, u32[]{:S(2)}) %collective-permute-start.5) | collective-permute-done | bytes 127008 | tf_op jit(solution)/shard_map/ppermute | solution.py:166
  20.6 1.5 %collective-permute-start.11 = (bf16[1008,128]{1,0:T(8,128)(2,1)S(1)}, bf16[1008,128]{1,0:T(8,128)(2,1)S(1)}, u32[]{:S(2)}, u32[]{:S(2)}) collective-permute-start(bf16[1008,128]{1,0:T(8,128)(2,1)S(1)} %get-tuple-element.22), channel_id=1, source_target_pairs={{0,1},{1,0},{2,4},{3,5},{4,2},{5,3},{6,7},{7,6},{8,9},{9,8},{10,12... | collective-permute-start | bytes 774152 | tf_op jit(solution)/shard_map/ppermute | solution.py:166
  22.2 0.4 collective-permute-done.6
  22.6 1.1 %collective-permute-done.7 = bf16[512,128]{1,0:T(8,128)(2,1)S(1)} collective-permute-done((bf16[512,128]{1,0:T(8,128)(2,1)S(1)}, bf16[512,128]{1,0:T(8,128)(2,1)S(1)}, u32[]{:S(2)}, u32[]{:S(2)}) %collective-permute-start.7) | collective-permute-done | bytes 131104 | tf_op jit(solution)/shard_map/ppermute | solution.py:166
  23.7 0.9 %collective-permute-start.16 = (bf16[992,128]{1,0:T(8,128)(2,1)S(1)}, bf16[992,128]{1,0:T(8,128)(2,1)S(1)}, u32[]{:S(2)}, u32[]{:S(2)}) collective-permute-start(bf16[992,128]{1,0:T(8,128)(2,1)S(1)} %get-tuple-element.21.refs_0_), channel_id=1, source_target_pairs={{0,8},{1,9},{2,3},{3,2},{4,5},{5,4},{6,14},{7,15},{8,0},{9,1},{10,... | collective-permute-start | bytes 761864 | tf_op jit(solution)/shard_map/ppermute | solution.py:166
  24.7 0.5 fusion.10
  25.3 3.8 %collective-permute-done.11 = bf16[1008,128]{1,0:T(8,128)(2,1)S(1)} collective-permute-done((bf16[1008,128]{1,0:T(8,128)(2,1)S(1)}, bf16[1008,128]{1,0:T(8,128)(2,1)S(1)}, u32[]{:S(2)}, u32[]{:S(2)}) %collective-permute-start.11) | collective-permute-done | bytes 258080 | tf_op jit(solution)/shard_map/ppermute | solution.py:166
  29.1 0.4 collective-permute-start.19
  29.5 0.5 fusion.8
  30.0 1.7 %collective-permute-start.12 = (bf16[992,128]{1,0:T(8,128)(2,1)S(1)}, bf16[992,128]{1,0:T(8,128)(2,1)S(1)}, u32[]{:S(2)}, u32[]{:S(2)}) collective-permute-start(bf16[992,128]{1,0:T(8,128)(2,1)S(1)} %collective-permute-done.10), channel_id=1, source_target_pairs={{0,2},{1,3},{2,0},{3,1},{4,6},{5,7},{6,4},{7,5},{8,10},{9,11},{10,... | collective-permute-start | bytes 761864 | tf_op jit(solution)/shard_map/ppermute | solution.py:166
  31.7 0.5 fusion.9
  32.3 1.6 %collective-permute-start.14 = (bf16[992,128]{1,0:T(8,128)(2,1)S(1)}, bf16[992,128]{1,0:T(8,128)(2,1)S(1)}, u32[]{:S(2)}, u32[]{:S(2)}) collective-permute-start(bf16[992,128]{1,0:T(8,128)(2,1)S(1)} %collective-permute-done.8), channel_id=1, source_target_pairs={{0,1},{1,0},{2,4},{3,5},{4,2},{5,3},{6,7},{7,6},{8,9},{9,8},{10,12... | collective-permute-start | bytes 761864 | tf_op jit(solution)/shard_map/ppermute | solution.py:166
  33.9 0.5 fusion.5
  34.4 0.2 collective-permute-start.26
  34.6 2.0 %collective-permute-done.19 = bf16[992,128]{1,0:T(8,128)(2,1)S(1)} collective-permute-done((bf16[992,128]{1,0:T(8,128)(2,1)S(1)}, bf16[992,128]{1,0:T(8,128)(2,1)S(1)}, u32[]{:S(2)}, u32[]{:S(2)}) %collective-permute-start.19) | collective-permute-done | bytes 253984 | tf_op jit(solution)/shard_map/ppermute | solution.py:166
  36.7 0.5 collective-permute-start.22
  37.2 13.6 %collective-permute-start.13 = (bf16[1008,128]{1,0:T(8,128)(2,1)S(1)}, bf16[1008,128]{1,0:T(8,128)(2,1)S(1)}, u32[]{:S(2)}, u32[]{:S(2)}) collective-permute-start(bf16[1008,128]{1,0:T(8,128)(2,1)S(1)} %collective-permute-done.11), channel_id=1, source_target_pairs={{0,2},{1,3},{2,0},{3,1},{4,6},{5,7},{6,4},{7,5},{8,10},{9,11},{10,... | collective-permute-start | bytes 774152 | tf_op jit(solution)/shard_map/ppermute | solution.py:166
  50.8 0.5 fusion.3
  51.3 1.6 %collective-permute-start.15 = (bf16[1008,128]{1,0:T(8,128)(2,1)S(1)}, bf16[1008,128]{1,0:T(8,128)(2,1)S(1)}, u32[]{:S(2)}, u32[]{:S(2)}) collective-permute-start(bf16[1008,128]{1,0:T(8,128)(2,1)S(1)} %collective-permute-done.9), channel_id=1, source_target_pairs={{0,1},{1,0},{2,4},{3,5},{4,2},{5,3},{6,7},{7,6},{8,9},{9,8},{10,12... | collective-permute-start | bytes 774152 | tf_op jit(solution)/shard_map/ppermute | solution.py:166
  52.8 2.7 %collective-permute-done.13 = bf16[1008,128]{1,0:T(8,128)(2,1)S(1)} collective-permute-done((bf16[1008,128]{1,0:T(8,128)(2,1)S(1)}, bf16[1008,128]{1,0:T(8,128)(2,1)S(1)}, u32[]{:S(2)}, u32[]{:S(2)}) %collective-permute-start.13) | collective-permute-done | bytes 258080 | tf_op jit(solution)/shard_map/ppermute | solution.py:166
  55.5 0.5 fusion.7
  56.0 0.6 collective-permute-start.28
  56.6 1.1 %collective-permute-done.15 = bf16[1008,128]{1,0:T(8,128)(2,1)S(1)} collective-permute-done((bf16[1008,128]{1,0:T(8,128)(2,1)S(1)}, bf16[1008,128]{1,0:T(8,128)(2,1)S(1)}, u32[]{:S(2)}, u32[]{:S(2)}) %collective-permute-start.15) | collective-permute-done | bytes 258080 | tf_op jit(solution)/shard_map/ppermute | solution.py:166
  57.7 0.5 fusion.6
  58.2 0.5 collective-permute-start.23
  58.9 1.2 %collective-permute-done.23 = bf16[1008,128]{1,0:T(8,128)(2,1)S(1)} collective-permute-done((bf16[1008,128]{1,0:T(8,128)(2,1)S(1)}, bf16[1008,128]{1,0:T(8,128)(2,1)S(1)}, u32[]{:S(2)}, u32[]{:S(2)}) %collective-permute-start.23) | collective-permute-done | bytes 258080 | tf_op jit(solution)/shard_map/ppermute | solution.py:166
  60.2 0.5 fusion.14
  60.7 7.5 %collective-permute-start.30 = (f16[128,4,128]{2,0,1:T(8,128)(2,1)S(1)}, f16[128,4,128]{2,0,1:T(8,128)(2,1)S(1)}, u32[]{:S(2)}, u32[]{:S(2)}) collective-permute-start(f16[128,4,128]{2,0,1:T(8,128)(2,1)S(1)} %fusion.14), channel_id=1, source_target_pairs={{0,2},{1,3},{2,0},{3,1},{4,6},{5,7},{6,4},{7,5},{8,10},{9,11},{10,... | collective-permute-start | bytes 393224 | tf_op jit(solution)/shard_map/ppermute | solution.py:166
  68.2 0.5 fusion.15
  68.8 0.5 fusion.1
  69.3 0.5 fusion.16
  69.8 2.1 %collective-permute-start.24 = (f16[128,4,128]{2,0,1:T(8,128)(2,1)S(1)}, f16[128,4,128]{2,0,1:T(8,128)(2,1)S(1)}, u32[]{:S(2)}, u32[]{:S(2)}) collective-permute-start(f16[128,4,128]{2,0,1:T(8,128)(2,1)S(1)} %fusion.16), channel_id=1, source_target_pairs={{0,2},{1,3},{2,0},{3,1},{4,6},{5,7},{6,4},{7,5},{8,10},{9,11},{10,... | collective-permute-start | bytes 393224 | tf_op jit(solution)/shard_map/ppermute | solution.py:166
  71.8 3.3 %collective-permute-done.27 = f16[128,4,128]{2,0,1:T(8,128)(2,1)S(1)} collective-permute-done((f16[128,4,128]{2,0,1:T(8,128)(2,1)S(1)}, f16[128,4,128]{2,0,1:T(8,128)(2,1)S(1)}, u32[]{:S(2)}, u32[]{:S(2)}) %collective-permute-start.27) | collective-permute-done | bytes 131104 | tf_op jit(solution)/shard_map/ppermute | solution.py:166
  75.1 1.7 %collective-permute-done.24 = f16[128,4,128]{2,0,1:T(8,128)(2,1)S(1)} collective-permute-done((f16[128,4,128]{2,0,1:T(8,128)(2,1)S(1)}, f16[128,4,128]{2,0,1:T(8,128)(2,1)S(1)}, u32[]{:S(2)}, u32[]{:S(2)}) %collective-permute-start.24) | collective-permute-done | bytes 131104 | tf_op jit(solution)/shard_map/ppermute | solution.py:166
  76.8 2.0 %store.1 = f32[8,128,4,128]{3,2,1,0:T(4,128)} custom-call(s32[7]{0:T(128)S(1)} %stack.31.slots, f32[4,128,128]{2,1,0:T(8,128)S(1)} %bitcast.94, f32[4,128,128]{2,1,0:T(8,128)S(1)} %bitcast.96, f32[4,128,128]{2,1,0:T(8,128)S(1)} %bitcast.95, f32[4,128,128]{2,1,0:T(8,128)S(1)} %bitcast.97, f32[4,128,128]{2,1,0:T(8,128)S(1)} %bitcast.98, ...), custom_call_target="tpu_custom_call" | custom-call | bytes 3670016 | tf_op jit(solution)/shard_map/store/pallas_call | solution.py:84
  78.9 0.9 %copy_dynamic-update-slice_fusion = f32[8,128,4,128]{3,2,1,0:T(4,128)} fusion(f32[8,128,4,128]{3,2,1,0:T(4,128)} %store.1, s32[]{:T(128)S(6)} %select_n.106, f32[1,128,4,128]{3,1,2,0:T(8,128)S(1)} %select_bitcast_fusion), kind=kLoop, calls=%fused_computation.46 | loop fusion | bytes 524292 | tf_op jit(solution)/shard_map/jit(dynamic_update_index_in_dim)/dynamic_update_slice | solution.py:340
  (53 shorter events, 1.1 us)
Async XLA Ops:
  1.6 9.5 %collective-permute-start.8 = (bf16[992,128]{1,0:T(8,128)(2,1)S(1)}, bf16[992,128]{1,0:T(8,128)(2,1)S(1)}, u32[]{:S(2)}, u32[]{:S(2)}) collective-permute-start(bf16[992,128]{1,0:T(8,128)(2,1)S(1)} %get-tuple-element.21.refs_0_), channel_id=1, source_target_pairs={{0,2},{1,3},{2,0},{3,1},{4,6},{5,7},{6,4},{7,5},{8,10},{9,11},{10,... | collective-permute-start | bytes 761864 | tf_op jit(solution)/shard_map/ppermute | solution.py:166
  4.7 20.5 %collective-permute-start.10 = (bf16[992,128]{1,0:T(8,128)(2,1)S(1)}, bf16[992,128]{1,0:T(8,128)(2,1)S(1)}, u32[]{:S(2)}, u32[]{:S(2)}) collective-permute-start(bf16[992,128]{1,0:T(8,128)(2,1)S(1)} %get-tuple-element.21.refs_0_), channel_id=1, source_target_pairs={{0,1},{1,0},{2,4},{3,5},{4,2},{5,3},{6,7},{7,6},{8,9},{9,8},{10,12... | collective-permute-start | bytes 761864 | tf_op jit(solution)/shard_map/ppermute | solution.py:166
  6.1 5.0 %collective-permute-start = (bf16[992,128]{1,0:T(8,128)(2,1)S(1)}, bf16[992,128]{1,0:T(8,128)(2,1)S(1)}, u32[]{:S(2)}, u32[]{:S(2)}) collective-permute-start(bf16[992,128]{1,0:T(8,128)(2,1)S(1)} %get-tuple-element.21.refs_0_), channel_id=1, source_target_pairs={{0,8},{1,9},{2,10},{3,11},{4,12},{5,13},{6,14},{7,15},{8,0},{9,1},... | collective-permute-start | bytes 761864 | tf_op jit(solution)/shard_map/ppermute | solution.py:166
  6.1 8.5 %collective-permute-start.1 = (bf16[992,128]{1,0:T(8,128)(2,1)S(1)}, bf16[992,128]{1,0:T(8,128)(2,1)S(1)}, u32[]{:S(2)}, u32[]{:S(2)}) collective-permute-start(bf16[992,128]{1,0:T(8,128)(2,1)S(1)} %get-tuple-element.21.refs_0_), channel_id=1, source_target_pairs={{0,16},{1,17},{2,18},{3,19},{4,20},{5,21},{6,22},{7,23},{8,24},{9,... | collective-permute-start | bytes 761864 | tf_op jit(solution)/shard_map/ppermute | solution.py:166
  7.7 22.3 %collective-permute-start.9 = (bf16[1008,128]{1,0:T(8,128)(2,1)S(1)}, bf16[1008,128]{1,0:T(8,128)(2,1)S(1)}, u32[]{:S(2)}, u32[]{:S(2)}) collective-permute-start(bf16[1008,128]{1,0:T(8,128)(2,1)S(1)} %get-tuple-element.22), channel_id=1, source_target_pairs={{0,2},{1,3},{2,0},{3,1},{4,6},{5,7},{6,4},{7,5},{8,10},{9,11},{10,... | collective-permute-start | bytes 774152 | tf_op jit(solution)/shard_map/ppermute | solution.py:166
  11.1 7.7 %collective-permute-start.3 = (bf16[1008,128]{1,0:T(8,128)(2,1)S(1)}, bf16[1008,128]{1,0:T(8,128)(2,1)S(1)}, u32[]{:S(2)}, u32[]{:S(2)}) collective-permute-start(bf16[1008,128]{1,0:T(8,128)(2,1)S(1)} %get-tuple-element.22), channel_id=1, source_target_pairs={{0,8},{1,9},{2,10},{3,11},{4,12},{5,13},{6,14},{7,15},{8,0},{9,1},... | collective-permute-start | bytes 774152 | tf_op jit(solution)/shard_map/ppermute | solution.py:166
  11.1 6.7 %collective-permute-start.4 = (bf16[496,128]{1,0:T(8,128)(2,1)S(1)}, bf16[496,128]{1,0:T(8,128)(2,1)S(1)}, u32[]{:S(2)}, u32[]{:S(2)}) collective-permute-start(bf16[496,128]{1,0:T(8,128)(2,1)S(1)} %slice.7), channel_id=1, source_target_pairs={{0,16},{1,17},{2,18},{3,19},{4,20},{5,21},{6,22},{7,23},{8,24},{9,... | collective-permute-start | bytes 380936 | tf_op jit(solution)/shard_map/ppermute | solution.py:166
  14.7 1.5 %collective-permute-start.2 = (bf16[992,128]{1,0:T(8,128)(2,1)S(1)}, bf16[992,128]{1,0:T(8,128)(2,1)S(1)}, u32[]{:S(2)}, u32[]{:S(2)}) collective-permute-start(bf16[992,128]{1,0:T(8,128)(2,1)S(1)} %collective-permute-done.1), channel_id=1, source_target_pairs={{0,8},{1,9},{2,10},{3,11},{4,12},{5,13},{6,14},{7,15},{8,0},{9,1},... | collective-permute-start | bytes 761864 | tf_op jit(solution)/shard_map/ppermute | solution.py:166
  16.2 6.4 %collective-permute-start.6 = (bf16[512,128]{1,0:T(8,128)(2,1)S(1)}, bf16[512,128]{1,0:T(8,128)(2,1)S(1)}, u32[]{:S(2)}, u32[]{:S(2)}) collective-permute-start(bf16[512,128]{1,0:T(8,128)(2,1)S(1)} %slice.8), channel_id=1, source_target_pairs={{0,16},{1,17},{2,18},{3,19},{4,20},{5,21},{6,22},{7,23},{8,24},{9,... | collective-permute-start | bytes 393224 | tf_op jit(solution)/shard_map/ppermute | solution.py:166
  17.8 5.9 %collective-permute-start.7 = (bf16[512,128]{1,0:T(8,128)(2,1)S(1)}, bf16[512,128]{1,0:T(8,128)(2,1)S(1)}, u32[]{:S(2)}, u32[]{:S(2)}) collective-permute-start(bf16[512,128]{1,0:T(8,128)(2,1)S(1)} %slice.8), channel_id=1, source_target_pairs={{0,24},{1,25},{2,26},{3,27},{4,28},{5,29},{6,30},{7,31},{8,16},{9,... | collective-permute-start | bytes 393224 | tf_op jit(solution)/shard_map/ppermute | solution.py:166
  18.8 1.8 %collective-permute-start.5 = (bf16[496,128]{1,0:T(8,128)(2,1)S(1)}, bf16[496,128]{1,0:T(8,128)(2,1)S(1)}, u32[]{:S(2)}, u32[]{:S(2)}) collective-permute-start(bf16[496,128]{1,0:T(8,128)(2,1)S(1)} %collective-permute-done.4), channel_id=1, source_target_pairs={{0,8},{1,9},{2,10},{3,11},{4,12},{5,13},{6,14},{7,15},{8,0},{9,1},... | collective-permute-start | bytes 380936 | tf_op jit(solution)/shard_map/ppermute | solution.py:166
  20.6 8.5 %collective-permute-start.11 = (bf16[1008,128]{1,0:T(8,128)(2,1)S(1)}, bf16[1008,128]{1,0:T(8,128)(2,1)S(1)}, u32[]{:S(2)}, u32[]{:S(2)}) collective-permute-start(bf16[1008,128]{1,0:T(8,128)(2,1)S(1)} %get-tuple-element.22), channel_id=1, source_target_pairs={{0,1},{1,0},{2,4},{3,5},{4,2},{5,3},{6,7},{7,6},{8,9},{9,8},{10,12... | collective-permute-start | bytes 774152 | tf_op jit(solution)/shard_map/ppermute | solution.py:166
  22.6 9.7 %collective-permute-start.17 = (bf16[1008,128]{1,0:T(8,128)(2,1)S(1)}, bf16[1008,128]{1,0:T(8,128)(2,1)S(1)}, u32[]{:S(2)}, u32[]{:S(2)}) collective-permute-start(bf16[1008,128]{1,0:T(8,128)(2,1)S(1)} %get-tuple-element.22), channel_id=1, source_target_pairs={{0,8},{1,9},{2,3},{3,2},{4,5},{5,4},{6,14},{7,15},{8,0},{9,1},{10,... | collective-permute-start | bytes 774152 | tf_op jit(solution)/shard_map/ppermute | solution.py:166
  23.7 8.5 %collective-permute-start.16 = (bf16[992,128]{1,0:T(8,128)(2,1)S(1)}, bf16[992,128]{1,0:T(8,128)(2,1)S(1)}, u32[]{:S(2)}, u32[]{:S(2)}) collective-permute-start(bf16[992,128]{1,0:T(8,128)(2,1)S(1)} %get-tuple-element.21.refs_0_), channel_id=1, source_target_pairs={{0,8},{1,9},{2,3},{3,2},{4,5},{5,4},{6,14},{7,15},{8,0},{9,1},{10,... | collective-permute-start | bytes 761864 | tf_op jit(solution)/shard_map/ppermute | solution.py:166
  25.2 9.2 %collective-permute-start.18 = (bf16[992,128]{1,0:T(8,128)(2,1)S(1)}, bf16[992,128]{1,0:T(8,128)(2,1)S(1)}, u32[]{:S(2)}, u32[]{:S(2)}) collective-permute-start(bf16[992,128]{1,0:T(8,128)(2,1)S(1)} %collective-permute-done.8), channel_id=1, source_target_pairs={{0,8},{1,9},{2,10},{3,11},{4,12},{5,13},{6,14},{7,15},{8,0},{9,1},... | collective-permute-start | bytes 761864 | tf_op jit(solution)/shard_map/ppermute | solution.py:166
  29.1 7.5 %collective-permute-start.19 = (bf16[992,128]{1,0:T(8,128)(2,1)S(1)}, bf16[992,128]{1,0:T(8,128)(2,1)S(1)}, u32[]{:S(2)}, u32[]{:S(2)}) collective-permute-start(bf16[992,128]{1,0:T(8,128)(2,1)S(1)} %collective-permute-done.8), channel_id=1, source_target_pairs={{0,16},{1,17},{2,18},{3,19},{4,20},{5,21},{6,22},{7,23},{8,24},{9,... | collective-permute-start | bytes 761864 | tf_op jit(solution)/shard_map/ppermute | solution.py:166
  30.0 21.3 %collective-permute-start.12 = (bf16[992,128]{1,0:T(8,128)(2,1)S(1)}, bf16[992,128]{1,0:T(8,128)(2,1)S(1)}, u32[]{:S(2)}, u32[]{:S(2)}) collective-permute-start(bf16[992,128]{1,0:T(8,128)(2,1)S(1)} %collective-permute-done.10), channel_id=1, source_target_pairs={{0,2},{1,3},{2,0},{3,1},{4,6},{5,7},{6,4},{7,5},{8,10},{9,11},{10,... | collective-permute-start | bytes 761864 | tf_op jit(solution)/shard_map/ppermute | solution.py:166
  32.2 4.5 %collective-permute-start.25 = (bf16[992,128]{1,0:T(8,128)(2,1)S(1)}, bf16[992,128]{1,0:T(8,128)(2,1)S(1)}, u32[]{:S(2)}, u32[]{:S(2)}) collective-permute-start(bf16[992,128]{1,0:T(8,128)(2,1)S(1)} %collective-permute-done.10), channel_id=1, source_target_pairs={{0,8},{1,9},{2,3},{3,2},{4,5},{5,4},{6,14},{7,15},{8,0},{9,1},{10,... | collective-permute-start | bytes 761864 | tf_op jit(solution)/shard_map/ppermute | solution.py:166
  32.3 23.7 %collective-permute-start.14 = (bf16[992,128]{1,0:T(8,128)(2,1)S(1)}, bf16[992,128]{1,0:T(8,128)(2,1)S(1)}, u32[]{:S(2)}, u32[]{:S(2)}) collective-permute-start(bf16[992,128]{1,0:T(8,128)(2,1)S(1)} %collective-permute-done.8), channel_id=1, source_target_pairs={{0,1},{1,0},{2,4},{3,5},{4,2},{5,3},{6,7},{7,6},{8,9},{9,8},{10,12... | collective-permute-start | bytes 761864 | tf_op jit(solution)/shard_map/ppermute | solution.py:166
  34.4 2.8 %collective-permute-start.26 = (bf16[1008,128]{1,0:T(8,128)(2,1)S(1)}, bf16[1008,128]{1,0:T(8,128)(2,1)S(1)}, u32[]{:S(2)}, u32[]{:S(2)}) collective-permute-start(bf16[1008,128]{1,0:T(8,128)(2,1)S(1)} %collective-permute-done.11), channel_id=1, source_target_pairs={{0,8},{1,9},{2,3},{3,2},{4,5},{5,4},{6,14},{7,15},{8,0},{9,1},{10,... | collective-permute-start | bytes 774152 | tf_op jit(solution)/shard_map/ppermute | solution.py:166
  36.7 22.2 %collective-permute-start.21 = (bf16[1008,128]{1,0:T(8,128)(2,1)S(1)}, bf16[1008,128]{1,0:T(8,128)(2,1)S(1)}, u32[]{:S(2)}, u32[]{:S(2)}) collective-permute-start(bf16[1008,128]{1,0:T(8,128)(2,1)S(1)} %collective-permute-done.9), channel_id=1, source_target_pairs={{0,8},{1,9},{2,10},{3,11},{4,12},{5,13},{6,14},{7,15},{8,0},{9,1},... | collective-permute-start | bytes 774152 | tf_op jit(solution)/shard_map/ppermute | solution.py:166
  36.7 21.5 %collective-permute-start.22 = (bf16[1008,128]{1,0:T(8,128)(2,1)S(1)}, bf16[1008,128]{1,0:T(8,128)(2,1)S(1)}, u32[]{:S(2)}, u32[]{:S(2)}) collective-permute-start(bf16[1008,128]{1,0:T(8,128)(2,1)S(1)} %collective-permute-done.9), channel_id=1, source_target_pairs={{0,16},{1,17},{2,18},{3,19},{4,20},{5,21},{6,22},{7,23},{8,24},{9,... | collective-permute-start | bytes 774152 | tf_op jit(solution)/shard_map/ppermute | solution.py:166
  37.2 18.4 %collective-permute-start.13 = (bf16[1008,128]{1,0:T(8,128)(2,1)S(1)}, bf16[1008,128]{1,0:T(8,128)(2,1)S(1)}, u32[]{:S(2)}, u32[]{:S(2)}) collective-permute-start(bf16[1008,128]{1,0:T(8,128)(2,1)S(1)} %collective-permute-done.11), channel_id=1, source_target_pairs={{0,2},{1,3},{2,0},{3,1},{4,6},{5,7},{6,4},{7,5},{8,10},{9,11},{10,... | collective-permute-start | bytes 774152 | tf_op jit(solution)/shard_map/ppermute | solution.py:166
  51.3 6.4 %collective-permute-start.15 = (bf16[1008,128]{1,0:T(8,128)(2,1)S(1)}, bf16[1008,128]{1,0:T(8,128)(2,1)S(1)}, u32[]{:S(2)}, u32[]{:S(2)}) collective-permute-start(bf16[1008,128]{1,0:T(8,128)(2,1)S(1)} %collective-permute-done.9), channel_id=1, source_target_pairs={{0,1},{1,0},{2,4},{3,5},{4,2},{5,3},{6,7},{7,6},{8,9},{9,8},{10,12... | collective-permute-start | bytes 774152 | tf_op jit(solution)/shard_map/ppermute | solution.py:166
  55.5 3.2 %collective-permute-start.20 = (bf16[992,128]{1,0:T(8,128)(2,1)S(1)}, bf16[992,128]{1,0:T(8,128)(2,1)S(1)}, u32[]{:S(2)}, u32[]{:S(2)}) collective-permute-start(bf16[992,128]{1,0:T(8,128)(2,1)S(1)} %collective-permute-done.19), channel_id=1, source_target_pairs={{0,8},{1,9},{2,10},{3,11},{4,12},{5,13},{6,14},{7,15},{8,0},{9,1},... | collective-permute-start | bytes 761864 | tf_op jit(solution)/shard_map/ppermute | solution.py:166
  56.0 4.1 %collective-permute-start.28 = (bf16[992,128]{1,0:T(8,128)(2,1)S(1)}, bf16[992,128]{1,0:T(8,128)(2,1)S(1)}, u32[]{:S(2)}, u32[]{:S(2)}) collective-permute-start(bf16[992,128]{1,0:T(8,128)(2,1)S(1)} %collective-permute-done.12), channel_id=1, source_target_pairs={{0,8},{1,9},{2,4},{3,5},{4,2},{5,3},{6,14},{7,15},{8,0},{9,1},{10,... | collective-permute-start | bytes 761864 | tf_op jit(solution)/shard_map/ppermute | solution.py:166
  58.2 2.0 %collective-permute-start.29 = (bf16[1008,128]{1,0:T(8,128)(2,1)S(1)}, bf16[1008,128]{1,0:T(8,128)(2,1)S(1)}, u32[]{:S(2)}, u32[]{:S(2)}) collective-permute-start(bf16[1008,128]{1,0:T(8,128)(2,1)S(1)} %collective-permute-done.15), channel_id=1, source_target_pairs={{0,8},{1,9},{2,3},{3,2},{4,5},{5,4},{6,14},{7,15},{8,0},{9,1},{10,... | collective-permute-start | bytes 774152 | tf_op jit(solution)/shard_map/ppermute | solution.py:166
  58.2 1.9 %collective-permute-start.23 = (bf16[1008,128]{1,0:T(8,128)(2,1)S(1)}, bf16[1008,128]{1,0:T(8,128)(2,1)S(1)}, u32[]{:S(2)}, u32[]{:S(2)}) collective-permute-start(bf16[1008,128]{1,0:T(8,128)(2,1)S(1)} %collective-permute-done.22), channel_id=1, source_target_pairs={{0,8},{1,9},{2,10},{3,11},{4,12},{5,13},{6,14},{7,15},{8,0},{9,1},... | collective-permute-start | bytes 774152 | tf_op jit(solution)/shard_map/ppermute | solution.py:166
  60.7 18.2 %collective-permute-start.30 = (f16[128,4,128]{2,0,1:T(8,128)(2,1)S(1)}, f16[128,4,128]{2,0,1:T(8,128)(2,1)S(1)}, u32[]{:S(2)}, u32[]{:S(2)}) collective-permute-start(f16[128,4,128]{2,0,1:T(8,128)(2,1)S(1)} %fusion.14), channel_id=1, source_target_pairs={{0,2},{1,3},{2,0},{3,1},{4,6},{5,7},{6,4},{7,5},{8,10},{9,11},{10,... | collective-permute-start | bytes 393224 | tf_op jit(solution)/shard_map/ppermute | solution.py:166
  68.7 6.4 %collective-permute-start.27 = (f16[128,4,128]{2,0,1:T(8,128)(2,1)S(1)}, f16[128,4,128]{2,0,1:T(8,128)(2,1)S(1)}, u32[]{:S(2)}, u32[]{:S(2)}) collective-permute-start(f16[128,4,128]{2,0,1:T(8,128)(2,1)S(1)} %fusion.15), channel_id=1, source_target_pairs={{0,2},{1,3},{2,0},{3,1},{4,6},{5,7},{6,4},{7,5},{8,10},{9,11},{10,... | collective-permute-start | bytes 393224 | tf_op jit(solution)/shard_map/ppermute | solution.py:166
  69.8 7.1 %collective-permute-start.24 = (f16[128,4,128]{2,0,1:T(8,128)(2,1)S(1)}, f16[128,4,128]{2,0,1:T(8,128)(2,1)S(1)}, u32[]{:S(2)}, u32[]{:S(2)}) collective-permute-start(f16[128,4,128]{2,0,1:T(8,128)(2,1)S(1)} %fusion.16), channel_id=1, source_target_pairs={{0,2},{1,3},{2,0},{3,1},{4,6},{5,7},{6,4},{7,5},{8,10},{9,11},{10,... | collective-permute-start | bytes 393224 | tf_op jit(solution)/shard_map/ppermute | solution.py:166
